TPU v7x, 128 devices: a whole 4x4x4 slice. The times are simulated.
128 devices in a mesh: circ: 8 (over z, y_hi), axial: 16 (over x, y_lo, core).
Axes of the slice: x: 4, y: 4 (y_hi: 2, y_lo: 2; y = y_hi * 2 + y_lo), z: 4, core: 2. Of those that a mesh axis runs over, the one named last changes fastest.
Arguments:
- position: float32 [3, 8, 16, 16384], P(None, 'circ', 'axial'), may hold values from -3 to 3
- displacement: float32 [3, 8, 16, 16384], P(None, 'circ', 'axial'), may hold values from -3 to 3
- velocity: float32 [3, 8, 16, 16384], P(None, 'circ', 'axial'), may hold values from -1.5 to 1.5
- bulk: float32 [8, 16, 16384], P('circ', 'axial'), may hold values from 6 to 30
- shear: float32 [8, 16, 16384], P('circ', 'axial'), may hold values from 0.5 to 2
- volume: float32 [8, 16, 16384], P('circ', 'axial'), may hold values from 60 to 200
- edges: int32 [8, 16, 2, 32], P('circ', 'axial'), may hold values from 0 to 127, as said below
- block_pairs: int32 [8, 16, 2, 320], P('circ', 'axial'), may hold values from 0 to 191, as said below
- block_counts: int32 [8, 16, 2], P('circ', 'axial'), may hold values from 128 to 320, as said below
- damage: int32 [8, 16, 320, 128, 128], P('circ', 'axial'), may hold values 0 or 1
Outputs:
- final_displacement: float32 [3, 8, 16, 16384], P(None, 'circ', 'axial')
- final_velocity: float32 [3, 8, 16, 16384], P(None, 'circ', 'axial')
- dilatation: float32 [8, 16, 16384], P('circ', 'axial')
Inputs may be any that keep to these rules, and one draw needn't show every extreme that they name: `edges`: for each device the 64 entries are distinct clusters of that device. `block_pairs`: slot b below 128 pairs cluster b with itself; the further slots below block_counts[c, a, 0] pair two different clusters of the device; the next slots up to block_counts[c, a, 1] are cross blocks whose target is an extended slot of 128 or more, each extended slot of the device's neighbours used exactly once (only the circumferential ones on the last axial section); later slots hold unused pairs of two different local clusters. `block_counts`: entry 0 is the number of local blocks, 128 or more; entry 1 the number of all blocks of the device, which is 32 or 64 more than entry 0.
All inputs are finite; a program needn't handle non-finite values. No bound on the sum of `damage` on one device may be relied on, other than what follows from the above.
Results may differ from a plain program's by a relative error of at most 0.0003.
Values sent between devices are 32-bit elements; how exact they have to be, the bound alone decides.
No kernel may reach another device: no remote copies, remote signals or barrier semaphores. Data moves between devices by JAX's collectives and lax.ppermute only.
A program may use at most 64 MiB of HBM per device.

v0:
```python
import jax
import jax.numpy as jnp
from jax import lax
from jax.sharding import PartitionSpec as P

FACING = 32
GROUP_SLOTS = 16
TIME_STEPS = 2


SOFTEN = 0.01
HORIZON_SQ = 1.0
TIMESTEP = 0.07


def from_behind(block, axis, distance):
    devices = range(lax.axis_size(axis))
    route = [((i - distance) % len(devices), i) for i in devices]
    return lax.ppermute(block, axis, route)


def shifted(shard, axis, by):
    size = lax.axis_size(axis)
    pairs = [(i, i + by) for i in range(size) if 0 <= i + by < size]
    return lax.ppermute(shard, axis, pairs)


def bond_geometry(source, target):
    spacing = target[:, 0:3, None, :] - source[:, 0:3, :, None]
    relative = target[:, 3:6, None, :] - source[:, 3:6, :, None]
    stretched = spacing + relative
    length_sq = jnp.sum(spacing * spacing, axis=1)
    deformed_sq = jnp.sum(stretched * stretched, axis=1)
    length = jnp.sqrt(length_sq)
    extension = jnp.sqrt(deformed_sq) - length
    influence = jnp.exp(-length_sq / HORIZON_SQ)
    return (stretched, deformed_sq, length, extension, influence)


def bond_pass(source, target, weight, phase_no):
    stretched, deformed_sq, length, extension, influence = bond_geometry(source, target)
    if phase_no == 1:
        bond_term = weight * influence * length * extension
        return (jnp.sum(bond_term, axis=2)[:, None, :], jnp.sum(bond_term, axis=1)[:, None, :])
    own_state = influence * (
        source[:, 6, :, None] * source[:, 8, :, None] * length + source[:, 7, :, None] * extension
    )
    other_state = influence * (
        target[:, 6, None, :] * target[:, 8, None, :] * length + target[:, 7, None, :] * extension
    )
    magnitude = weight * (own_state + other_state) / jnp.sqrt(deformed_sq + SOFTEN)
    bond_force = magnitude[:, None] * stretched
    return (jnp.sum(bond_force, axis=3), -jnp.sum(bond_force, axis=2))


def sweep_blocks(
    point_table, source_list, target_list, damage_all, begin_slot, finish, phase_no, row_width
):
    extent = point_table.shape[0]
    points = point_table.shape[-1]
    cluster_ids = jnp.arange(extent, dtype=jnp.int32)
    upper_tri = lax.broadcasted_iota(jnp.int32, (points, points), 0) < lax.broadcasted_iota(
        jnp.int32, (points, points), 1
    )

    def turn(group_index, accumulated):
        first_slot = group_index * GROUP_SLOTS
        slot_ids = first_slot + jnp.arange(GROUP_SLOTS, dtype=jnp.int32)
        usable = (slot_ids >= begin_slot) & (slot_ids < finish)
        source_ids = jnp.where(
            usable, lax.dynamic_slice_in_dim(source_list, first_slot, GROUP_SLOTS), 0
        )
        target_ids = jnp.where(
            usable, lax.dynamic_slice_in_dim(target_list, first_slot, GROUP_SLOTS), 0
        )
        damage_slab = lax.dynamic_slice_in_dim(damage_all, first_slot, GROUP_SLOTS)
        keeper = (
            jnp.where((source_ids == target_ids)[:, None, None], upper_tri[None], True)
            & usable[:, None, None]
        )
        weight = jnp.where(
            keeper, damage_slab.astype(jnp.float32), jnp.zeros(damage_slab.shape, jnp.float32)
        )
        source_rows = jnp.take(point_table, source_ids, axis=0)
        target_rows = jnp.take(point_table, target_ids, axis=0)
        source_part, target_part = bond_pass(source_rows, target_rows, weight, phase_no)
        source_hot = (source_ids[:, None] == cluster_ids[None]).astype(jnp.float32)
        target_hot = (target_ids[:, None] == cluster_ids[None]).astype(jnp.float32)
        accumulated = accumulated + jnp.dot(
            source_hot.T,
            source_part.reshape(GROUP_SLOTS, row_width * points),
            precision=lax.Precision.HIGHEST,
            preferred_element_type=jnp.float32,
        )
        accumulated = accumulated + jnp.dot(
            target_hot.T,
            target_part.reshape(GROUP_SLOTS, row_width * points),
            precision=lax.Precision.HIGHEST,
            preferred_element_type=jnp.float32,
        )
        return accumulated

    empty = jnp.zeros((extent, row_width * points), jnp.float32)
    return lax.fori_loop(
        begin_slot // GROUP_SLOTS, (finish + GROUP_SLOTS - 1) // GROUP_SLOTS, turn, empty
    )


def body(
    position, displacement, velocity, bulk, shear, volume, edges, block_pairs, block_counts, damage
):
    points = damage.shape[-1]
    clusters = position.shape[-1] // points

    def clustered(quantity):
        row_count = quantity.shape[0]
        return jnp.transpose(quantity.reshape(row_count, clusters, points), (1, 0, 2))

    def flattened(quantity):
        return jnp.transpose(quantity, (1, 0, 2)).reshape(
            quantity.shape[1], 1, 1, clusters * points
        )

    point_positions = clustered(position)
    moving_state = clustered(displacement)
    velocities = clustered(velocity)
    weighted_volume = clustered(volume)
    bulk_modulus = clustered(bulk)
    shear_modulus = clustered(shear)
    dilatation_factor = (3.0 * bulk_modulus - 5.0 * shear_modulus) / weighted_volume
    deviatoric_factor = 15.0 * shear_modulus / weighted_volume
    circ_ids = edges[0, 0, 0]
    axial_ids = edges[0, 0, 1]
    source_list = block_pairs[0, 0, 0]
    target_list = block_pairs[0, 0, 1]
    total_count = block_counts[0, 0, 1]
    damage_all = damage[0, 0]

    def pull_edges(stacked):
        upward = from_behind(stacked[circ_ids], "circ", -1)
        axially = shifted(stacked[axial_ids], "axial", -1)
        return (upward, axially)

    def push_edges(partials):
        upward = from_behind(partials[clusters : clusters + FACING], "circ", 1)
        axially = shifted(partials[clusters + FACING :], "axial", 1)
        return partials[:clusters].at[circ_ids].add(upward).at[axial_ids].add(axially)

    def evaluate(local_table, upper_table, after_table, phase_no, row_width):
        full_table = jnp.concatenate([local_table, upper_table, after_table], axis=0)
        summed = sweep_blocks(
            full_table, source_list, target_list, damage_all, 0, total_count, phase_no, row_width
        )
        return summed.reshape(summed.shape[0], row_width, points)

    dilatation = jnp.zeros_like(weighted_volume)
    static_point_rows = jnp.concatenate(
        [point_positions, dilatation_factor, deviatoric_factor], axis=1
    )
    upper_static, after_static = pull_edges(static_point_rows)
    for step_index in range(TIME_STEPS):
        upper_move, after_move = pull_edges(moving_state)
        first_local = jnp.concatenate([point_positions, moving_state], axis=1)
        first_upper = jnp.concatenate([upper_static[:, 0:3], upper_move], axis=1)
        first_after = jnp.concatenate([after_static[:, 0:3], after_move], axis=1)
        partials = evaluate(first_local, first_upper, first_after, 1, 1)
        dilatation = 3.0 * push_edges(partials) / weighted_volume
        upper_theta, after_theta = pull_edges(dilatation)
        second_local_part = jnp.concatenate(
            [point_positions, moving_state, dilatation_factor, deviatoric_factor, dilatation],
            axis=1,
        )
        second_upper = jnp.concatenate(
            [upper_static[:, 0:3], upper_move, upper_static[:, 3:5], upper_theta], axis=1
        )
        second_after = jnp.concatenate(
            [after_static[:, 0:3], after_move, after_static[:, 3:5], after_theta], axis=1
        )
        partials = evaluate(second_local_part, second_upper, second_after, 2, 3)
        force = push_edges(partials)
        velocities = velocities + TIMESTEP * force
        moving_state = moving_state + TIMESTEP * velocities
    return (flattened(moving_state), flattened(velocities), flattened(dilatation)[0])


def solution(mesh):
    placed = (
        P(None, "circ", "axial", None),
        P(None, "circ", "axial", None),
        P(None, "circ", "axial", None),
        P("circ", "axial", None),
        P("circ", "axial", None),
        P("circ", "axial", None),
        P("circ", "axial", None, None),
        P("circ", "axial", None, None),
        P("circ", "axial", None),
        P("circ", "axial", None, None, None),
    )
    return jax.shard_map(
        body,
        mesh=mesh,
        in_specs=placed,
        out_specs=(
            P(None, "circ", "axial", None),
            P(None, "circ", "axial", None),
            P("circ", "axial", None),
        ),
        check_vma=False,
    )
```

profile of v0, /device:TPU:43, one launch (start us, length us, event | category | flops | bytes accessed | tf_op | source)
XLA Modules:
  0.0 791.7 jit_solution(624399127797896220)
XLA Ops:
  19.9 108.3 %while.48 = (s32[]{:T(128)}, f32[192,128]{1,0:T(8,128)S(1)}, s32[]{:T(128)}, s32[]{:T(128)}, s32[320]{0:T(512)S(1)}, /*index=5*/s32[320]{0:T(512)S(1)}, s32[320,...) while((s32[]{:T(128)}, f32[192,128]{1,0:T(8,128)S(1)}, ...), condition=%wide.region_5.7_spmd.clone.clone, body=%wide.region_0.6_spmd.clone.clone.sunk | while | flops 17396116 | bytes 6399283 | solution.py:104
  128.2 38.2 %collective-permute-start.4 = (f32[32,1,128]{2,0,1:T(8,128)S(1)}, f32[32,1,128]{2,0,1:T(8,128)S(1)}, u32[]{:S(2)}, u32[]{:S(2)}) collective-permute-start(f32[32,1,128]{2,0,1:T(8,128)S(1)} %get-tuple-element.603), channel_id=1, source_target_pairs={{112,0},{0,16},{16,32},{32,48},{48,64},{64,80},{80,96},{96,112},{1... | collective-permute-start | bytes 49160 | tf_op jit(solution)/shard_map/ppermute | solution.py:19
  166.3 3.7 collective-permute-start.5
  180.6 156.3 %while.49 = (s32[]{:T(128)}, f32[192,384]{1,0:T(8,128)S(1)}, s32[]{:T(128)}, s32[]{:T(128)}, s32[320]{0:T(512)S(1)}, /*index=5*/s32[320]{0:T(512)S(1)}, s32[320,...) while((s32[]{:T(128)}, f32[192,384]{1,0:T(8,128)S(1)}, ...), condition=%wide.region_13.16_spmd.clone.clone, body=%wide.region_8.15_spmd.clone.clone.sunk | while | flops 42674580 | bytes 9807155 | solution.py:104
  187.3 2.9 fusion.136
  197.7 2.9 fusion.136
  208.1 2.9 fusion.136
  218.5 2.9 fusion.136
  239.3 2.9 fusion.136
  270.6 2.9 fusion.136
  291.4 2.9 fusion.136
  336.9 54.8 %collective-permute-start.8 = (f32[32,3,128]{2,1,0:T(4,128)S(1)}, f32[32,3,128]{2,1,0:T(4,128)S(1)}, u32[]{:S(2)}, u32[]{:S(2)}) collective-permute-start(f32[32,3,128]{2,1,0:T(4,128)S(1)} %slice.209), channel_id=1, source_target_pairs={{112,0},{0,16},{16,32},{32,48},{48,64},{64,80},{80,96},{96,112},{1... | collective-permute-start | bytes 147464 | tf_op jit(solution)/shard_map/ppermute | solution.py:19
  391.7 4.1 collective-permute-start.9
  408.3 108.2 %while.50 = (s32[]{:T(128)}, f32[192,128]{1,0:T(8,128)S(1)}, s32[]{:T(128)}, s32[]{:T(128)}, s32[320]{0:T(512)S(1)}, /*index=5*/s32[320]{0:T(512)S(1)}, s32[320,...) while((s32[]{:T(128)}, f32[192,128]{1,0:T(8,128)S(1)}, ...), condition=%wide.region_21.24_spmd.clone.clone, body=%wide.region_16.23_spmd.clone.clone.sunk | while | flops 17396116 | bytes 6399283 | solution.py:104
  516.6 39.0 %collective-permute-start.12 = (f32[32,1,128]{2,0,1:T(8,128)S(1)}, f32[32,1,128]{2,0,1:T(8,128)S(1)}, u32[]{:S(2)}, u32[]{:S(2)}) collective-permute-start(f32[32,1,128]{2,0,1:T(8,128)S(1)} %get-tuple-element.601), channel_id=1, source_target_pairs={{112,0},{0,16},{16,32},{32,48},{48,64},{64,80},{80,96},{96,112},{1... | collective-permute-start | bytes 49160 | tf_op jit(solution)/shard_map/ppermute | solution.py:19
  555.6 4.2 collective-permute-start.13
  570.5 156.3 %while.51 = (s32[]{:T(128)}, f32[192,384]{1,0:T(8,128)S(1)}, s32[]{:T(128)}, s32[]{:T(128)}, s32[320]{0:T(512)S(1)}, /*index=5*/s32[320]{0:T(512)S(1)}, s32[320,...) while((s32[]{:T(128)}, f32[192,384]{1,0:T(8,128)S(1)}, ...), condition=%wide.region_29.32_spmd.clone.clone, body=%wide.region_24.31_spmd.clone.clone.sunk | while | flops 42674580 | bytes 9807155 | solution.py:104
  587.6 2.9 fusion.151
  608.5 2.9 fusion.151
  639.7 2.9 fusion.151
  660.5 2.9 fusion.151
  712.6 2.9 fusion.151
  726.8 54.7 %collective-permute-start.16 = (f32[32,3,128]{2,1,0:T(4,128)S(1)}, f32[32,3,128]{2,1,0:T(4,128)S(1)}, u32[]{:S(2)}, u32[]{:S(2)}) collective-permute-start(f32[32,3,128]{2,1,0:T(4,128)S(1)} %slice.221), channel_id=1, source_target_pairs={{112,0},{0,16},{16,32},{32,48},{48,64},{64,80},{80,96},{96,112},{1... | collective-permute-start | bytes 147464 | tf_op jit(solution)/shard_map/ppermute | solution.py:19
  781.6 3.6 collective-permute-start.17
  (1209 shorter events, 543.6 us)
Async XLA Ops:
  4.3 13.3 %collective-permute-start = (f32[32,5,128]{2,1,0:T(8,128)S(1)}, f32[32,5,128]{2,1,0:T(8,128)S(1)}, u32[]{:S(2)}, u32[]{:S(2)}) collective-permute-start(f32[32,5,128]{2,1,0:T(8,128)S(1)} %gather_fusion.8), channel_id=1, source_target_pairs={{16,0},{32,16},{48,32},{64,48},{80,64},{96,80},{112,96},{0,112},{1... | collective-permute-start | bytes 245768 | tf_op jit(solution)/shard_map/ppermute | solution.py:19
  6.5 11.1 %collective-permute-start.2 = (f32[32,5,128]{2,1,0:T(8,128)S(1)}, f32[32,5,128]{2,1,0:T(8,128)S(1)}, u32[]{:S(2)}, u32[]{:S(2)}) collective-permute-start(f32[32,5,128]{2,1,0:T(8,128)S(1)} %gather_fusion.10), channel_id=1, source_target_pairs={{1,0},{2,1},{3,2},{4,3},{5,4},{6,5},{7,6},{8,7},{9,8},{10,9},{11,1... | collective-permute-start | bytes 245768 | tf_op jit(solution)/shard_map/ppermute | solution.py:25
  11.1 6.6 collective-permute-start.1
  12.7 6.5 collective-permute-start.3
  17.7 390.0 %copy-start.2 = (f32[32,3,128]{2,1,0:T(4,128)}, f32[32,3,128]{2,1,0:T(4,128)S(1)}, u32[]{:S(2)}) copy-start(f32[32,3,128]{2,1,0:T(4,128)S(1)} %slice.345) | copy-start | bytes 147460
  128.2 41.9 %collective-permute-start.4 = (f32[32,1,128]{2,0,1:T(8,128)S(1)}, f32[32,1,128]{2,0,1:T(8,128)S(1)}, u32[]{:S(2)}, u32[]{:S(2)}) collective-permute-start(f32[32,1,128]{2,0,1:T(8,128)S(1)} %get-tuple-element.603), channel_id=1, source_target_pairs={{112,0},{0,16},{16,32},{32,48},{48,64},{64,80},{80,96},{96,112},{1... | collective-permute-start | bytes 49160 | tf_op jit(solution)/shard_map/ppermute | solution.py:19
  166.3 4.5 collective-permute-start.5
  172.8 4.2 collective-permute-start.6
  172.9 6.5 collective-permute-start.7
  180.5 218.9 %copy-start.9 = (f32[3,1,1,16384]{3,2,1,0:T(1,128)S(1)}, f32[3,1,1,16384]{3,2,1,0:T(1,128)}, u32[]{:S(2)}) copy-start(f32[3,1,1,16384]{3,2,1,0:T(1,128)} %param.23) | copy-start | bytes 589828
  180.6 218.9 %copy-start.10 = (f32[3,1,1,16384]{3,2,1,0:T(1,128)S(1)}, f32[3,1,1,16384]{3,2,1,0:T(1,128)}, u32[]{:S(2)}) copy-start(f32[3,1,1,16384]{3,2,1,0:T(1,128)} %param.24) | copy-start | bytes 589828
  336.9 59.2 %collective-permute-start.8 = (f32[32,3,128]{2,1,0:T(4,128)S(1)}, f32[32,3,128]{2,1,0:T(4,128)S(1)}, u32[]{:S(2)}, u32[]{:S(2)}) collective-permute-start(f32[32,3,128]{2,1,0:T(4,128)S(1)} %slice.209), channel_id=1, source_target_pairs={{112,0},{0,16},{16,32},{32,48},{48,64},{64,80},{80,96},{96,112},{1... | collective-permute-start | bytes 147464 | tf_op jit(solution)/shard_map/ppermute | solution.py:19
  391.7 6.1 collective-permute-start.9
  401.0 4.7 collective-permute-start.10
  401.1 6.6 collective-permute-start.11
  516.6 43.3 %collective-permute-start.12 = (f32[32,1,128]{2,0,1:T(8,128)S(1)}, f32[32,1,128]{2,0,1:T(8,128)S(1)}, u32[]{:S(2)}, u32[]{:S(2)}) collective-permute-start(f32[32,1,128]{2,0,1:T(8,128)S(1)} %get-tuple-element.601), channel_id=1, source_target_pairs={{112,0},{0,16},{16,32},{32,48},{48,64},{64,80},{80,96},{96,112},{1... | collective-permute-start | bytes 49160 | tf_op jit(solution)/shard_map/ppermute | solution.py:19
  555.6 5.1 collective-permute-start.13
  562.7 4.5 collective-permute-start.14
  562.8 6.5 collective-permute-start.15
  570.5 217.5 %copy-start.20 = (s32[32]{0:T(128)S(1)}, s32[32]{0:T(128)}, u32[]{:S(2)}) copy-start(s32[32]{0:T(128)} %copy-done.18) | copy-start | bytes 388
  570.5 219.1 %copy-start.1 = (f32[128,3,128]{2,1,0:T(4,128)S(1)}, f32[128,3,128]{2,1,0:T(4,128)}, u32[]{:S(2)}) copy-start(f32[128,3,128]{2,1,0:T(4,128)} %copy-done) | copy-start | bytes 589828
  570.5 219.1 %copy-start.11 = (f32[3,1,1,16384]{3,2,1,0:T(1,128)S(1)}, f32[3,1,1,16384]{3,2,1,0:T(1,128)}, u32[]{:S(2)}) copy-start(f32[3,1,1,16384]{3,2,1,0:T(1,128)} %param.24) | copy-start | bytes 589828
  726.8 59.5 %collective-permute-start.16 = (f32[32,3,128]{2,1,0:T(4,128)S(1)}, f32[32,3,128]{2,1,0:T(4,128)S(1)}, u32[]{:S(2)}, u32[]{:S(2)}) collective-permute-start(f32[32,3,128]{2,1,0:T(4,128)S(1)} %slice.221), channel_id=1, source_target_pairs={{112,0},{0,16},{16,32},{32,48},{48,64},{64,80},{80,96},{96,112},{1... | collective-permute-start | bytes 147464 | tf_op jit(solution)/shard_map/ppermute | solution.py:19
  781.6 6.4 collective-permute-start.17
  (18 other events, 2247.4 us)
where the time goes:
time: 800 us; the launch traced here: 792 us
  other arithmetic  422 us (53%)
  starting transfers between devices  216 us (27%)
  local copies, waits for them, and re-layouts  84.5 us (11%)
  matrix products  44.8 us (6%)
  waiting for transfers between devices  13.8 us (2%)
  loops' own time  8.57 us (1%)
    ppermute x9, starting transfers between devices, from_behind(): return lax.ppermute(block, axis, route)  190 us
    reduce_sum x60, other arithmetic, bond_geometry(): length_sq = jnp.sum(spacing * spacing, axis=1)  125 us
    reduce_sum x30, other arithmetic, bond_pass(): return (jnp.sum(bond_force, axis=3), -jnp.sum(bond_force, axis=2))  87.9 us
    div x30, other arithmetic, bond_pass(): weight * (own_state + other_state) / jnp.sqrt(deformed_sq + SOFTEN)  70 us
    reduce_sum x30, other arithmetic, bond_pass(): jnp.sum(bond_term, axis=1)[:, None, :]  67.8 us
    eq x60, other arithmetic, turn(): source_ids == target_ids  42.1 us
    gather x60, local copies, waits for them, and re-layouts, turn(): target_rows = jnp.take(point_table, target_ids, axis=0)  33.9 us
    gather x60, local copies, waits for them, and re-layouts, turn(): source_rows = jnp.take(point_table, source_ids, axis=0)  33.9 us
  transfers between devices with their start and end apart: 18, of which 7 were waited for; matrix products, arithmetic and copies ran while one was open for 2% of the time, Pallas kernels for 0%

commit v1 on v0

v1 whole, which is shorter than its diff:
```python
import functools

import jax
import jax.numpy as jnp
from jax import lax
from jax.experimental import pallas as pl
from jax.experimental.pallas import tpu as pltpu
from jax.sharding import PartitionSpec as P

PTS = 128
CL = 128
FACING = 32
EXT = CL + 2 * FACING
SLOTS = 320
STEPS = 2
TIMESTEP = 0.07
SOFTEN = 0.01
LOG2E = 1.4426950408889634
KAPPA = LOG2E**0.5
TINY = 1e-30
GROUP = 16
UNROLL = 8
OWN = CL * PTS
GHOST = FACING * PTS
F32 = jnp.float32
BF16 = jnp.bfloat16
NT = (((1,), (1,)), ((), ()))
NN = (((1,), (0,)), ((), ()))


def lanes(c):
    return pl.ds(pl.multiple_of(c * PTS, PTS), PTS)


def dot(a, b, dims):
    return lax.dot_general(a, b, dims, preferred_element_type=F32)


def split3(x):
    h = x.astype(BF16).astype(F32)
    rest = x - h
    m = rest.astype(BF16).astype(F32)
    return h, m, rest - m


def hilo(x):
    h = x.astype(BF16)
    return h, (x - h.astype(F32)).astype(BF16)


def rows8():
    return lax.broadcasted_iota(jnp.int32, (8, PTS), 0)


def coordinate_parts(s):
    row = rows8()
    sq = s * s
    nx = sq[0:1] + sq[1:2] + sq[2:3]
    ny = sq[4:5] + sq[5:6] + sq[6:7]
    full = jnp.where(row == 3, nx, jnp.where(row == 7, ny, s))
    return split3(full)


def source_features(parts):
    p0, p1, p2 = parts
    one = jnp.ones((8, PTS), F32)
    stack = jnp.concatenate([p0, p0, p0, p1, p1, p2, one, one], axis=0)
    return jnp.transpose(stack).astype(BF16)


def target_features(parts):
    p0, p1, p2 = parts
    row = rows8()
    norm = (row == 3) | (row == 7)
    a0 = jnp.where(norm, -1.0, 2.0 * p0)
    a1 = jnp.where(norm, 0.0, 2.0 * p1)
    a2 = jnp.where(norm, 0.0, 2.0 * p2)
    n0 = jnp.where(norm, -p0, 0.0)
    shifted = pltpu.roll(p2, 1, 0)
    n1 = jnp.where(norm, -p1, 0.0)
    upper = row < 4
    after = (row == 4) | (row == 0)
    stack = jnp.concatenate([a0, a1, a2, a0, a1, a0], axis=0)
    up6 = jnp.concatenate([upper] * 6, axis=0)

    def half(top):
        keep = up6 if top else ~up6
        body = jnp.where(keep, stack, 0.0)
        near = upper if top else ~upper
        tail0 = jnp.where(near, n0, 0.0)
        tail1 = jnp.where(near, n1, 0.0) - jnp.where(row == (4 if top else 0), shifted, 0.0)
        return jnp.concatenate([body, tail0, tail1], axis=0).astype(BF16)

    return half(True), half(False)


def moment_features(parts):
    p0, p1, p2 = parts
    row = rows8()
    first = jnp.where(row == 3, 1.0, jnp.where(row > 3, p0, 0.0))
    first = jnp.where(row == 7, 0.0, first)
    second = jnp.where((row > 3) & (row < 7), p1, 0.0) + jnp.where(
        row < 3, pltpu.roll(p2, 4, 0), 0.0
    )
    m = jnp.concatenate([first, second], axis=0).astype(BF16)
    return jnp.concatenate([m, m], axis=1)


def pack_kernel(edges, x_ref, u_ref, v_ref, bulk, shear, volume, s_out, v_out, mean, send_c, send_a):
    chunk = 2048
    zero = jnp.zeros((1, chunk), F32)

    def turn(i, total):
        sl = pl.ds(pl.multiple_of(i * chunk, chunk), chunk)
        x = KAPPA * x_ref[:, sl]
        y = x + KAPPA * u_ref[:, sl]
        s = jnp.concatenate([x, zero, y, zero], axis=0)
        s_out[:, sl] = s
        vol = volume[:, sl]
        mu = shear[:, sl]
        dil = (3.0 * bulk[:, sl] - 5.0 * mu) / vol
        dev = 15.0 * mu / vol
        thr = (3.0 / LOG2E) / vol
        v_out[:, sl] = jnp.concatenate([dil, dev, thr, zero, KAPPA * v_ref[:, sl], zero], axis=0)
        return total + jnp.sum(s, axis=1, keepdims=True)

    total = lax.fori_loop(0, OWN // chunk, turn, jnp.zeros((8, 1), F32))
    mean[...] = jnp.broadcast_to(total * (1.0 / OWN), (8, PTS))

    def copy(f, _):
        for side, out in ((0, send_c), (1, send_a)):
            e = edges[side, f]
            out[0:8, lanes(f)] = s_out[:, lanes(e)]
            out[8:16, lanes(f)] = v_out[:, lanes(e)]
        return 0

    lax.fori_loop(0, FACING, copy, 0, unroll=4)


def each_cluster(own, ghost_c, ghost_a, fn, unroll):
    lax.fori_loop(0, CL, lambda c, _: (fn(c, own[:, lanes(c)]), 0)[1], 0, unroll=unroll)
    lax.fori_loop(
        0, FACING, lambda c, _: (fn(CL + c, ghost_c[:, lanes(c)]), 0)[1], 0, unroll=unroll
    )
    lax.fori_loop(
        0,
        FACING,
        lambda c, _: (fn(CL + FACING + c, ghost_a[:, lanes(c)]), 0)[1],
        0,
        unroll=unroll,
    )


def build_geometry(c, s, left, right, moments):
    parts = coordinate_parts(s)
    if left is not None:
        left[jnp.minimum(c, CL)] = source_features(parts)
    t0, t1 = target_features(parts)
    right[c, :, 0:PTS] = t0
    right[c, :, PTS:] = t1
    if moments is not None:
        moments[c] = moment_features(parts)


def slot_ids(pairs, counts, slot):
    p = pairs[0, slot]
    q = pairs[1, slot]
    live = slot < counts[1]
    return p, q, jnp.where(live, p, EXT), jnp.where(live, q, EXT)


def for_groups(counts, one_turn):
    g = pl.program_id(0)

    @pl.when(g * GROUP < counts[1])
    def _():
        def turn(i, _):
            one_turn(g * GROUP + i * UNROLL, i * UNROLL)
            return 0

        lax.fori_loop(0, GROUP // UNROLL, turn, 0)


def first_sums(pairs, counts, base, inner, weight_of, left, right, acc):
    ones = jnp.ones((16, 2 * PTS), BF16)
    found = []
    for j in range(UNROLL):
        p, q, pa, qa = slot_ids(pairs, counts, base + j)
        ab = dot(left[p], right[q], NN)
        na = ab[:, :PTS]
        nb = ab[:, PTS:]
        w = weight_of(na, inner + j, base + j)
        x = jnp.maximum(na * nb, TINY)
        t = (x * lax.rsqrt(x) + na) * w
        h, l = hilo(t)
        both_q = dot(ones, jnp.concatenate([h, l], axis=0), NN)
        both_p = dot(ones, jnp.concatenate([h, l], axis=1), NT)
        found.append((pa, qa, both_p, both_q))
    for pa, qa, gp, gq in found:
        acc[qa] += gq[0:8]
        acc[pa] += gp[0:8]


def send_rows(edges, acc_row, own_out, gc_out, ga_out, send_c, send_a):
    def own(c, _):
        own_out[:, lanes(c)] = acc_row(c)
        return 0

    lax.fori_loop(0, CL, own, 0, unroll=4)

    def ghost(f, _):
        gc_out[:, lanes(f)] = acc_row(CL + f)
        ga_out[:, lanes(f)] = acc_row(CL + FACING + f)
        send_c[:, lanes(f)] = acc_row(edges[0, f])
        send_a[:, lanes(f)] = acc_row(edges[1, f])
        return 0

    lax.fori_loop(0, FACING, ghost, 0, unroll=4)


def zero_acc(acc):
    acc[...] = jnp.zeros_like(acc)


def dilatation_first(
    pairs, counts, edges, s_own, s_c, s_a, mean, damage,
    w_out, n_own, n_c, n_a, send_c, send_a,
    left, right, acc, cut,
):
    g = pl.program_id(0)

    @pl.when(g == 0)
    def _():
        zero_acc(acc)
        i0 = lax.broadcasted_iota(jnp.int32, (PTS, PTS), 0)
        i1 = lax.broadcasted_iota(jnp.int32, (PTS, PTS), 1)
        cut[0] = jnp.where(i0 < i1, 0, 1)
        cut[1] = jnp.zeros((PTS, PTS), jnp.int32)
        shift = mean[...]
        fn = lambda c, s: build_geometry(c, s[0:8] - shift, left, right, None)
        each_cluster(s_own, s_c, s_a, fn, 2)

    def weight_of(na, k, slot):
        keep = damage[k] > cut[jnp.where(slot < CL, 0, 1)]
        w = jnp.where(keep, jnp.exp2(na), 0.0)
        w_out[k] = w
        return w

    for_groups(
        counts,
        lambda base, inner: first_sums(pairs, counts, base, inner, weight_of, left, right, acc),
    )

    @pl.when(g == pl.num_programs(0) - 1)
    def _():
        row = lambda c: acc[c, 0:1, :]
        send_rows(edges, row, n_own, n_c, n_a, send_c, send_a)


def dilatation_again(
    pairs, counts, edges, s_own, s_c, s_a, v_own, v_c, v_a, mean, f_own, f_c, f_a,
    up_c, up_a, back_c, back_a, weights,
    s_own2, s_c2, s_a2, v_own2, v_c2, v_a2, n_own, n_c, n_a, send_c, send_a,
    left, right, acc,
):
    g = pl.program_id(0)

    @pl.when(g == 0)
    def _():
        zero_acc(acc)
        advance(edges, s_own, s_c, s_a, v_own, v_c, v_a, f_own, f_c, f_a, up_c, up_a, back_c,
                back_a, s_own2, s_c2, s_a2, v_own2, v_c2, v_a2)
        shift = mean[...]
        fn = lambda c, s: build_geometry(c, s[0:8] - shift, left, right, None)
        each_cluster(s_own2, s_c2, s_a2, fn, 2)

    weight_of = lambda na, k, slot: weights[k]
    for_groups(
        counts,
        lambda base, inner: first_sums(pairs, counts, base, inner, weight_of, left, right, acc),
    )

    @pl.when(g == pl.num_programs(0) - 1)
    def _():
        row = lambda c: acc[c, 0:1, :]
        send_rows(edges, row, n_own, n_c, n_a, send_c, send_a)


def advance(edges, s_own, s_c, s_a, v_own, v_c, v_a, f_own, f_c, f_a, up_c, up_a, back_c, back_a,
            s_own2, s_c2, s_a2, v_own2, v_c2, v_a2):
    pad = jnp.zeros((4, PTS), F32)

    def moved(s, v, f):
        f8 = jnp.concatenate([pad, f], axis=0)
        v2 = v + TIMESTEP * f8
        keep = rows8() < 4
        return s + jnp.where(keep, 0.0, TIMESTEP * v2), v2

    def own(c, _):
        s2, v2 = moved(s_own[:, lanes(c)], v_own[:, lanes(c)], f_own[:, lanes(c)])
        s_own2[:, lanes(c)] = s2
        v_own2[:, lanes(c)] = v2
        return 0

    lax.fori_loop(0, CL, own, 0, unroll=4)

    def ghost(f, _):
        for side, back in ((0, back_c), (1, back_a)):
            e = edges[side, f]
            total = f_own[:, lanes(e)] + back[:, lanes(f)]
            s2, v2 = moved(s_own[:, lanes(e)], v_own[:, lanes(e)], total)
            s_own2[:, lanes(e)] = s2
            v_own2[:, lanes(e)] = v2
        for s, v, part, up, s_out, v_out in (
            (s_c, v_c, f_c, up_c, s_c2, v_c2),
            (s_a, v_a, f_a, up_a, s_a2, v_a2),
        ):
            total = up[:, lanes(f)] + part[:, lanes(f)]
            s2, v2 = moved(s[0:8, lanes(f)], v[:, lanes(f)], total)
            s_out[:, lanes(f)] = s2
            v_out[:, lanes(f)] = v2
        return 0

    lax.fori_loop(0, FACING, ghost, 0, unroll=2)


def force_pass(
    pairs, counts, edges, s_own, s_c, s_a, v_own, v_c, v_a, mean, n_own, n_c, n_a,
    up_c, up_a, back_c, back_a, weights,
    theta_out, f_own, f_c, f_a, send_c, send_a,
    left, right, moments, acc, n_full, coef_row, coef_col,
):
    g = pl.program_id(0)

    @pl.when(g == 0)
    def _():
        zero_acc(acc)
        shift = mean[...]
        fn = lambda c, s: build_geometry(c, s[0:8] - shift, left, right, moments)
        each_cluster(s_own, s_c, s_a, fn, 2)
        n_full[:, 0:OWN] = n_own[...]

        def mend(f, _):
            n_full[:, lanes(edges[0, f])] = n_own[:, lanes(edges[0, f])] + back_c[:, lanes(f)]
            n_full[:, lanes(edges[1, f])] = n_own[:, lanes(edges[1, f])] + back_a[:, lanes(f)]
            n_full[:, lanes(CL + f)] = up_c[:, lanes(f)] + n_c[:, lanes(f)]
            n_full[:, lanes(CL + FACING + f)] = up_a[:, lanes(f)] + n_a[:, lanes(f)]
            return 0

        lax.fori_loop(0, FACING, mend, 0, unroll=4)

        def coefs(c, v):
            theta = v[2:3] * n_full[:, lanes(c)]
            dev = v[1:2]
            minus = dev - v[0:1] * theta
            row = jnp.concatenate([minus, -dev, theta, jnp.zeros((5, PTS), F32)], axis=0)
            coef_row[c] = row
            return row

        def own(c, _):
            row = coefs(c, v_own[:, lanes(c)])
            theta_out[:, lanes(c)] = row[2:3]
            coef_col[c] = jnp.transpose(row)
            return 0

        lax.fori_loop(0, CL, own, 0, unroll=4)

        def ghost(f, _):
            coefs(CL + f, v_c[:, lanes(f)])
            coefs(CL + FACING + f, v_a[:, lanes(f)])
            return 0

        lax.fori_loop(0, FACING, ghost, 0, unroll=4)

    def turn(base, inner):
        found = []
        for j in range(UNROLL):
            p, q, pa, qa = slot_ids(pairs, counts, base + j)
            ab = dot(left[p], right[q], NN)
            na = jnp.minimum(ab[:, :PTS], -TINY)
            nb = jnp.minimum(ab[:, PTS:], -TINY)
            nu = nb - SOFTEN * LOG2E
            col = coef_col[p]
            row = coef_row[q]
            mc = jnp.broadcast_to(col[:, 0:1], (PTS, PTS)) + row[0:1]
            mb = jnp.broadcast_to(col[:, 1:2], (PTS, PTS)) + row[1:2]
            za = na * lax.rsqrt(na * nu)
            zb = nb * lax.rsqrt(nb * nu)
            m = weights[inner + j] * (mc * za + mb * zb)
            h, l = hilo(m)
            gq = dot(moments[p], jnp.concatenate([h, l], axis=0), NN)
            gp = dot(moments[q], jnp.concatenate([h, l], axis=1), NT)
            found.append((pa, qa, gp, gq))
        for pa, qa, gp, gq in found:
            acc[qa] += gq
            acc[pa] += gp

    for_groups(counts, turn)

    @pl.when(g == pl.num_programs(0) - 1)
    def _():
        shift = mean[...]

        def force(c, s):
            gsum = acc[c]
            first, second = gsum[0:8], gsum[8:16]
            y = s[0:8] - shift
            total = first + second + pltpu.roll(second, 4, 0)
            return (total - y * first[3:4])[4:8]

        def own(c, _):
            f_own[:, lanes(c)] = force(c, s_own[:, lanes(c)])
            return 0

        lax.fori_loop(0, CL, own, 0, unroll=4)

        def ghost(f, _):
            f_c[:, lanes(f)] = force(CL + f, s_c[0:8, lanes(f)])
            f_a[:, lanes(f)] = force(CL + FACING + f, s_a[0:8, lanes(f)])
            send_c[:, lanes(f)] = f_own[:, lanes(edges[0, f])]
            send_a[:, lanes(f)] = f_own[:, lanes(edges[1, f])]
            return 0

        lax.fori_loop(0, FACING, ghost, 0, unroll=4)


def finish_kernel(edges, u_ref, s_start, s_own, v_own, f_own, back_c, back_a, u_out, vel_out):
    chunk = 2048

    def turn(i, _):
        sl = pl.ds(pl.multiple_of(i * chunk, chunk), chunk)
        v2 = v_own[4:7, sl] + TIMESTEP * f_own[0:3, sl]
        vel_out[:, sl] = v2 * (1.0 / KAPPA)
        gone = (s_own[4:7, sl] - s_start[4:7, sl]) + TIMESTEP * v2
        u_out[:, sl] = u_ref[:, sl] + gone * (1.0 / KAPPA)
        return 0

    lax.fori_loop(0, OWN // chunk, turn, 0)

    def mend(f, _):
        for side, back in ((0, back_c), (1, back_a)):
            sl = lanes(edges[side, f])
            more = (TIMESTEP / KAPPA) * back[0:3, lanes(f)]
            vel_out[:, sl] = vel_out[:, sl] + more
            u_out[:, sl] = u_out[:, sl] + TIMESTEP * more
        return 0

    lax.fori_loop(0, FACING, mend, 0, unroll=4)


SMEM = pl.BlockSpec(memory_space=pltpu.SMEM)
VMEM = pl.BlockSpec(memory_space=pltpu.VMEM)


def table(rows, n):
    return jax.ShapeDtypeStruct((rows, n), F32)


def slab_spec():
    def index(g, pairs, counts):
        return (jnp.minimum(g, (counts[1] - 1) // GROUP), 0, 0)

    return pl.BlockSpec((GROUP, PTS, PTS), index)


def sweep(kernel, name, pairs, counts, edges, tables, slab, out_tables, scratch, slab_out=None):
    spec = lambda *shape: pl.BlockSpec(shape, lambda g, a, b: (0, 0))
    whole = [pl.BlockSpec(x.shape, lambda g, a, b: (0, 0), pipeline_mode=pl.Buffered(1)) for x in tables]
    outs = [spec(*x.shape) for x in out_tables]
    out_shape = list(out_tables)
    if slab_out is not None:
        outs = [slab_spec()] + outs
        out_shape = [slab_out] + out_shape
    return pl.pallas_call(
        kernel,
        out_shape=out_shape,
        grid_spec=pltpu.PrefetchScalarGridSpec(
            num_scalar_prefetch=2,
            grid=(SLOTS // GROUP,),
            in_specs=[SMEM] + whole + [slab_spec()],
            out_specs=outs,
            scratch_shapes=scratch,
        ),
        compiler_params=pltpu.CompilerParams(
            dimension_semantics=("arbitrary",), vmem_limit_bytes=56 << 20
        ),
        name=name,
    )(pairs, counts, edges, *tables, slab)


LEFT = pltpu.VMEM((CL + 1, PTS, 64), BF16)
RIGHT = pltpu.VMEM((EXT, 64, 2 * PTS), BF16)
N_TABLES = [table(1, OWN)] + [table(1, GHOST)] * 4
F_TABLES = [table(4, OWN)] + [table(4, GHOST)] * 4


def run_first(pairs, counts, edges, s_own, s_c, s_a, mean, damage):
    return sweep(
        dilatation_first, "dil0", pairs, counts, edges, [s_own, s_c, s_a, mean], damage, N_TABLES,
        [LEFT, RIGHT, pltpu.VMEM((EXT + 1, 8, PTS), F32), pltpu.VMEM((2, PTS, PTS), jnp.int32)],
        slab_out=jax.ShapeDtypeStruct((SLOTS, PTS, PTS), F32),
    )


def run_again(pairs, counts, edges, tables, weights):
    states = [table(8, OWN), table(8, GHOST), table(8, GHOST)] * 2
    return sweep(
        dilatation_again, "dil1", pairs, counts, edges, tables, weights, states + N_TABLES,
        [LEFT, RIGHT, pltpu.VMEM((EXT + 1, 8, PTS), F32)],
    )


def run_force(pairs, counts, edges, tables, weights):
    return sweep(
        force_pass, "force", pairs, counts, edges, tables, weights, [table(1, OWN)] + F_TABLES,
        [
            LEFT,
            RIGHT,
            pltpu.VMEM((EXT, 16, 2 * PTS), BF16),
            pltpu.VMEM((EXT + 1, 16, PTS), F32),
            pltpu.VMEM((1, EXT * PTS), F32),
            pltpu.VMEM((EXT, 8, PTS), F32),
            pltpu.VMEM((CL, PTS, 8), F32),
        ],
    )


def run_pack(edges, *args):
    return pl.pallas_call(
        pack_kernel,
        out_shape=[table(8, OWN), table(8, OWN), table(8, PTS), table(16, GHOST), table(16, GHOST)],
        in_specs=[SMEM] + [VMEM] * 6,
        out_specs=[VMEM] * 5,
        name="pack",
    )(edges, *args)


def run_finish(edges, *args):
    return pl.pallas_call(
        finish_kernel,
        out_shape=[table(3, OWN), table(3, OWN)],
        in_specs=[SMEM] + [VMEM] * 7,
        out_specs=[VMEM] * 2,
        name="finish",
    )(edges, *args)


def lower(block, axis, ring):
    n = lax.axis_size(axis)
    route = [(i, (i - 1) % n) for i in range(n) if ring or i > 0]
    return lax.ppermute(block, axis, route)


def upper(block, axis, ring):
    n = lax.axis_size(axis)
    route = [(i, (i + 1) % n) for i in range(n) if ring or i < n - 1]
    return lax.ppermute(block, axis, route)


def exchange(part_c, part_a, own_c, own_a):
    return (
        lower(own_c, "circ", True),
        lower(own_a, "axial", False),
        upper(part_c, "circ", True),
        upper(part_a, "axial", False),
    )


def body(
    position, displacement, velocity, bulk, shear, volume, edges, block_pairs, block_counts, damage
):
    x = position.reshape(3, OWN)
    u = displacement.reshape(3, OWN)
    v = velocity.reshape(3, OWN)
    flat = lambda t: t.reshape(1, OWN)
    edge = edges[0, 0]
    pairs = block_pairs[0, 0]
    counts = block_counts[0, 0]
    s_own, v_own, mean, send_c, send_a = run_pack(
        edge, x, u, v, flat(bulk), flat(shear), flat(volume)
    )
    s_start = s_own
    got_c = lower(send_c, "circ", True)
    got_a = lower(send_a, "axial", False)
    s_c, s_a = got_c[:8], got_a[:8]
    v_c, v_a = got_c[8:], got_a[8:]
    weights, n_own, n_c, n_a, send_c, send_a = run_first(
        pairs, counts, edge, s_own, s_c, s_a, mean, damage[0, 0]
    )
    for step in range(STEPS):
        got = exchange(n_c, n_a, send_c, send_a)
        theta, f_own, f_c, f_a, send_c, send_a = run_force(
            pairs, counts, edge,
            [s_own, s_c, s_a, v_own, v_c, v_a, mean, n_own, n_c, n_a, *got],
            weights,
        )
        if step == STEPS - 1:
            back_c = upper(f_c, "circ", True)
            back_a = upper(f_a, "axial", False)
            u_out, vel_out = run_finish(edge, u, s_start, s_own, v_own, f_own, back_c, back_a)
        else:
            got = exchange(f_c, f_a, send_c, send_a)
            s_own, s_c, s_a, v_own, v_c, v_a, n_own, n_c, n_a, send_c, send_a = run_again(
                pairs, counts, edge,
                [s_own, s_c, s_a, v_own, v_c, v_a, mean, f_own, f_c, f_a, *got],
                weights,
            )
    wide = lambda t: t.reshape(t.shape[0], 1, 1, OWN)
    return wide(u_out), wide(vel_out), theta.reshape(1, 1, OWN)


def solution(mesh):
    placed = (
        P(None, "circ", "axial", None),
        P(None, "circ", "axial", None),
        P(None, "circ", "axial", None),
        P("circ", "axial", None),
        P("circ", "axial", None),
        P("circ", "axial", None),
        P("circ", "axial", None, None),
        P("circ", "axial", None, None),
        P("circ", "axial", None),
        P("circ", "axial", None, None, None),
    )
    return jax.shard_map(
        body,
        mesh=mesh,
        in_specs=placed,
        out_specs=(
            P(None, "circ", "axial", None),
            P(None, "circ", "axial", None),
            P("circ", "axial", None),
        ),
        check_vma=False,
    )
```

time: 800 us -> 403 us (0.50)
  the two profiles are of different devices: /device:TPU:43 before, /device:TPU:2 now
where the time goes in v1:
time: 403 us; the launch traced here: 400 us
  Pallas kernels  254 us (63%)
  starting transfers between devices  109 us (27%)
  waiting for transfers between devices  24 us (6%)
  local copies, waits for them, and re-layouts  11.4 us (3%)
    pallas_call x4, Pallas kernels, sweep(): pl.pallas_call(kernel, out_shape=out_shape, grid_spec=pltpu.PrefetchScala...  248 us
    ppermute x8, starting transfers between devices, upper(): return lax.ppermute(block, axis, route)  75.1 us
    ppermute x8, starting transfers between devices, lower(): return lax.ppermute(block, axis, route)  34.2 us
    ppermute x8, waiting for transfers between devices, upper(): return lax.ppermute(block, axis, route)  17.2 us
    unnamed x32, local copies, waits for them, and re-layouts  9.97 us
  transfers between devices with their start and end apart: 16, of which 7 were waited for; matrix products, arithmetic and copies ran while one was open for 0% of the time, Pallas kernels for 0%

profile of v1, /device:TPU:2, one launch (start us, length us, event | category | flops | bytes accessed | tf_op | source)
XLA Modules:
  0.0 400.0 jit_solution(9921089384489837173)
XLA Ops:
  2.4 2.1 copy_bitcast_fusion
  4.5 3.6 pack.1
  8.0 6.7 %collective-permute-start = (f32[16,4096]{1,0:T(8,128)}, f32[16,4096]{1,0:T(8,128)S(1)}, u32[]{:S(2)}, u32[]{:S(2)}) collective-permute-start(f32[16,4096]{1,0:T(8,128)} %get-tuple-element.37), channel_id=1, source_target_pairs={{0,112},{16,0},{32,16},{48,32},{64,48},{80,64},{96,80},{112,96},{1... | collective-permute-start | bytes 786440 | tf_op jit(solution)/shard_map/ppermute | solution.py:551
  14.7 1.9 collective-permute-start.1
  16.6 6.8 %collective-permute-done = f32[16,4096]{1,0:T(8,128)S(1)} collective-permute-done((f32[16,4096]{1,0:T(8,128)}, f32[16,4096]{1,0:T(8,128)S(1)}, u32[]{:S(2)}, u32[]{:S(2)}) %collective-permute-start) | collective-permute-done | bytes 262176 | tf_op jit(solution)/shard_map/ppermute | solution.py:551
  24.8 58.1 %dil0.1 = (f32[320,128,128]{2,1,0:T(8,128)}, f32[1,16384]{1,0:T(1,128)}, f32[1,4096]{1,0:T(1,128)}, f32[1,4096]{1,0:T(1,128)}, f32[1,4096]{1,0:T(1,128)}, /*index=5*/f32[1,4096]{1,0:T(1,128)}) custom-call(s32[2,320]{1,0:T(2,128)} %bitcast.25, s32[2]{0:T(128)} %bitcast.35, s32[2,32]{1,0:T(2,128)} %bitcast.30, f32[8,16384]{1,0:T(8,128)} %get-tuple-element.36.s_own.s_start, ...), custom_call_target="tpu_custom_call" | custom-call | tf_op jit(solution)/shard_map/dil0/pallas_call | solution.py:474
  83.0 8.9 %collective-permute-start.2 = (f32[1,4096]{1,0:T(1,128)}, f32[1,4096]{1,0:T(1,128)S(1)}, u32[]{:S(2)}, u32[]{:S(2)}) collective-permute-start(f32[1,4096]{1,0:T(1,128)} %get-tuple-element.44), channel_id=1, source_target_pairs={{0,112},{16,0},{32,16},{48,32},{64,48},{80,64},{96,80},{112,96},{1... | collective-permute-start | bytes 49160 | tf_op jit(solution)/shard_map/ppermute | solution.py:551
  93.8 10.1 %collective-permute-start.4 = (f32[1,4096]{1,0:T(1,128)}, f32[1,4096]{1,0:T(1,128)S(1)}, u32[]{:S(2)}, u32[]{:S(2)}) collective-permute-start(f32[1,4096]{1,0:T(1,128)} %get-tuple-element.42.n_c), channel_id=1, source_target_pairs={{0,16},{16,32},{32,48},{48,64},{64,80},{80,96},{96,112},{112,0},{1... | collective-permute-start | bytes 49160 | tf_op jit(solution)/shard_map/ppermute | solution.py:557
  103.9 2.1 collective-permute-start.5
  106.1 4.0 collective-permute-done.5.back_a
  110.7 65.0 %force.2 = (f32[1,16384]{1,0:T(1,128)}, f32[4,16384]{1,0:T(4,128)}, f32[4,4096]{1,0:T(4,128)}, f32[4,4096]{1,0:T(4,128)}, f32[4,4096]{1,0:T(4,128)}, /*index=5*/f32[4,4096]{1,0:T(4,128)}) custom-call(s32[2,320]{1,0:T(2,128)} %bitcast.26, s32[2]{0:T(128)} %bitcast.36, s32[2,32]{1,0:T(2,128)} %bitcast.31, f32[8,16384]{1,0:T(8,128)} %get-tuple-element.36.s_own.s_start, ...), custom_call_target="tpu_custom_call" | custom-call | tf_op jit(solution)/shard_map/force/pallas_call | solution.py:474
  175.8 7.4 %collective-permute-start.7 = (f32[4,4096]{1,0:T(4,128)}, f32[4,4096]{1,0:T(4,128)S(1)}, u32[]{:S(2)}, u32[]{:S(2)}) collective-permute-start(f32[4,4096]{1,0:T(4,128)} %get-tuple-element.51), channel_id=1, source_target_pairs={{1,0},{2,1},{3,2},{4,3},{5,4},{6,5},{7,6},{8,7},{9,8},{10,9},{11,1... | collective-permute-start | bytes 196616 | tf_op jit(solution)/shard_map/ppermute | solution.py:551
  183.3 17.3 %collective-permute-start.8 = (f32[4,4096]{1,0:T(4,128)}, f32[4,4096]{1,0:T(4,128)S(1)}, u32[]{:S(2)}, u32[]{:S(2)}) collective-permute-start(f32[4,4096]{1,0:T(4,128)} %get-tuple-element.48.f_c), channel_id=1, source_target_pairs={{0,16},{16,32},{32,48},{48,64},{64,80},{80,96},{96,112},{112,0},{1... | collective-permute-start | bytes 196616 | tf_op jit(solution)/shard_map/ppermute | solution.py:557
  200.5 2.1 collective-permute-start.9
  202.8 4.3 %collective-permute-done.9.back_a = f32[4,4096]{1,0:T(4,128)S(1)} collective-permute-done((f32[4,4096]{1,0:T(4,128)}, f32[4,4096]{1,0:T(4,128)S(1)}, u32[]{:S(2)}, u32[]{:S(2)}) %collective-permute-start.9) | collective-permute-done | bytes 65568 | tf_op jit(solution)/shard_map/ppermute | solution.py:557
  207.8 59.7 %dil1.1 = (f32[8,16384]{1,0:T(8,128)}, f32[8,4096]{1,0:T(8,128)}, f32[8,4096]{1,0:T(8,128)}, f32[8,16384]{1,0:T(8,128)}, f32[8,4096]{1,0:T(8,128)}, /*index=5*/f...) custom-call(s32[2,320]{1,0:T(2,128)} %bitcast.27, ...), custom_call_target="tpu_custom_call" | custom-call | tf_op jit(solution)/shard_map/dil1/pallas_call | solution.py:474
  267.6 7.2 %collective-permute-start.11 = (f32[1,4096]{1,0:T(1,128)}, f32[1,4096]{1,0:T(1,128)S(1)}, u32[]{:S(2)}, u32[]{:S(2)}) collective-permute-start(f32[1,4096]{1,0:T(1,128)} %get-tuple-element.62), channel_id=1, source_target_pairs={{1,0},{2,1},{3,2},{4,3},{5,4},{6,5},{7,6},{8,7},{9,8},{10,9},{11,1... | collective-permute-start | bytes 49160 | tf_op jit(solution)/shard_map/ppermute | solution.py:551
  274.9 16.7 %collective-permute-start.12 = (f32[1,4096]{1,0:T(1,128)}, f32[1,4096]{1,0:T(1,128)S(1)}, u32[]{:S(2)}, u32[]{:S(2)}) collective-permute-start(f32[1,4096]{1,0:T(1,128)} %get-tuple-element.59.n_c), channel_id=1, source_target_pairs={{0,16},{16,32},{32,48},{48,64},{64,80},{80,96},{96,112},{112,0},{1... | collective-permute-start | bytes 49160 | tf_op jit(solution)/shard_map/ppermute | solution.py:557
  291.6 2.1 collective-permute-start.13
  293.8 4.0 collective-permute-done.13.back_a
  298.3 65.0 %force.3 = (f32[1,16384]{1,0:T(1,128)}, f32[4,16384]{1,0:T(4,128)}, f32[4,4096]{1,0:T(4,128)}, f32[4,4096]{1,0:T(4,128)}, f32[4,4096]{1,0:T(4,128)}, /*index=5*/f32[4,4096]{1,0:T(4,128)}) custom-call(s32[2,320]{1,0:T(2,128)} %bitcast.28, s32[2]{0:T(128)} %bitcast.38, s32[2,32]{1,0:T(2,128)} %bitcast.33, f32[8,16384]{1,0:T(8,128)} %get-tuple-element.52.s_own, ...), custom_call_target="tpu_custom_call" | custom-call | tf_op jit(solution)/shard_map/force/pallas_call | solution.py:474
  363.3 22.8 %collective-permute-start.14 = (f32[4,4096]{1,0:T(4,128)}, f32[4,4096]{1,0:T(4,128)S(1)}, u32[]{:S(2)}, u32[]{:S(2)}) collective-permute-start(f32[4,4096]{1,0:T(4,128)} %get-tuple-element.64), channel_id=1, source_target_pairs={{0,16},{16,32},{32,48},{48,64},{64,80},{80,96},{96,112},{112,0},{1... | collective-permute-start | bytes 196616 | tf_op jit(solution)/shard_map/ppermute | solution.py:557
  388.3 4.5 %collective-permute-done.15.back_a = f32[4,4096]{1,0:T(4,128)S(1)} collective-permute-done((f32[4,4096]{1,0:T(4,128)}, f32[4,4096]{1,0:T(4,128)S(1)}, u32[]{:S(2)}, u32[]{:S(2)}) %collective-permute-start.15) | collective-permute-done | bytes 65568 | tf_op jit(solution)/shard_map/ppermute | solution.py:557
  393.4 2.9 finish.1
  (48 shorter events, 13.8 us)
Async XLA Ops:
  8.0 15.4 %collective-permute-start = (f32[16,4096]{1,0:T(8,128)}, f32[16,4096]{1,0:T(8,128)S(1)}, u32[]{:S(2)}, u32[]{:S(2)}) collective-permute-start(f32[16,4096]{1,0:T(8,128)} %get-tuple-element.37), channel_id=1, source_target_pairs={{0,112},{16,0},{32,16},{48,32},{64,48},{80,64},{96,80},{112,96},{1... | collective-permute-start | bytes 786440 | tf_op jit(solution)/shard_map/ppermute | solution.py:551
  14.7 9.4 %collective-permute-start.1 = (f32[16,4096]{1,0:T(8,128)}, f32[16,4096]{1,0:T(8,128)S(1)}, u32[]{:S(2)}, u32[]{:S(2)}) collective-permute-start(f32[16,4096]{1,0:T(8,128)} %get-tuple-element.38), channel_id=1, source_target_pairs={{1,0},{2,1},{3,2},{4,3},{5,4},{6,5},{7,6},{8,7},{9,8},{10,9},{11,1... | collective-permute-start | bytes 786440 | tf_op jit(solution)/shard_map/ppermute | solution.py:551
  83.0 23.1 %collective-permute-start.2 = (f32[1,4096]{1,0:T(1,128)}, f32[1,4096]{1,0:T(1,128)S(1)}, u32[]{:S(2)}, u32[]{:S(2)}) collective-permute-start(f32[1,4096]{1,0:T(1,128)} %get-tuple-element.44), channel_id=1, source_target_pairs={{0,112},{16,0},{32,16},{48,32},{64,48},{80,64},{96,80},{112,96},{1... | collective-permute-start | bytes 49160 | tf_op jit(solution)/shard_map/ppermute | solution.py:551
  91.9 14.2 %collective-permute-start.3 = (f32[1,4096]{1,0:T(1,128)}, f32[1,4096]{1,0:T(1,128)S(1)}, u32[]{:S(2)}, u32[]{:S(2)}) collective-permute-start(f32[1,4096]{1,0:T(1,128)} %get-tuple-element.45), channel_id=1, source_target_pairs={{1,0},{2,1},{3,2},{4,3},{5,4},{6,5},{7,6},{8,7},{9,8},{10,9},{11,1... | collective-permute-start | bytes 49160 | tf_op jit(solution)/shard_map/ppermute | solution.py:551
  93.8 12.3 %collective-permute-start.4 = (f32[1,4096]{1,0:T(1,128)}, f32[1,4096]{1,0:T(1,128)S(1)}, u32[]{:S(2)}, u32[]{:S(2)}) collective-permute-start(f32[1,4096]{1,0:T(1,128)} %get-tuple-element.42.n_c), channel_id=1, source_target_pairs={{0,16},{16,32},{32,48},{48,64},{64,80},{80,96},{96,112},{112,0},{1... | collective-permute-start | bytes 49160 | tf_op jit(solution)/shard_map/ppermute | solution.py:557
  103.9 6.2 %collective-permute-start.5 = (f32[1,4096]{1,0:T(1,128)}, f32[1,4096]{1,0:T(1,128)S(1)}, u32[]{:S(2)}, u32[]{:S(2)}) collective-permute-start(f32[1,4096]{1,0:T(1,128)} %get-tuple-element.43.n_a), channel_id=1, source_target_pairs={{0,1},{1,2},{2,3},{3,4},{4,5},{5,6},{6,7},{7,8},{8,9},{9,10},{10,1... | collective-permute-start | bytes 49160 | tf_op jit(solution)/shard_map/ppermute | solution.py:557
  106.1 4.0 %copy-start.7 = (f32[1,4096]{1,0:T(1,128)}, f32[1,4096]{1,0:T(1,128)S(1)}, u32[]{:S(2)}) copy-start(f32[1,4096]{1,0:T(1,128)S(1)} %collective-permute-done.2.up_c) | copy-start | bytes 49156
  106.1 4.0 %copy-start.9 = (f32[1,4096]{1,0:T(1,128)}, f32[1,4096]{1,0:T(1,128)S(1)}, u32[]{:S(2)}) copy-start(f32[1,4096]{1,0:T(1,128)S(1)} %collective-permute-done.3.up_a) | copy-start | bytes 49156
  175.7 26.9 %collective-permute-start.6 = (f32[4,4096]{1,0:T(4,128)}, f32[4,4096]{1,0:T(4,128)S(1)}, u32[]{:S(2)}, u32[]{:S(2)}) collective-permute-start(f32[4,4096]{1,0:T(4,128)} %get-tuple-element.50), channel_id=1, source_target_pairs={{0,112},{16,0},{32,16},{48,32},{64,48},{80,64},{96,80},{112,96},{1... | collective-permute-start | bytes 196616 | tf_op jit(solution)/shard_map/ppermute | solution.py:551
  175.8 26.8 %collective-permute-start.7 = (f32[4,4096]{1,0:T(4,128)}, f32[4,4096]{1,0:T(4,128)S(1)}, u32[]{:S(2)}, u32[]{:S(2)}) collective-permute-start(f32[4,4096]{1,0:T(4,128)} %get-tuple-element.51), channel_id=1, source_target_pairs={{1,0},{2,1},{3,2},{4,3},{5,4},{6,5},{7,6},{8,7},{9,8},{10,9},{11,1... | collective-permute-start | bytes 196616 | tf_op jit(solution)/shard_map/ppermute | solution.py:551
  183.3 19.6 %collective-permute-start.8 = (f32[4,4096]{1,0:T(4,128)}, f32[4,4096]{1,0:T(4,128)S(1)}, u32[]{:S(2)}, u32[]{:S(2)}) collective-permute-start(f32[4,4096]{1,0:T(4,128)} %get-tuple-element.48.f_c), channel_id=1, source_target_pairs={{0,16},{16,32},{32,48},{48,64},{64,80},{80,96},{96,112},{112,0},{1... | collective-permute-start | bytes 196616 | tf_op jit(solution)/shard_map/ppermute | solution.py:557
  200.5 6.7 %collective-permute-start.9 = (f32[4,4096]{1,0:T(4,128)}, f32[4,4096]{1,0:T(4,128)S(1)}, u32[]{:S(2)}, u32[]{:S(2)}) collective-permute-start(f32[4,4096]{1,0:T(4,128)} %get-tuple-element.49.f_a), channel_id=1, source_target_pairs={{0,1},{1,2},{2,3},{3,4},{4,5},{5,6},{6,7},{7,8},{8,9},{9,10},{10,1... | collective-permute-start | bytes 196616 | tf_op jit(solution)/shard_map/ppermute | solution.py:557
  202.6 4.6 %copy-start = (f32[4,4096]{1,0:T(4,128)}, f32[4,4096]{1,0:T(4,128)S(1)}, u32[]{:S(2)}) copy-start(f32[4,4096]{1,0:T(4,128)S(1)} %collective-permute-done.6.up_c) | copy-start | bytes 196612
  202.7 4.5 %copy-start.1 = (f32[4,4096]{1,0:T(4,128)}, f32[4,4096]{1,0:T(4,128)S(1)}, u32[]{:S(2)}) copy-start(f32[4,4096]{1,0:T(4,128)S(1)} %collective-permute-done.7.up_a) | copy-start | bytes 196612
  202.8 4.4 %copy-start.2 = (f32[4,4096]{1,0:T(4,128)}, f32[4,4096]{1,0:T(4,128)S(1)}, u32[]{:S(2)}) copy-start(f32[4,4096]{1,0:T(4,128)S(1)} %collective-permute-done.8.back_c) | copy-start | bytes 196612
  267.5 26.2 %collective-permute-start.10 = (f32[1,4096]{1,0:T(1,128)}, f32[1,4096]{1,0:T(1,128)S(1)}, u32[]{:S(2)}, u32[]{:S(2)}) collective-permute-start(f32[1,4096]{1,0:T(1,128)} %get-tuple-element.61), channel_id=1, source_target_pairs={{0,112},{16,0},{32,16},{48,32},{64,48},{80,64},{96,80},{112,96},{1... | collective-permute-start | bytes 49160 | tf_op jit(solution)/shard_map/ppermute | solution.py:551
  267.6 26.1 %collective-permute-start.11 = (f32[1,4096]{1,0:T(1,128)}, f32[1,4096]{1,0:T(1,128)S(1)}, u32[]{:S(2)}, u32[]{:S(2)}) collective-permute-start(f32[1,4096]{1,0:T(1,128)} %get-tuple-element.62), channel_id=1, source_target_pairs={{1,0},{2,1},{3,2},{4,3},{5,4},{6,5},{7,6},{8,7},{9,8},{10,9},{11,1... | collective-permute-start | bytes 49160 | tf_op jit(solution)/shard_map/ppermute | solution.py:551
  274.9 18.9 %collective-permute-start.12 = (f32[1,4096]{1,0:T(1,128)}, f32[1,4096]{1,0:T(1,128)S(1)}, u32[]{:S(2)}, u32[]{:S(2)}) collective-permute-start(f32[1,4096]{1,0:T(1,128)} %get-tuple-element.59.n_c), channel_id=1, source_target_pairs={{0,16},{16,32},{32,48},{48,64},{64,80},{80,96},{96,112},{112,0},{1... | collective-permute-start | bytes 49160 | tf_op jit(solution)/shard_map/ppermute | solution.py:557
  291.6 6.2 %collective-permute-start.13 = (f32[1,4096]{1,0:T(1,128)}, f32[1,4096]{1,0:T(1,128)S(1)}, u32[]{:S(2)}, u32[]{:S(2)}) collective-permute-start(f32[1,4096]{1,0:T(1,128)} %get-tuple-element.60.n_a), channel_id=1, source_target_pairs={{0,1},{1,2},{2,3},{3,4},{4,5},{5,6},{6,7},{7,8},{8,9},{9,10},{10,1... | collective-permute-start | bytes 49160 | tf_op jit(solution)/shard_map/ppermute | solution.py:557
  293.7 4.0 %copy-start.6 = (f32[1,4096]{1,0:T(1,128)}, f32[1,4096]{1,0:T(1,128)S(1)}, u32[]{:S(2)}) copy-start(f32[1,4096]{1,0:T(1,128)S(1)} %collective-permute-done.10.up_c) | copy-start | bytes 49156
  293.7 4.0 %copy-start.8 = (f32[1,4096]{1,0:T(1,128)}, f32[1,4096]{1,0:T(1,128)S(1)}, u32[]{:S(2)}) copy-start(f32[1,4096]{1,0:T(1,128)S(1)} %collective-permute-done.11.up_a) | copy-start | bytes 49156
  363.3 25.0 %collective-permute-start.14 = (f32[4,4096]{1,0:T(4,128)}, f32[4,4096]{1,0:T(4,128)S(1)}, u32[]{:S(2)}, u32[]{:S(2)}) collective-permute-start(f32[4,4096]{1,0:T(4,128)} %get-tuple-element.64), channel_id=1, source_target_pairs={{0,16},{16,32},{32,48},{48,64},{64,80},{80,96},{96,112},{112,0},{1... | collective-permute-start | bytes 196616 | tf_op jit(solution)/shard_map/ppermute | solution.py:557
  386.1 6.7 %collective-permute-start.15 = (f32[4,4096]{1,0:T(4,128)}, f32[4,4096]{1,0:T(4,128)S(1)}, u32[]{:S(2)}, u32[]{:S(2)}) collective-permute-start(f32[4,4096]{1,0:T(4,128)} %get-tuple-element.65), channel_id=1, source_target_pairs={{0,1},{1,2},{2,3},{3,4},{4,5},{5,6},{6,7},{7,8},{8,9},{9,10},{10,1... | collective-permute-start | bytes 196616 | tf_op jit(solution)/shard_map/ppermute | solution.py:557
  388.3 4.5 %copy-start.4 = (f32[4,4096]{1,0:T(4,128)}, f32[4,4096]{1,0:T(4,128)S(1)}, u32[]{:S(2)}) copy-start(f32[4,4096]{1,0:T(4,128)S(1)} %collective-permute-done.14.back_c) | copy-start | bytes 196612
  (6 other events, 10.4 us)

commit v2 on v1

v2 whole, which is shorter than its diff:
```python
import functools

import jax
import jax.numpy as jnp
from jax import lax
from jax.experimental import pallas as pl
from jax.experimental.pallas import tpu as pltpu
from jax.sharding import PartitionSpec as P

PTS = 128
CL = 128
FACING = 32
EXT = CL + 2 * FACING
SLOTS = 320
STEPS = 2
TIMESTEP = 0.07
SOFTEN = 0.01
LOG2E = 1.4426950408889634
KAPPA = LOG2E**0.5
TINY = 1e-30
GROUP = 32
UNROLL = 16
OWN = CL * PTS
GHOST = FACING * PTS
F32 = jnp.float32
BF16 = jnp.bfloat16
NT = (((1,), (1,)), ((), ()))
NN = (((1,), (0,)), ((), ()))


def dot(a, b, dims):
    return lax.dot_general(a, b, dims, preferred_element_type=F32)


def split3(x):
    h = x.astype(BF16).astype(F32)
    rest = x - h
    m = rest.astype(BF16).astype(F32)
    return h, m, rest - m


def hilo(x):
    h = x.astype(BF16)
    return h, (x - h.astype(F32)).astype(BF16)


def rows8():
    return lax.broadcasted_iota(jnp.int32, (8, PTS), 0)


def coordinate_parts(s):
    row = rows8()
    sq = s * s
    nx = sq[0:1] + sq[1:2] + sq[2:3]
    ny = sq[4:5] + sq[5:6] + sq[6:7]
    full = jnp.where(row == 3, nx, jnp.where(row == 7, ny, s))
    return split3(full)


def source_features(parts):
    p0, p1, p2 = parts
    one = jnp.ones((8, PTS), F32)
    stack = jnp.concatenate([p0, p0, p0, p1, p1, p2, one, one], axis=0)
    return jnp.transpose(stack).astype(BF16)


def target_features(parts):
    p0, p1, p2 = parts
    row = rows8()
    norm = (row == 3) | (row == 7)
    a0 = jnp.where(norm, -1.0, 2.0 * p0)
    a1 = jnp.where(norm, 0.0, 2.0 * p1)
    a2 = jnp.where(norm, 0.0, 2.0 * p2)
    n0 = jnp.where(norm, -p0, 0.0)
    shifted = pltpu.roll(p2, 1, 0)
    n1 = jnp.where(norm, -p1, 0.0)
    upper = row < 4
    after = (row == 4) | (row == 0)
    stack = jnp.concatenate([a0, a1, a2, a0, a1, a0], axis=0)
    up6 = jnp.concatenate([upper] * 6, axis=0)

    def half(top):
        keep = up6 if top else ~up6
        body = jnp.where(keep, stack, 0.0)
        near = upper if top else ~upper
        tail0 = jnp.where(near, n0, 0.0)
        tail1 = jnp.where(near, n1, 0.0) - jnp.where(row == (4 if top else 0), shifted, 0.0)
        return jnp.concatenate([body, tail0, tail1], axis=0).astype(BF16)

    return half(True), half(False)


def moment_features(parts):
    p0, p1, p2 = parts
    row = rows8()
    first = jnp.where(row == 3, 1.0, jnp.where(row > 3, p0, 0.0))
    first = jnp.where(row == 7, 0.0, first)
    second = jnp.where((row > 3) & (row < 7), p1, 0.0) + jnp.where(
        row < 3, pltpu.roll(p2, 4, 0), 0.0
    )
    m = jnp.concatenate([first, second], axis=0).astype(BF16)
    return jnp.concatenate([m, m], axis=1)


def coef_features(minus, neg_dev):
    row = rows8()
    pair = jnp.where(row == 0, minus, jnp.where(row == 1, neg_dev, 0.0))
    h, m, l = split3(pair)
    q = h + pltpu.roll(m, 2, 0) + pltpu.roll(l, 4, 0)
    even = (row == 0) | (row == 2) | (row == 4)
    odd = (row == 1) | (row == 3) | (row == 5)
    src = jnp.transpose(jnp.concatenate([q, jnp.ones((8, PTS), F32)], axis=0)).astype(BF16)
    t0 = jnp.concatenate([jnp.where(even, 1.0, 0.0), jnp.where(even, q, 0.0)], axis=0)
    t1 = jnp.concatenate([jnp.where(odd, 1.0, 0.0), jnp.where(odd, q, 0.0)], axis=0)
    return src, t0.astype(BF16), t1.astype(BF16)


def one_row(c):
    return pl.ds(c, 1)


def loop(n, fn, unroll):
    lax.fori_loop(0, n, lambda c, _: (fn(c), 0)[1], 0, unroll=unroll)


def pack_kernel(edges, x_ref, u_ref, v_ref, bulk, shear, volume, s_out, v_out, mean,
                sc_out, sa_out, vc_out, va_out):
    zero = jnp.zeros((1, PTS), F32)

    def cluster(c):
        r = one_row(c)
        x = [KAPPA * x_ref[k, r, :] for k in range(3)]
        y = [x[k] + KAPPA * u_ref[k, r, :] for k in range(3)]
        s_out[c] = jnp.concatenate([*x, zero, *y, zero], axis=0)
        inv = 1.0 / volume[r, :]
        mu = shear[r, :]
        dil = (3.0 * bulk[r, :] - 5.0 * mu) * inv
        dev = 15.0 * mu * inv
        thr = (3.0 / LOG2E) * inv
        v = [KAPPA * v_ref[k, r, :] for k in range(3)]
        v_out[c] = jnp.concatenate([dil, dev, thr, zero, *v, zero], axis=0)

    loop(CL, cluster, 4)
    total = jnp.sum(jnp.sum(s_out[...], axis=0), axis=1, keepdims=True)
    mean[...] = jnp.broadcast_to(total * (1.0 / OWN), (8, PTS))

    def copy(f):
        for side, s, v in ((0, sc_out, vc_out), (1, sa_out, va_out)):
            e = edges[side, f]
            s[f] = s_out[e]
            v[f] = v_out[e]

    loop(FACING, copy, 4)


def build_geometry(c, s, left, right, moments):
    parts = coordinate_parts(s)
    if left is not None:
        left[c] = source_features(parts)
    t0, t1 = target_features(parts)
    right[c, :, 0:PTS] = t0
    right[c, :, PTS:] = t1
    if moments is not None:
        moments[c] = moment_features(parts)


def build_all(s_own, s_c, s_a, mean, left, right, moments):
    shift = mean[...]
    loop(CL, lambda c: build_geometry(c, s_own[c] - shift, left, right, moments), 4)

    def ghost(f):
        build_geometry(CL + f, s_c[f] - shift, None, right, moments)
        build_geometry(CL + FACING + f, s_a[f] - shift, None, right, moments)

    loop(FACING, ghost, 2)


def turns_here(counts):
    g = pl.program_id(0)
    left_over = (counts[1] - g * GROUP + UNROLL - 1) // UNROLL
    return g, jnp.clip(left_over, 0, GROUP // UNROLL)


def first_sweep(pairs, counts, weight_of, left, right, acc, racc):
    g, turns = turns_here(counts)

    def turn(i, _):
        for j in range(UNROLL):
            k = i * UNROLL + j
            slot = g * GROUP + k
            p = pairs[0, slot]
            q = pairs[1, slot]
            live = slot < counts[1]
            ab = dot(left[p], right[q], NN)
            na = ab[:, :PTS]
            nb = ab[:, PTS:]
            w = weight_of(na, k, slot)
            x = jnp.maximum(na * nb, TINY)
            t = (x * lax.rsqrt(x) + na) * w
            acc[jnp.where(live, q, EXT)] += jnp.sum(t.reshape(16, 8, PTS), axis=0)
            racc[jnp.where(live, p, CL)] += t
        return 0

    lax.fori_loop(0, turns, turn, 0)


def first_finish(edges, acc, racc, n_own, n_c, n_a, send_c, send_a):
    ones = jnp.ones((16, 2 * PTS), BF16)

    def own(c):
        h, l = hilo(racc[c])
        across = dot(ones, jnp.concatenate([h, l], axis=1), NT)
        n_own[one_row(c), :] = across[0:1] + jnp.sum(acc[c], axis=0, keepdims=True)

    loop(CL, own, 4)

    def ghost(f):
        r = one_row(f)
        n_c[r, :] = jnp.sum(acc[CL + f], axis=0, keepdims=True)
        n_a[r, :] = jnp.sum(acc[CL + FACING + f], axis=0, keepdims=True)
        send_c[r, :] = n_own[one_row(edges[0, f]), :]
        send_a[r, :] = n_own[one_row(edges[1, f]), :]

    loop(FACING, ghost, 4)


def clear(ref):
    loop(ref.shape[0], lambda c: ref.__setitem__(c, jnp.zeros(ref.shape[1:], ref.dtype)), 1)


def dilatation_first(
    pairs, counts, edges, s_own, s_c, s_a, mean, damage,
    w_out, n_own, n_c, n_a, send_c, send_a,
    left, right, acc, racc, cut,
):
    g = pl.program_id(0)

    @pl.when(g == 0)
    def _():
        clear(acc)
        clear(racc)
        i0 = lax.broadcasted_iota(jnp.int32, (PTS, PTS), 0)
        i1 = lax.broadcasted_iota(jnp.int32, (PTS, PTS), 1)
        cut[0] = jnp.where(i0 < i1, 0, 1)
        cut[1] = jnp.zeros((PTS, PTS), jnp.int32)
        build_all(s_own, s_c, s_a, mean, left, right, None)

    def weight_of(na, k, slot):
        keep = damage[k] > cut[jnp.where(slot < CL, 0, 1)]
        w = jnp.where(keep, jnp.exp2(na), 0.0)
        w_out[k] = w
        return w

    first_sweep(pairs, counts, weight_of, left, right, acc, racc)

    @pl.when(g == pl.num_programs(0) - 1)
    def _():
        first_finish(edges, acc, racc, n_own, n_c, n_a, send_c, send_a)


def dilatation_again(
    pairs, counts, edges, s_own, s_c, s_a, v_own, v_c, v_a, mean, f_own, f_c, f_a,
    up_c, up_a, back_c, back_a, weights,
    s_own2, s_c2, s_a2, v_own2, v_c2, v_a2, n_own, n_c, n_a, send_c, send_a,
    left, right, acc, racc,
):
    g = pl.program_id(0)

    @pl.when(g == 0)
    def _():
        clear(acc)
        clear(racc)
        advance(edges, s_own, s_c, s_a, v_own, v_c, v_a, f_own, f_c, f_a, up_c, up_a, back_c,
                back_a, s_own2, s_c2, s_a2, v_own2, v_c2, v_a2)
        build_all(s_own2, s_c2, s_a2, mean, left, right, None)

    first_sweep(pairs, counts, lambda na, k, slot: weights[k], left, right, acc, racc)

    @pl.when(g == pl.num_programs(0) - 1)
    def _():
        first_finish(edges, acc, racc, n_own, n_c, n_a, send_c, send_a)


def advance(edges, s_own, s_c, s_a, v_own, v_c, v_a, f_own, f_c, f_a, up_c, up_a, back_c, back_a,
            s_own2, s_c2, s_a2, v_own2, v_c2, v_a2):
    pad = jnp.zeros((4, PTS), F32)

    def moved(s, v, f):
        v2 = v + TIMESTEP * jnp.concatenate([pad, f], axis=0)
        return s + jnp.where(rows8() < 4, 0.0, TIMESTEP * v2), v2

    def own(c):
        s_own2[c], v_own2[c] = moved(s_own[c], v_own[c], f_own[c])

    loop(CL, own, 8)

    def ghost(f):
        for side, back in ((0, back_c), (1, back_a)):
            e = edges[side, f]
            s_own2[e], v_own2[e] = moved(s_own[e], v_own[e], f_own[e] + back[f])
        s_c2[f], v_c2[f] = moved(s_c[f], v_c[f], up_c[f] + f_c[f])
        s_a2[f], v_a2[f] = moved(s_a[f], v_a[f], up_a[f] + f_a[f])

    loop(FACING, ghost, 4)


def force_pass(
    pairs, counts, edges, s_own, s_c, s_a, v_own, v_c, v_a, mean, n_own, n_c, n_a,
    up_c, up_a, back_c, back_a, weights,
    theta_out, f_own, f_c, f_a, send_c, send_a,
    left, right, left2, right2, moments, acc, n_full, geo, halves,
):
    def geometry(slot, j):
        s = jnp.minimum(slot, SLOTS - 1)
        p = pairs[0, s]
        q = pairs[1, s]
        geo[j, :, 0 : 2 * PTS] = dot(left[p], right[q], NN)
        geo[j, :, 2 * PTS :] = dot(left2[p], right2[q], NN)

    def chain(k, j):
        na = jnp.minimum(geo[j, :, 0:PTS], -TINY)
        nb = jnp.minimum(geo[j, :, PTS : 2 * PTS], -TINY)
        nu = nb - SOFTEN * LOG2E
        za = na * lax.rsqrt(na * nu)
        zb = nb * lax.rsqrt(nb * nu)
        m = weights[k] * (geo[j, :, 2 * PTS : 3 * PTS] * za + geo[j, :, 3 * PTS :] * zb)
        h, l = hilo(m)
        halves[j, 0:PTS, :] = h
        halves[j, PTS:, :] = l

    def gather(slot, j):
        s = jnp.maximum(slot, 0)
        p = pairs[0, s]
        q = pairs[1, s]
        live = (slot >= 0) & (slot < counts[1])
        hl = halves[j]
        gq = dot(moments[p], hl, NN)
        gp = dot(moments[q], jnp.concatenate([hl[:PTS], hl[PTS:]], axis=1), NT)
        return jnp.where(live, p, EXT), jnp.where(live, q, EXT), gp, gq

    def flush(found):
        for pa, qa, gp, gq in found:
            acc[qa] += gq
            acc[pa] += gp

    g, turns = turns_here(counts)

    @pl.when(g == 0)
    def _():
        clear(acc)
        build_all(s_own, s_c, s_a, mean, left, right, moments)
        n_full[0:CL, :] = n_own[...]

        def mend(f):
            r = one_row(f)
            for side, back in ((0, back_c), (1, back_a)):
                e = one_row(edges[side, f])
                n_full[e, :] = n_own[e, :] + back[r, :]
            n_full[one_row(CL + f), :] = up_c[r, :] + n_c[r, :]
            n_full[one_row(CL + FACING + f), :] = up_a[r, :] + n_a[r, :]

        loop(FACING, mend, 4)

        def coefs(c, v):
            theta = v[2:3] * n_full[one_row(c), :]
            src, t0, t1 = coef_features(v[1:2] - v[0:1] * theta, -v[1:2])
            right2[c, :, 0:PTS] = t0
            right2[c, :, PTS:] = t1
            return theta, src

        def own(c):
            theta, src = coefs(c, v_own[c])
            theta_out[one_row(c), :] = theta
            left2[c] = src

        loop(CL, own, 4)

        def ghost(f):
            coefs(CL + f, v_c[f])
            coefs(CL + FACING + f, v_a[f])

        loop(FACING, ghost, 4)
        for j in range(UNROLL):
            geometry(j, j)

    def turn(i, _):
        base = g * GROUP + i * UNROLL
        found = []
        for j in range(UNROLL + 1):
            if j < UNROLL:
                found.append(gather(base - UNROLL + j, j))
            if j > 0:
                chain(i * UNROLL + j - 1, j - 1)
                geometry(base + UNROLL + j - 1, j - 1)
        flush(found)
        return 0

    lax.fori_loop(0, turns, turn, 0)

    @pl.when(g == pl.num_programs(0) - 1)
    def _():
        last = (counts[1] + UNROLL - 1) // UNROLL * UNROLL - UNROLL
        flush([gather(last + j, j) for j in range(UNROLL)])
        shift = mean[...]

        def force(c, s):
            gsum = acc[c]
            first, second = gsum[0:8], gsum[8:16]
            total = first + second + pltpu.roll(second, 4, 0)
            return (total - (s - shift) * first[3:4])[4:8]

        def own(c):
            f_own[c] = force(c, s_own[c])

        loop(CL, own, 4)

        def ghost(f):
            f_c[f] = force(CL + f, s_c[f])
            f_a[f] = force(CL + FACING + f, s_a[f])
            send_c[f] = f_own[edges[0, f]]
            send_a[f] = f_own[edges[1, f]]

        loop(FACING, ghost, 4)


def finish_kernel(edges, u_ref, s_start, s_own, v_own, f_own, back_c, back_a, u_out, vel_out, f_sum):
    f_sum[...] = f_own[...]

    def mend(f):
        for side, back in ((0, back_c), (1, back_a)):
            e = edges[side, f]
            f_sum[e] = f_sum[e] + back[f]

    loop(FACING, mend, 4)

    def cluster(c):
        r = one_row(c)
        v2 = v_own[c][4:8] + TIMESTEP * f_sum[c]
        vel = v2 * (1.0 / KAPPA)
        gone = ((s_own[c] - s_start[c])[4:8] + TIMESTEP * v2) * (1.0 / KAPPA)
        for k in range(3):
            vel_out[k, r, :] = vel[k : k + 1]
            u_out[k, r, :] = u_ref[k, r, :] + gone[k : k + 1]

    loop(CL, cluster, 4)


SMEM = pl.BlockSpec(memory_space=pltpu.SMEM)
VMEM = pl.BlockSpec(memory_space=pltpu.VMEM)


def table(*shape):
    return jax.ShapeDtypeStruct(shape, F32)


def slab_spec():
    def index(g, pairs, counts):
        return (jnp.minimum(g, (counts[1] - 1) // GROUP), 0, 0)

    return pl.BlockSpec((GROUP, PTS, PTS), index)


def sweep(kernel, name, pairs, counts, edges, tables, slab, out_tables, scratch, slab_out=None):
    def whole(x, **kw):
        return pl.BlockSpec(x.shape, lambda g, a, b: (0,) * x.ndim, **kw)

    outs = [whole(x) for x in out_tables]
    out_shape = list(out_tables)
    if slab_out is not None:
        outs = [slab_spec()] + outs
        out_shape = [slab_out] + out_shape
    return pl.pallas_call(
        kernel,
        out_shape=out_shape,
        grid_spec=pltpu.PrefetchScalarGridSpec(
            num_scalar_prefetch=2,
            grid=(SLOTS // GROUP,),
            in_specs=[SMEM] + [whole(x, pipeline_mode=pl.Buffered(1)) for x in tables] + [slab_spec()],
            out_specs=outs,
            scratch_shapes=scratch,
        ),
        compiler_params=pltpu.CompilerParams(
            dimension_semantics=("arbitrary",), vmem_limit_bytes=56 << 20
        ),
        name=name,
    )(pairs, counts, edges, *tables, slab)


LEFT = pltpu.VMEM((CL, PTS, 64), BF16)
RIGHT = pltpu.VMEM((EXT, 64, 2 * PTS), BF16)
N_TABLES = [table(CL, PTS)] + [table(FACING, PTS)] * 4
F_TABLES = [table(CL, 4, PTS)] + [table(FACING, 4, PTS)] * 4
STATES = [table(CL, 8, PTS), table(FACING, 8, PTS), table(FACING, 8, PTS)]
SUMS = [pltpu.VMEM((EXT + 1, 8, PTS), F32), pltpu.VMEM((CL + 1, PTS, PTS), F32)]


def run_first(pairs, counts, edges, s_own, s_c, s_a, mean, damage):
    return sweep(
        dilatation_first, "dil0", pairs, counts, edges, [s_own, s_c, s_a, mean], damage, N_TABLES,
        [LEFT, RIGHT, *SUMS, pltpu.VMEM((2, PTS, PTS), jnp.int32)],
        slab_out=table(SLOTS, PTS, PTS),
    )


def run_again(pairs, counts, edges, tables, weights):
    return sweep(
        dilatation_again, "dil1", pairs, counts, edges, tables, weights, STATES * 2 + N_TABLES,
        [LEFT, RIGHT, *SUMS],
    )


def run_force(pairs, counts, edges, tables, weights):
    return sweep(
        force_pass, "force", pairs, counts, edges, tables, weights, [table(CL, PTS)] + F_TABLES,
        [
            LEFT,
            RIGHT,
            pltpu.VMEM((CL, PTS, 16), BF16),
            pltpu.VMEM((EXT, 16, 2 * PTS), BF16),
            pltpu.VMEM((EXT, 16, 2 * PTS), BF16),
            pltpu.VMEM((EXT + 1, 16, PTS), F32),
            pltpu.VMEM((EXT, PTS), F32),
            pltpu.VMEM((UNROLL, PTS, 4 * PTS), F32),
            pltpu.VMEM((UNROLL, 2 * PTS, PTS), BF16),
        ],
    )


def run_pack(edges, *args):
    return pl.pallas_call(
        pack_kernel,
        out_shape=[table(CL, 8, PTS)] * 2 + [table(8, PTS)] + [table(FACING, 8, PTS)] * 4,
        in_specs=[SMEM] + [VMEM] * 6,
        out_specs=[VMEM] * 7,
        name="pack",
    )(edges, *args)


def run_finish(edges, *args):
    return pl.pallas_call(
        finish_kernel,
        out_shape=[table(3, CL, PTS), table(3, CL, PTS)],
        in_specs=[SMEM] + [VMEM] * 7,
        out_specs=[VMEM] * 2,
        scratch_shapes=[pltpu.VMEM((CL, 4, PTS), F32)],
        name="finish",
    )(edges, *args)


def shift_ring(block, axis, by):
    n = lax.axis_size(axis)
    return lax.ppermute(block, axis, [(i, (i + by) % n) for i in range(n)])


def exchange(part_c, part_a, own_c, own_a):
    return (
        shift_ring(own_c, "circ", -1),
        shift_ring(own_a, "axial", -1),
        shift_ring(part_c, "circ", 1),
        shift_ring(part_a, "axial", 1),
    )


def body(
    position, displacement, velocity, bulk, shear, volume, edges, block_pairs, block_counts, damage
):
    cube = lambda t: t.reshape(3, CL, PTS)
    flat = lambda t: t.reshape(CL, PTS)
    u = cube(displacement)
    edge = edges[0, 0]
    pairs = block_pairs[0, 0]
    counts = block_counts[0, 0]
    s_own, v_own, mean, s_c, s_a, v_c, v_a = run_pack(
        edge, cube(position), u, cube(velocity), flat(bulk), flat(shear), flat(volume)
    )
    s_start = s_own
    s_c = shift_ring(s_c, "circ", -1)
    s_a = shift_ring(s_a, "axial", -1)
    s_c, s_a, v_c, v_a = lax.optimization_barrier((s_c, s_a, v_c, v_a))
    v_c = shift_ring(v_c, "circ", -1)
    v_a = shift_ring(v_a, "axial", -1)
    weights, n_own, n_c, n_a, send_c, send_a = run_first(
        pairs, counts, edge, s_own, s_c, s_a, mean, damage[0, 0]
    )
    for step in range(STEPS):
        got = exchange(n_c, n_a, send_c, send_a)
        theta, f_own, f_c, f_a, send_c, send_a = run_force(
            pairs, counts, edge,
            [s_own, s_c, s_a, v_own, v_c, v_a, mean, n_own, n_c, n_a, *got],
            weights,
        )
        if step == STEPS - 1:
            back_c = shift_ring(f_c, "circ", 1)
            back_a = shift_ring(f_a, "axial", 1)
            u_out, vel_out = run_finish(edge, u, s_start, s_own, v_own, f_own, back_c, back_a)
        else:
            got = exchange(f_c, f_a, send_c, send_a)
            s_own, s_c, s_a, v_own, v_c, v_a, n_own, n_c, n_a, send_c, send_a = run_again(
                pairs, counts, edge,
                [s_own, s_c, s_a, v_own, v_c, v_a, mean, f_own, f_c, f_a, *got],
                weights,
            )
    wide = lambda t: t.reshape(3, 1, 1, OWN)
    return wide(u_out), wide(vel_out), theta.reshape(1, 1, OWN)


def solution(mesh):
    placed = (
        P(None, "circ", "axial", None),
        P(None, "circ", "axial", None),
        P(None, "circ", "axial", None),
        P("circ", "axial", None),
        P("circ", "axial", None),
        P("circ", "axial", None),
        P("circ", "axial", None, None),
        P("circ", "axial", None, None),
        P("circ", "axial", None),
        P("circ", "axial", None, None, None),
    )
    return jax.shard_map(
        body,
        mesh=mesh,
        in_specs=placed,
        out_specs=(
            P(None, "circ", "axial", None),
            P(None, "circ", "axial", None),
            P("circ", "axial", None),
        ),
        check_vma=False,
    )
```

time: 403 us -> 192 us (0.48)
  the two profiles are of different devices: /device:TPU:2 before, /device:TPU:0 now
where the time goes in v2:
time: 192 us; the launch traced here: 189 us
  Pallas kernels  126 us (66%)
  waiting for transfers between devices  33.1 us (17%)
  starting transfers between devices  26.6 us (14%)
  local copies, waits for them, and re-layouts  2.59 us (1%)
    pallas_call x4, Pallas kernels, sweep(): pl.pallas_call(kernel, out_shape=out_shape, grid_spec=pltpu.PrefetchScala...  120 us
    ppermute x18, waiting for transfers between devices, shift_ring(): return lax.ppermute(block, axis, [(i, (i + by) % n) for i in range(n)])  33.1 us
    ppermute x18, starting transfers between devices, shift_ring(): return lax.ppermute(block, axis, [(i, (i + by) % n) for i in range(n)])  26.6 us
  transfers between devices with their start and end apart: 18, of which 10 were waited for; matrix products, arithmetic and copies ran while one was open for 0% of the time, Pallas kernels for 16%

profile of v2, /device:TPU:0, one launch (start us, length us, event | category | flops | bytes accessed | tf_op | source)
XLA Modules:
  0.0 189.3 jit_solution(1149250107054107320)
XLA Ops:
  0.6 3.7 %pack.1 = (f32[128,8,128]{2,1,0:T(8,128)}, f32[128,8,128]{2,1,0:T(8,128)}, f32[8,128]{1,0:T(8,128)}, f32[32,8,128]{2,1,0:T(8,128)}, f32[32,8,128]{2,1,0:T(8,128)...) custom-call(s32[2,32]{1,0:T(2,128)} %bitcast.25, f32[3,128,128]{2,1,0:T(8,128)} %bitcast.16, f32[3,128,128]{2,1,0:T(8,128)} %bitcast.14, ...), custom_call_target="tpu_custom_call" | custom-call | tf_op jit(solution)/shard_map/pack/pallas_call | solution.py:530
  4.3 6.8 %collective-permute-start = (f32[32,8,128]{2,1,0:T(8,128)}, f32[32,8,128]{2,1,0:T(8,128)S(1)}, u32[]{:S(2)}, u32[]{:S(2)}) collective-permute-start(f32[32,8,128]{2,1,0:T(8,128)} %get-tuple-element.43), channel_id=1, source_target_pairs={{0,112},{16,0},{32,16},{48,32},{64,48},{80,64},{96,80},{112,96},{1... | collective-permute-start | bytes 393224 | tf_op jit(solution)/shard_map/ppermute | solution.py:552
  11.1 2.0 %collective-permute-start.1 = (f32[32,8,128]{2,1,0:T(8,128)}, f32[32,8,128]{2,1,0:T(8,128)S(1)}, u32[]{:S(2)}, u32[]{:S(2)}) collective-permute-start(f32[32,8,128]{2,1,0:T(8,128)} %get-tuple-element.44), channel_id=1, source_target_pairs={{0,15},{1,0},{2,1},{3,2},{4,3},{5,4},{6,5},{7,6},{8,7},{9,8},{10,9... | collective-permute-start | bytes 393224 | tf_op jit(solution)/shard_map/ppermute | solution.py:552
  13.1 2.4 %collective-permute-done.s_c = f32[32,8,128]{2,1,0:T(8,128)S(1)} collective-permute-done((f32[32,8,128]{2,1,0:T(8,128)}, f32[32,8,128]{2,1,0:T(8,128)S(1)}, u32[]{:S(2)}, u32[]{:S(2)}) %collective-permute-start) | collective-permute-done | bytes 131104 | tf_op jit(solution)/shard_map/ppermute | solution.py:552
  15.9 5.7 %collective-permute-start.2 = (f32[32,8,128]{2,1,0:T(8,128)}, f32[32,8,128]{2,1,0:T(8,128)S(1)}, u32[]{:S(2)}, u32[]{:S(2)}) collective-permute-start(f32[32,8,128]{2,1,0:T(8,128)} %get-tuple-element.50), channel_id=1, source_target_pairs={{0,112},{16,0},{32,16},{48,32},{64,48},{80,64},{96,80},{112,96},{1... | collective-permute-start | bytes 393224 | tf_op jit(solution)/shard_map/ppermute | solution.py:552
  21.6 30.9 %dil0.1 = (f32[320,128,128]{2,1,0:T(8,128)}, f32[128,128]{1,0:T(8,128)}, f32[32,128]{1,0:T(8,128)}, f32[32,128]{1,0:T(8,128)}, f32[32,128]{1,0:T(8,128)}, /*index=5*/f32[32,128]{1,0:T(8,128)}) custom-call(s32[2,320]{1,0:T(2,128)} %bitcast.21, s32[2]{0:T(128)} %bitcast.31, s32[2,32]{1,0:T(2,128)} %bitcast.26, f32[128,8,128]{2,1,0:T(8,128)} %get-tuple-element.42.s_own.s_start, ...), custom_call_target="tpu_custom_call" | custom-call | tf_op jit(solution)/shard_map/dil0/pallas_call | solution.py:472
  52.5 1.9 collective-permute-start.4
  54.4 1.6 collective-permute-start.6
  56.0 1.9 %collective-permute-done.4.up_c = f32[32,128]{1,0:T(8,128)S(1)} collective-permute-done((f32[32,128]{1,0:T(8,128)}, f32[32,128]{1,0:T(8,128)S(1)}, u32[]{:S(2)}, u32[]{:S(2)}) %collective-permute-start.4) | collective-permute-done | bytes 16416 | tf_op jit(solution)/shard_map/ppermute | solution.py:552
  58.0 4.1 %collective-permute-done.6.back_c = f32[32,128]{1,0:T(8,128)S(1)} collective-permute-done((f32[32,128]{1,0:T(8,128)}, f32[32,128]{1,0:T(8,128)S(1)}, u32[]{:S(2)}, u32[]{:S(2)}) %collective-permute-start.6) | collective-permute-done | bytes 16416 | tf_op jit(solution)/shard_map/ppermute | solution.py:552
  62.1 1.4 collective-permute-done.7.back_a
  64.2 30.4 %force.2 = (f32[128,128]{1,0:T(8,128)}, f32[128,4,128]{2,1,0:T(4,128)}, f32[32,4,128]{2,1,0:T(4,128)}, f32[32,4,128]{2,1,0:T(4,128)}, f32[32,4,128]{2,1,0:T(4,128)}, /*index=5*/f32[32,4,128]{2,1,0:T(4,128)}) custom-call(s32[2,320]{1,0:T(2,128)} %bitcast.22, s32[2]{0:T(128)} %bitcast.32, s32[2,32]{1,0:T(2,128)} %bitcast.27, ...), custom_call_target="tpu_custom_call" | custom-call | tf_op jit(solution)/shard_map/force/pallas_call | solution.py:472
  94.6 4.1 %collective-permute-start.8 = (f32[32,4,128]{2,1,0:T(4,128)}, f32[32,4,128]{2,1,0:T(4,128)S(1)}, u32[]{:S(2)}, u32[]{:S(2)}) collective-permute-start(f32[32,4,128]{2,1,0:T(4,128)} %get-tuple-element.62), channel_id=1, source_target_pairs={{0,112},{16,0},{32,16},{48,32},{64,48},{80,64},{96,80},{112,96},{1... | collective-permute-start | bytes 196616 | tf_op jit(solution)/shard_map/ppermute | solution.py:552
  99.2 2.3 %collective-permute-done.8.up_c = f32[32,4,128]{2,1,0:T(4,128)S(1)} collective-permute-done((f32[32,4,128]{2,1,0:T(4,128)}, f32[32,4,128]{2,1,0:T(4,128)S(1)}, u32[]{:S(2)}, u32[]{:S(2)}) %collective-permute-start.8) | collective-permute-done | bytes 65568 | tf_op jit(solution)/shard_map/ppermute | solution.py:552
  101.5 6.0 %collective-permute-done.10.back_c = f32[32,4,128]{2,1,0:T(4,128)S(1)} collective-permute-done((f32[32,4,128]{2,1,0:T(4,128)}, f32[32,4,128]{2,1,0:T(4,128)S(1)}, u32[]{:S(2)}, u32[]{:S(2)}) %collective-permute-start.10) | collective-permute-done | bytes 65568 | tf_op jit(solution)/shard_map/ppermute | solution.py:552
  108.1 27.8 %dil1.1 = (f32[128,8,128]{2,1,0:T(8,128)}, f32[32,8,128]{2,1,0:T(8,128)}, f32[32,8,128]{2,1,0:T(8,128)}, f32[128,8,128]{2,1,0:T(8,128)}, f32[32,8,128]{2,1,0:T(8...) custom-call(s32[2,320]{1,0:T(2,128)} %bitcast.23, ...), custom_call_target="tpu_custom_call" | custom-call | tf_op jit(solution)/shard_map/dil1/pallas_call | solution.py:472
  135.9 2.9 %collective-permute-start.12 = (f32[32,128]{1,0:T(8,128)}, f32[32,128]{1,0:T(8,128)S(1)}, u32[]{:S(2)}, u32[]{:S(2)}) collective-permute-start(f32[32,128]{1,0:T(8,128)} %get-tuple-element.73), channel_id=1, source_target_pairs={{0,112},{16,0},{32,16},{48,32},{64,48},{80,64},{96,80},{112,96},{1... | collective-permute-start | bytes 49160 | tf_op jit(solution)/shard_map/ppermute | solution.py:552
  138.8 0.7 collective-permute-start.14
  139.8 1.9 collective-permute-done.12.up_c
  141.6 4.8 %collective-permute-done.14.back_c = f32[32,128]{1,0:T(8,128)S(1)} collective-permute-done((f32[32,128]{1,0:T(8,128)}, f32[32,128]{1,0:T(8,128)S(1)}, u32[]{:S(2)}, u32[]{:S(2)}) %collective-permute-start.14) | collective-permute-done | bytes 16416 | tf_op jit(solution)/shard_map/ppermute | solution.py:552
  147.0 30.4 %force.3 = (f32[128,128]{1,0:T(8,128)}, f32[128,4,128]{2,1,0:T(4,128)}, f32[32,4,128]{2,1,0:T(4,128)}, f32[32,4,128]{2,1,0:T(4,128)}, f32[32,4,128]{2,1,0:T(4,128)}, /*index=5*/f32[32,4,128]{2,1,0:T(4,128)}) custom-call(s32[2,320]{1,0:T(2,128)} %bitcast.24, s32[2]{0:T(128)} %bitcast.34, s32[2,32]{1,0:T(2,128)} %bitcast.29, ...), custom_call_target="tpu_custom_call" | custom-call | tf_op jit(solution)/shard_map/force/pallas_call | solution.py:472
  177.6 8.0 %collective-permute-done.16.back_c = f32[32,4,128]{2,1,0:T(4,128)S(1)} collective-permute-done((f32[32,4,128]{2,1,0:T(4,128)}, f32[32,4,128]{2,1,0:T(4,128)S(1)}, u32[]{:S(2)}, u32[]{:S(2)}) %collective-permute-start.16) | collective-permute-done | bytes 65568 | tf_op jit(solution)/shard_map/ppermute | solution.py:552
  185.6 0.6 copy-done.8
  186.2 3.0 %finish.1 = (f32[3,128,128]{2,1,0:T(8,128)}, f32[3,128,128]{2,1,0:T(8,128)}) custom-call(s32[2,32]{1,0:T(2,128)} %bitcast.30, f32[3,128,128]{2,1,0:T(8,128)} %bitcast.15, f32[128,8,128]{2,1,0:T(8,128)} %get-tuple-element.42.s_own.s_start, f32[128,8,128]{2,1,0:T(8,128)} %get-tuple-element.64.s_own, f32[128,8,128]{2,1,0:T(8,128)} %get-tuple-element.65.v_own, ...), custom_call_target="tpu_custom_call" | custom-call | tf_op jit(solution)/shard_map/finish/pallas_call | solution.py:540
  (54 shorter events, 3.3 us)
Async XLA Ops:
  4.3 11.3 %collective-permute-start = (f32[32,8,128]{2,1,0:T(8,128)}, f32[32,8,128]{2,1,0:T(8,128)S(1)}, u32[]{:S(2)}, u32[]{:S(2)}) collective-permute-start(f32[32,8,128]{2,1,0:T(8,128)} %get-tuple-element.43), channel_id=1, source_target_pairs={{0,112},{16,0},{32,16},{48,32},{64,48},{80,64},{96,80},{112,96},{1... | collective-permute-start | bytes 393224 | tf_op jit(solution)/shard_map/ppermute | solution.py:552
  11.1 4.9 %collective-permute-start.1 = (f32[32,8,128]{2,1,0:T(8,128)}, f32[32,8,128]{2,1,0:T(8,128)S(1)}, u32[]{:S(2)}, u32[]{:S(2)}) collective-permute-start(f32[32,8,128]{2,1,0:T(8,128)} %get-tuple-element.44), channel_id=1, source_target_pairs={{0,15},{1,0},{2,1},{3,2},{4,3},{5,4},{6,5},{7,6},{8,7},{9,8},{10,9... | collective-permute-start | bytes 393224 | tf_op jit(solution)/shard_map/ppermute | solution.py:552
  15.5 6.1 %copy-start = (f32[32,8,128]{2,1,0:T(8,128)}, f32[32,8,128]{2,1,0:T(8,128)S(1)}, u32[]{:S(2)}) copy-start(f32[32,8,128]{2,1,0:T(8,128)S(1)} %collective-permute-done.s_c) | copy-start | bytes 393220
  15.9 5.7 %copy-start.1 = (f32[32,8,128]{2,1,0:T(8,128)}, f32[32,8,128]{2,1,0:T(8,128)S(1)}, u32[]{:S(2)}) copy-start(f32[32,8,128]{2,1,0:T(8,128)S(1)} %collective-permute-done.1.s_a) | copy-start | bytes 393220
  15.9 47.5 %collective-permute-start.2 = (f32[32,8,128]{2,1,0:T(8,128)}, f32[32,8,128]{2,1,0:T(8,128)S(1)}, u32[]{:S(2)}, u32[]{:S(2)}) collective-permute-start(f32[32,8,128]{2,1,0:T(8,128)} %get-tuple-element.50), channel_id=1, source_target_pairs={{0,112},{16,0},{32,16},{48,32},{64,48},{80,64},{96,80},{112,96},{1... | collective-permute-start | bytes 393224 | tf_op jit(solution)/shard_map/ppermute | solution.py:552
  21.6 41.9 %collective-permute-start.3 = (f32[32,8,128]{2,1,0:T(8,128)}, f32[32,8,128]{2,1,0:T(8,128)S(1)}, u32[]{:S(2)}, u32[]{:S(2)}) collective-permute-start(f32[32,8,128]{2,1,0:T(8,128)} %get-tuple-element.51), channel_id=1, source_target_pairs={{0,15},{1,0},{2,1},{3,2},{4,3},{5,4},{6,5},{7,6},{8,7},{9,8},{10,9... | collective-permute-start | bytes 393224 | tf_op jit(solution)/shard_map/ppermute | solution.py:552
  52.5 5.5 %collective-permute-start.4 = (f32[32,128]{1,0:T(8,128)}, f32[32,128]{1,0:T(8,128)S(1)}, u32[]{:S(2)}, u32[]{:S(2)}) collective-permute-start(f32[32,128]{1,0:T(8,128)} %get-tuple-element.56), channel_id=1, source_target_pairs={{0,112},{16,0},{32,16},{48,32},{64,48},{80,64},{96,80},{112,96},{1... | collective-permute-start | bytes 49160 | tf_op jit(solution)/shard_map/ppermute | solution.py:552
  54.4 3.6 %collective-permute-start.5 = (f32[32,128]{1,0:T(8,128)}, f32[32,128]{1,0:T(8,128)S(1)}, u32[]{:S(2)}, u32[]{:S(2)}) collective-permute-start(f32[32,128]{1,0:T(8,128)} %get-tuple-element.57), channel_id=1, source_target_pairs={{0,15},{1,0},{2,1},{3,2},{4,3},{5,4},{6,5},{7,6},{8,7},{9,8},{10,9... | collective-permute-start | bytes 49160 | tf_op jit(solution)/shard_map/ppermute | solution.py:552
  54.4 7.7 %collective-permute-start.6 = (f32[32,128]{1,0:T(8,128)}, f32[32,128]{1,0:T(8,128)S(1)}, u32[]{:S(2)}, u32[]{:S(2)}) collective-permute-start(f32[32,128]{1,0:T(8,128)} %get-tuple-element.54.n_c), channel_id=1, source_target_pairs={{0,16},{16,32},{32,48},{48,64},{64,80},{80,96},{96,112},{112,0},{1... | collective-permute-start | bytes 49160 | tf_op jit(solution)/shard_map/ppermute | solution.py:552
  58.0 5.5 %copy-start.10 = (f32[32,128]{1,0:T(8,128)}, f32[32,128]{1,0:T(8,128)S(1)}, u32[]{:S(2)}) copy-start(f32[32,128]{1,0:T(8,128)S(1)} %collective-permute-done.4.up_c) | copy-start | bytes 49156
  58.0 5.5 %collective-permute-start.7 = (f32[32,128]{1,0:T(8,128)}, f32[32,128]{1,0:T(8,128)S(1)}, u32[]{:S(2)}, u32[]{:S(2)}) collective-permute-start(f32[32,128]{1,0:T(8,128)} %get-tuple-element.55.n_a), channel_id=1, source_target_pairs={{0,1},{1,2},{2,3},{3,4},{4,5},{5,6},{6,7},{7,8},{8,9},{9,10},{10,1... | collective-permute-start | bytes 49160 | tf_op jit(solution)/shard_map/ppermute | solution.py:552
  58.0 5.5 %copy-start.11 = (f32[32,128]{1,0:T(8,128)}, f32[32,128]{1,0:T(8,128)S(1)}, u32[]{:S(2)}) copy-start(f32[32,128]{1,0:T(8,128)S(1)} %collective-permute-done.5.up_a) | copy-start | bytes 49156
  94.6 6.9 %collective-permute-start.8 = (f32[32,4,128]{2,1,0:T(4,128)}, f32[32,4,128]{2,1,0:T(4,128)S(1)}, u32[]{:S(2)}, u32[]{:S(2)}) collective-permute-start(f32[32,4,128]{2,1,0:T(4,128)} %get-tuple-element.62), channel_id=1, source_target_pairs={{0,112},{16,0},{32,16},{48,32},{64,48},{80,64},{96,80},{112,96},{1... | collective-permute-start | bytes 196616 | tf_op jit(solution)/shard_map/ppermute | solution.py:552
  98.7 2.8 %collective-permute-start.9 = (f32[32,4,128]{2,1,0:T(4,128)}, f32[32,4,128]{2,1,0:T(4,128)S(1)}, u32[]{:S(2)}, u32[]{:S(2)}) collective-permute-start(f32[32,4,128]{2,1,0:T(4,128)} %get-tuple-element.63), channel_id=1, source_target_pairs={{0,15},{1,0},{2,1},{3,2},{4,3},{5,4},{6,5},{7,6},{8,7},{9,8},{10,9... | collective-permute-start | bytes 196616 | tf_op jit(solution)/shard_map/ppermute | solution.py:552
  98.7 8.8 %collective-permute-start.10 = (f32[32,4,128]{2,1,0:T(4,128)}, f32[32,4,128]{2,1,0:T(4,128)S(1)}, u32[]{:S(2)}, u32[]{:S(2)}) collective-permute-start(f32[32,4,128]{2,1,0:T(4,128)} %get-tuple-element.60.f_c), channel_id=1, source_target_pairs={{0,16},{16,32},{32,48},{48,64},{64,80},{80,96},{96,112},{112,0},{1... | collective-permute-start | bytes 196616 | tf_op jit(solution)/shard_map/ppermute | solution.py:552
  98.7 8.8 %collective-permute-start.11 = (f32[32,4,128]{2,1,0:T(4,128)}, f32[32,4,128]{2,1,0:T(4,128)S(1)}, u32[]{:S(2)}, u32[]{:S(2)}) collective-permute-start(f32[32,4,128]{2,1,0:T(4,128)} %get-tuple-element.61.f_a), channel_id=1, source_target_pairs={{0,1},{1,2},{2,3},{3,4},{4,5},{5,6},{6,7},{7,8},{8,9},{9,10},{10,1... | collective-permute-start | bytes 196616 | tf_op jit(solution)/shard_map/ppermute | solution.py:552
  101.5 6.0 %copy-start.4 = (f32[32,4,128]{2,1,0:T(4,128)}, f32[32,4,128]{2,1,0:T(4,128)S(1)}, u32[]{:S(2)}) copy-start(f32[32,4,128]{2,1,0:T(4,128)S(1)} %collective-permute-done.8.up_c) | copy-start | bytes 196612
  101.5 6.0 %copy-start.5 = (f32[32,4,128]{2,1,0:T(4,128)}, f32[32,4,128]{2,1,0:T(4,128)S(1)}, u32[]{:S(2)}) copy-start(f32[32,4,128]{2,1,0:T(4,128)S(1)} %collective-permute-done.9.up_a) | copy-start | bytes 196612
  135.9 5.7 %collective-permute-start.12 = (f32[32,128]{1,0:T(8,128)}, f32[32,128]{1,0:T(8,128)S(1)}, u32[]{:S(2)}, u32[]{:S(2)}) collective-permute-start(f32[32,128]{1,0:T(8,128)} %get-tuple-element.73), channel_id=1, source_target_pairs={{0,112},{16,0},{32,16},{48,32},{64,48},{80,64},{96,80},{112,96},{1... | collective-permute-start | bytes 49160 | tf_op jit(solution)/shard_map/ppermute | solution.py:552
  138.8 2.8 %collective-permute-start.13 = (f32[32,128]{1,0:T(8,128)}, f32[32,128]{1,0:T(8,128)S(1)}, u32[]{:S(2)}, u32[]{:S(2)}) collective-permute-start(f32[32,128]{1,0:T(8,128)} %get-tuple-element.74), channel_id=1, source_target_pairs={{0,15},{1,0},{2,1},{3,2},{4,3},{5,4},{6,5},{7,6},{8,7},{9,8},{10,9... | collective-permute-start | bytes 49160 | tf_op jit(solution)/shard_map/ppermute | solution.py:552
  138.8 7.6 %collective-permute-start.14 = (f32[32,128]{1,0:T(8,128)}, f32[32,128]{1,0:T(8,128)S(1)}, u32[]{:S(2)}, u32[]{:S(2)}) collective-permute-start(f32[32,128]{1,0:T(8,128)} %get-tuple-element.71.n_c), channel_id=1, source_target_pairs={{0,16},{16,32},{32,48},{48,64},{64,80},{80,96},{96,112},{112,0},{1... | collective-permute-start | bytes 49160 | tf_op jit(solution)/shard_map/ppermute | solution.py:552
  139.5 6.9 %collective-permute-start.15 = (f32[32,128]{1,0:T(8,128)}, f32[32,128]{1,0:T(8,128)S(1)}, u32[]{:S(2)}, u32[]{:S(2)}) collective-permute-start(f32[32,128]{1,0:T(8,128)} %get-tuple-element.72.n_a), channel_id=1, source_target_pairs={{0,1},{1,2},{2,3},{3,4},{4,5},{5,6},{6,7},{7,8},{8,9},{9,10},{10,1... | collective-permute-start | bytes 49160 | tf_op jit(solution)/shard_map/ppermute | solution.py:552
  177.4 8.2 %collective-permute-start.16 = (f32[32,4,128]{2,1,0:T(4,128)}, f32[32,4,128]{2,1,0:T(4,128)S(1)}, u32[]{:S(2)}, u32[]{:S(2)}) collective-permute-start(f32[32,4,128]{2,1,0:T(4,128)} %get-tuple-element.76), channel_id=1, source_target_pairs={{0,16},{16,32},{32,48},{48,64},{64,80},{80,96},{96,112},{112,0},{1... | collective-permute-start | bytes 196616 | tf_op jit(solution)/shard_map/ppermute | solution.py:552
  177.5 8.1 %collective-permute-start.17 = (f32[32,4,128]{2,1,0:T(4,128)}, f32[32,4,128]{2,1,0:T(4,128)S(1)}, u32[]{:S(2)}, u32[]{:S(2)}) collective-permute-start(f32[32,4,128]{2,1,0:T(4,128)} %get-tuple-element.77), channel_id=1, source_target_pairs={{0,1},{1,2},{2,3},{3,4},{4,5},{5,6},{6,7},{7,8},{8,9},{9,10},{10,1... | collective-permute-start | bytes 196616 | tf_op jit(solution)/shard_map/ppermute | solution.py:552
  (12 other events, 16.7 us)

commit v3 on v2

--- a/solution.py
+++ b/solution.py
@@ -20,6 +20,7 @@
 TINY = 1e-30
 GROUP = 32
 UNROLL = 16
+KERNEL_VMEM = 36 << 20
 OWN = CL * PTS
 GHOST = FACING * PTS
 F32 = jnp.float32
@@ -72,22 +73,13 @@
     a1 = jnp.where(norm, 0.0, 2.0 * p1)
     a2 = jnp.where(norm, 0.0, 2.0 * p2)
     n0 = jnp.where(norm, -p0, 0.0)
-    shifted = pltpu.roll(p2, 1, 0)
     n1 = jnp.where(norm, -p1, 0.0)
-    upper = row < 4
-    after = (row == 4) | (row == 0)
-    stack = jnp.concatenate([a0, a1, a2, a0, a1, a0], axis=0)
-    up6 = jnp.concatenate([upper] * 6, axis=0)
-
-    def half(top):
-        keep = up6 if top else ~up6
-        body = jnp.where(keep, stack, 0.0)
-        near = upper if top else ~upper
-        tail0 = jnp.where(near, n0, 0.0)
-        tail1 = jnp.where(near, n1, 0.0) - jnp.where(row == (4 if top else 0), shifted, 0.0)
-        return jnp.concatenate([body, tail0, tail1], axis=0).astype(BF16)
-
-    return half(True), half(False)
+    n2 = jnp.where((row == 2) | (row == 6), -pltpu.roll(p2, 7, 0), 0.0)
+    stack = jnp.concatenate([a0, a1, a2, a0, a1, a0, n0, n1 + n2], axis=0).astype(BF16)
+    top = (lax.broadcasted_iota(jnp.int32, (64, PTS), 0) & 4) == 0
+    ones = jnp.where(top, 1.0, 0.0).astype(BF16)
+    zeros = jnp.where(top, 0.0, 1.0).astype(BF16)
+    return stack * ones, stack * zeros
 
 
 def moment_features(parts):
@@ -125,22 +117,30 @@
 
 def pack_kernel(edges, x_ref, u_ref, v_ref, bulk, shear, volume, s_out, v_out, mean,
                 sc_out, sa_out, vc_out, va_out):
-    zero = jnp.zeros((1, PTS), F32)
-
-    def cluster(c):
-        r = one_row(c)
+    zero = jnp.zeros((8, PTS), F32)
+    s_rows = s_out.reshape(CL * 8, PTS)
+    v_rows = v_out.reshape(CL * 8, PTS)
+
+    def eight(i):
+        r = pl.ds(pl.multiple_of(i * 8, 8), 8)
+
+        def put(ref, k, value):
+            ref[pl.ds(i * 64 + k, 8, stride=8), :] = value
+
         x = [KAPPA * x_ref[k, r, :] for k in range(3)]
         y = [x[k] + KAPPA * u_ref[k, r, :] for k in range(3)]
-        s_out[c] = jnp.concatenate([*x, zero, *y, zero], axis=0)
-        inv = 1.0 / volume[r, :]
+        vol = volume[r, :]
         mu = shear[r, :]
-        dil = (3.0 * bulk[r, :] - 5.0 * mu) * inv
-        dev = 15.0 * mu * inv
-        thr = (3.0 / LOG2E) * inv
+        dil = (3.0 * bulk[r, :] - 5.0 * mu) / vol
+        dev = 15.0 * mu / vol
+        thr = (3.0 / LOG2E) / vol
         v = [KAPPA * v_ref[k, r, :] for k in range(3)]
-        v_out[c] = jnp.concatenate([dil, dev, thr, zero, *v, zero], axis=0)
-
-    loop(CL, cluster, 4)
+        for k, value in enumerate([*x, zero, *y, zero]):
+            put(s_rows, k, value)
+        for k, value in enumerate([dil, dev, thr, zero, *v, zero]):
+            put(v_rows, k, value)
+
+    loop(CL // 8, eight, 2)
     total = jnp.sum(jnp.sum(s_out[...], axis=0), axis=1, keepdims=True)
     mean[...] = jnp.broadcast_to(total * (1.0 / OWN), (8, PTS))
 
@@ -153,26 +153,33 @@
     loop(FACING, copy, 4)
 
 
-def build_geometry(c, s, left, right, moments):
+def build_one(c, s, left, right, moments):
     parts = coordinate_parts(s)
     if left is not None:
         left[c] = source_features(parts)
     t0, t1 = target_features(parts)
     right[c, :, 0:PTS] = t0
     right[c, :, PTS:] = t1
-    if moments is not None:
-        moments[c] = moment_features(parts)
-
-
-def build_all(s_own, s_c, s_a, mean, left, right, moments):
+    moments[c] = moment_features(parts)
+
+
+def build_own(s_own, mean, left, right, moments):
     shift = mean[...]
-    loop(CL, lambda c: build_geometry(c, s_own[c] - shift, left, right, moments), 4)
+    loop(CL, lambda c: build_one(c, s_own[c] - shift, left, right, moments), 4)
+
+
+def build_ghosts(s_c, s_a, mean, right, moments):
+    shift = mean[...]
 
     def ghost(f):
-        build_geometry(CL + f, s_c[f] - shift, None, right, moments)
-        build_geometry(CL + FACING + f, s_a[f] - shift, None, right, moments)
-
-    loop(FACING, ghost, 2)
+        build_one(CL + f, s_c[f] - shift, None, right, moments)
+        build_one(CL + FACING + f, s_a[f] - shift, None, right, moments)
+
+    loop(FACING, ghost, 4)
+
+
+def ghosts_kernel(s_c, s_a, mean, right_in, moments_in, right, moments):
+    build_ghosts(s_c, s_a, mean, right, moments)
 
 
 def turns_here(counts):
@@ -205,14 +212,18 @@
 
 
 def first_finish(edges, acc, racc, n_own, n_c, n_a, send_c, send_a):
-    ones = jnp.ones((16, 2 * PTS), BF16)
+    ones = jnp.ones((2 * PTS, PTS), BF16)
+    i0 = lax.broadcasted_iota(jnp.int32, (PTS, PTS), 0)
+    i1 = lax.broadcasted_iota(jnp.int32, (PTS, PTS), 1)
+    diagonal = i0 == i1
 
     def own(c):
         h, l = hilo(racc[c])
-        across = dot(ones, jnp.concatenate([h, l], axis=1), NT)
-        n_own[one_row(c), :] = across[0:1] + jnp.sum(acc[c], axis=0, keepdims=True)
-
-    loop(CL, own, 4)
+        across = dot(jnp.concatenate([h, l], axis=1), ones, NN)
+        along = jnp.sum(jnp.where(diagonal, across, 0.0).reshape(16, 8, PTS), axis=0)
+        n_own[one_row(c), :] = jnp.sum(along + acc[c], axis=0, keepdims=True)
+
+    loop(CL, own, 8)
 
     def ghost(f):
         r = one_row(f)
@@ -225,13 +236,21 @@
 
 
 def clear(ref):
-    loop(ref.shape[0], lambda c: ref.__setitem__(c, jnp.zeros(ref.shape[1:], ref.dtype)), 1)
+    n = ref.shape[0] // 8 * 8
+    zero = jnp.zeros(ref.shape[1:], ref.dtype)
+
+    def one(c):
+        ref[c] = zero
+
+    loop(n, one, 8)
+    for c in range(n, ref.shape[0]):
+        one(c)
 
 
 def dilatation_first(
-    pairs, counts, edges, s_own, s_c, s_a, mean, damage,
+    pairs, counts, edges, left, right, damage,
     w_out, n_own, n_c, n_a, send_c, send_a,
-    left, right, acc, racc, cut,
+    acc, racc, cut,
 ):
     g = pl.program_id(0)
 
@@ -243,7 +262,6 @@
         i1 = lax.broadcasted_iota(jnp.int32, (PTS, PTS), 1)
         cut[0] = jnp.where(i0 < i1, 0, 1)
         cut[1] = jnp.zeros((PTS, PTS), jnp.int32)
-        build_all(s_own, s_c, s_a, mean, left, right, None)
 
     def weight_of(na, k, slot):
         keep = damage[k] > cut[jnp.where(slot < CL, 0, 1)]
@@ -258,11 +276,18 @@
         first_finish(edges, acc, racc, n_own, n_c, n_a, send_c, send_a)
 
 
+def advance_kernel(
+    edges, s_own, s_c, s_a, v_own, v_c, v_a, mean, f_own, f_c, f_a, up_c, up_a, back_c, back_a,
+    s_own2, s_c2, s_a2, v_own2, v_c2, v_a2, left, right, moments,
+):
+    advance(edges, s_own, s_c, s_a, v_own, v_c, v_a, f_own, f_c, f_a, up_c, up_a, back_c,
+            back_a, s_own2, s_c2, s_a2, v_own2, v_c2, v_a2)
+    build_own(s_own2, mean, left, right, moments)
+    build_ghosts(s_c2, s_a2, mean, right, moments)
+
+
 def dilatation_again(
-    pairs, counts, edges, s_own, s_c, s_a, v_own, v_c, v_a, mean, f_own, f_c, f_a,
-    up_c, up_a, back_c, back_a, weights,
-    s_own2, s_c2, s_a2, v_own2, v_c2, v_a2, n_own, n_c, n_a, send_c, send_a,
-    left, right, acc, racc,
+    pairs, counts, edges, left, right, weights, n_own, n_c, n_a, send_c, send_a, acc, racc
 ):
     g = pl.program_id(0)
 
@@ -270,9 +295,6 @@
     def _():
         clear(acc)
         clear(racc)
-        advance(edges, s_own, s_c, s_a, v_own, v_c, v_a, f_own, f_c, f_a, up_c, up_a, back_c,
-                back_a, s_own2, s_c2, s_a2, v_own2, v_c2, v_a2)
-        build_all(s_own2, s_c2, s_a2, mean, left, right, None)
 
     first_sweep(pairs, counts, lambda na, k, slot: weights[k], left, right, acc, racc)
 
@@ -305,10 +327,10 @@
 
 
 def force_pass(
-    pairs, counts, edges, s_own, s_c, s_a, v_own, v_c, v_a, mean, n_own, n_c, n_a,
-    up_c, up_a, back_c, back_a, weights,
+    pairs, counts, edges, left, right, moments, s_own, s_c, s_a, v_own, v_c, v_a, mean,
+    n_own, n_c, n_a, up_c, up_a, back_c, back_a, weights,
     theta_out, f_own, f_c, f_a, send_c, send_a,
-    left, right, left2, right2, moments, acc, n_full, geo, halves,
+    left2, right2, acc, n_full, geo, halves,
 ):
     def geometry(slot, j):
         s = jnp.minimum(slot, SLOTS - 1)
@@ -348,7 +370,6 @@
     @pl.when(g == 0)
     def _():
         clear(acc)
-        build_all(s_own, s_c, s_a, mean, left, right, moments)
         n_full[0:CL, :] = n_own[...]
 
         def mend(f):
@@ -433,16 +454,19 @@
 
     loop(FACING, mend, 4)
 
-    def cluster(c):
-        r = one_row(c)
-        v2 = v_own[c][4:8] + TIMESTEP * f_sum[c]
-        vel = v2 * (1.0 / KAPPA)
-        gone = ((s_own[c] - s_start[c])[4:8] + TIMESTEP * v2) * (1.0 / KAPPA)
+    views = [t.reshape(CL * 8, PTS) for t in (s_own, s_start, v_own)]
+    f_rows = f_sum.reshape(CL * 4, PTS)
+
+    def eight(i):
+        r = pl.ds(pl.multiple_of(i * 8, 8), 8)
         for k in range(3):
-            vel_out[k, r, :] = vel[k : k + 1]
-            u_out[k, r, :] = u_ref[k, r, :] + gone[k : k + 1]
-
-    loop(CL, cluster, 4)
+            now, start, vel = (t[pl.ds(i * 64 + 4 + k, 8, stride=8), :] for t in views)
+            vel = vel + TIMESTEP * f_rows[pl.ds(i * 32 + k, 8, stride=4), :]
+            vel_out[k, r, :] = vel * (1.0 / KAPPA)
+            gone = (now - start) + TIMESTEP * vel
+            u_out[k, r, :] = u_ref[k, r, :] + gone * (1.0 / KAPPA)
+
+    loop(CL // 8, eight, 2)
 
 
 SMEM = pl.BlockSpec(memory_space=pltpu.SMEM)
@@ -460,7 +484,9 @@
     return pl.BlockSpec((GROUP, PTS, PTS), index)
 
 
-def sweep(kernel, name, pairs, counts, edges, tables, slab, out_tables, scratch, slab_out=None):
+def sweep(
+    kernel, name, pairs, counts, edges, resident, tables, slab, out_tables, scratch, slab_out=None
+):
     def whole(x, **kw):
         return pl.BlockSpec(x.shape, lambda g, a, b: (0,) * x.ndim, **kw)
 
@@ -475,48 +501,78 @@
         grid_spec=pltpu.PrefetchScalarGridSpec(
             num_scalar_prefetch=2,
             grid=(SLOTS // GROUP,),
-            in_specs=[SMEM] + [whole(x, pipeline_mode=pl.Buffered(1)) for x in tables] + [slab_spec()],
+            in_specs=[SMEM]
+            + [VMEM] * len(resident)
+            + [whole(x, pipeline_mode=pl.Buffered(1)) for x in tables]
+            + [slab_spec()],
             out_specs=outs,
             scratch_shapes=scratch,
         ),
         compiler_params=pltpu.CompilerParams(
-            dimension_semantics=("arbitrary",), vmem_limit_bytes=56 << 20
+            dimension_semantics=("arbitrary",), vmem_limit_bytes=KERNEL_VMEM
         ),
         name=name,
-    )(pairs, counts, edges, *tables, slab)
-
-
-LEFT = pltpu.VMEM((CL, PTS, 64), BF16)
-RIGHT = pltpu.VMEM((EXT, 64, 2 * PTS), BF16)
+    )(pairs, counts, edges, *resident, *tables, slab)
+
+
+LEFT = jax.ShapeDtypeStruct((CL, PTS, 64), BF16)
+RIGHT = jax.ShapeDtypeStruct((EXT, 64, 2 * PTS), BF16)
+MOMENTS = jax.ShapeDtypeStruct((EXT, 16, 2 * PTS), BF16)
 N_TABLES = [table(CL, PTS)] + [table(FACING, PTS)] * 4
 F_TABLES = [table(CL, 4, PTS)] + [table(FACING, 4, PTS)] * 4
 STATES = [table(CL, 8, PTS), table(FACING, 8, PTS), table(FACING, 8, PTS)]
 SUMS = [pltpu.VMEM((EXT + 1, 8, PTS), F32), pltpu.VMEM((CL + 1, PTS, PTS), F32)]
 
 
-def run_first(pairs, counts, edges, s_own, s_c, s_a, mean, damage):
+def small(kernel, name, out_shape, args, smem=0, aliases=None):
+    return pl.pallas_call(
+        kernel,
+        out_shape=out_shape,
+        in_specs=[SMEM] * smem + [VMEM] * (len(args) - smem),
+        out_specs=[VMEM] * len(out_shape),
+        input_output_aliases=aliases or {},
+        compiler_params=pltpu.CompilerParams(vmem_limit_bytes=KERNEL_VMEM),
+        name=name,
+    )(*args)
+
+
+def run_build(s_own, mean):
+    return small(build_own, "build", [LEFT, RIGHT, MOMENTS], [s_own, mean])
+
+
+def run_ghosts(s_c, s_a, mean, right, moments):
+    return small(
+        ghosts_kernel, "ghosts", [RIGHT, MOMENTS], [s_c, s_a, mean, right, moments],
+        aliases={3: 0, 4: 1},
+    )
+
+
+def run_advance(edges, tables):
+    return small(
+        advance_kernel, "advance", STATES * 2 + [LEFT, RIGHT, MOMENTS], [edges, *tables], smem=1
+    )
+
+
+def run_first(pairs, counts, edges, resident, damage):
     return sweep(
-        dilatation_first, "dil0", pairs, counts, edges, [s_own, s_c, s_a, mean], damage, N_TABLES,
-        [LEFT, RIGHT, *SUMS, pltpu.VMEM((2, PTS, PTS), jnp.int32)],
+        dilatation_first, "dil0", pairs, counts, edges, resident, [], damage, N_TABLES,
+        [*SUMS, pltpu.VMEM((2, PTS, PTS), jnp.int32)],
         slab_out=table(SLOTS, PTS, PTS),
     )
 
 
-def run_again(pairs, counts, edges, tables, weights):
+def run_again(pairs, counts, edges, resident, weights):
     return sweep(
-        dilatation_again, "dil1", pairs, counts, edges, tables, weights, STATES * 2 + N_TABLES,
-        [LEFT, RIGHT, *SUMS],
-    )
-
-
-def run_force(pairs, counts, edges, tables, weights):
+        dilatation_again, "dil1", pairs, counts, edges, resident, [], weights, N_TABLES, SUMS
+    )
+
+
+def run_force(pairs, counts, edges, resident, tables, weights):
     return sweep(
-        force_pass, "force", pairs, counts, edges, tables, weights, [table(CL, PTS)] + F_TABLES,
+        force_pass, "force", pairs, counts, edges, resident, tables, weights,
+        [table(CL, PTS)] + F_TABLES,
         [
-            LEFT,
-            RIGHT,
             pltpu.VMEM((CL, PTS, 16), BF16),
-            pltpu.VMEM((EXT, 16, 2 * PTS), BF16),
             pltpu.VMEM((EXT, 16, 2 * PTS), BF16),
             pltpu.VMEM((EXT + 1, 16, PTS), F32),
             pltpu.VMEM((EXT, PTS), F32),
@@ -576,16 +632,18 @@
     s_start = s_own
     s_c = shift_ring(s_c, "circ", -1)
     s_a = shift_ring(s_a, "axial", -1)
+    left, right, moments = run_build(s_own, mean)
     s_c, s_a, v_c, v_a = lax.optimization_barrier((s_c, s_a, v_c, v_a))
+    right, moments = run_ghosts(s_c, s_a, mean, right, moments)
     v_c = shift_ring(v_c, "circ", -1)
     v_a = shift_ring(v_a, "axial", -1)
     weights, n_own, n_c, n_a, send_c, send_a = run_first(
-        pairs, counts, edge, s_own, s_c, s_a, mean, damage[0, 0]
+        pairs, counts, edge, [left, right], damage[0, 0]
     )
     for step in range(STEPS):
         got = exchange(n_c, n_a, send_c, send_a)
         theta, f_own, f_c, f_a, send_c, send_a = run_force(
-            pairs, counts, edge,
+            pairs, counts, edge, [left, right, moments],
             [s_own, s_c, s_a, v_own, v_c, v_a, mean, n_own, n_c, n_a, *got],
             weights,
         )
@@ -595,10 +653,11 @@
             u_out, vel_out = run_finish(edge, u, s_start, s_own, v_own, f_own, back_c, back_a)
         else:
             got = exchange(f_c, f_a, send_c, send_a)
-            s_own, s_c, s_a, v_own, v_c, v_a, n_own, n_c, n_a, send_c, send_a = run_again(
-                pairs, counts, edge,
-                [s_own, s_c, s_a, v_own, v_c, v_a, mean, f_own, f_c, f_a, *got],
-                weights,
+            s_own, s_c, s_a, v_own, v_c, v_a, left, right, moments = run_advance(
+                edge, [s_own, s_c, s_a, v_own, v_c, v_a, mean, f_own, f_c, f_a, *got]
+            )
+            n_own, n_c, n_a, send_c, send_a = run_again(
+                pairs, counts, edge, [left, right], weights
             )
     wide = lambda t: t.reshape(3, 1, 1, OWN)
     return wide(u_out), wide(vel_out), theta.reshape(1, 1, OWN)

time: 192 us -> 177 us (0.922); the launches traced: 189 us -> 180 us
  Pallas kernels: 126 us -> 106 us
  starting transfers between devices: 26.6 us -> 35.4 us
    pallas_call x4, Pallas kernels: 120 us -> 90.1 us  [sweep(): pl.pallas_call(kernel, out_shape=out_shape, grid_spec=pltpu.PrefetchScala...]
    pallas_call x0 -> x3, Pallas kernels: none -> 10.8 us  [small(): pl.pallas_call(kernel, out_shape=out_shape, in_specs=[SMEM] * smem + [VME...]
    ppermute x18, starting transfers between devices: 26.6 us -> 35.4 us  [shift_ring(): return lax.ppermute(block, axis, [(i, (i + by) % n) for i in range(n)])]
  transfers between devices with their start and end apart: 18 -> 18, of which waited for: 10 -> 9; matrix products, arithmetic and copies ran while one was open for 0% -> 0% of each run, Pallas kernels for 16% -> 16%
where the time goes in v3:
time: 177 us; the launch traced here: 180 us
  Pallas kernels  106 us (60%)
  starting transfers between devices  35.4 us (20%)
  waiting for transfers between devices  34.5 us (19%)
  local copies, waits for them, and re-layouts  3.12 us (2%)
    pallas_call x4, Pallas kernels, sweep(): pl.pallas_call(kernel, out_shape=out_shape, grid_spec=pltpu.PrefetchScala...  90.1 us
    ppermute x18, starting transfers between devices, shift_ring(): return lax.ppermute(block, axis, [(i, (i + by) % n) for i in range(n)])  35.4 us
    ppermute x18, waiting for transfers between devices, shift_ring(): return lax.ppermute(block, axis, [(i, (i + by) % n) for i in range(n)])  34.5 us
    pallas_call x3, Pallas kernels, small(): pl.pallas_call(kernel, out_shape=out_shape, in_specs=[SMEM] * smem + [VME...  10.8 us
  transfers between devices with their start and end apart: 18, of which 9 were waited for; matrix products, arithmetic and copies ran while one was open for 0% of the time, Pallas kernels for 16%

profile of v3, /device:TPU:0, one launch (start us, length us, event | category | flops | bytes accessed | tf_op | source)
XLA Modules:
  0.0 180.2 jit_solution(10440137607420876301)
XLA Ops:
  0.7 2.9 %pack.1 = (f32[128,8,128]{2,1,0:T(8,128)}, f32[128,8,128]{2,1,0:T(8,128)}, f32[8,128]{1,0:T(8,128)}, f32[32,8,128]{2,1,0:T(8,128)}, f32[32,8,128]{2,1,0:T(8,128)...) custom-call(s32[2,32]{1,0:T(2,128)} %bitcast.13, f32[3,128,128]{2,1,0:T(8,128)} %bitcast.31, f32[3,128,128]{2,1,0:T(8,128)} %bitcast.29, ...), custom_call_target="tpu_custom_call" | custom-call | tf_op jit(solution)/shard_map/pack/pallas_call | solution.py:586
  3.5 6.8 %collective-permute-start = (f32[32,8,128]{2,1,0:T(8,128)}, f32[32,8,128]{2,1,0:T(8,128)S(1)}, u32[]{:S(2)}, u32[]{:S(2)}) collective-permute-start(f32[32,8,128]{2,1,0:T(8,128)} %get-tuple-element.51), channel_id=1, source_target_pairs={{0,112},{16,0},{32,16},{48,32},{64,48},{80,64},{96,80},{112,96},{1... | collective-permute-start | bytes 393224 | tf_op jit(solution)/shard_map/ppermute | solution.py:608
  10.3 2.0 %collective-permute-start.1 = (f32[32,8,128]{2,1,0:T(8,128)}, f32[32,8,128]{2,1,0:T(8,128)S(1)}, u32[]{:S(2)}, u32[]{:S(2)}) collective-permute-start(f32[32,8,128]{2,1,0:T(8,128)} %get-tuple-element.52), channel_id=1, source_target_pairs={{0,15},{1,0},{2,1},{3,2},{4,3},{5,4},{6,5},{7,6},{8,7},{9,8},{10,9... | collective-permute-start | bytes 393224 | tf_op jit(solution)/shard_map/ppermute | solution.py:608
  12.4 2.4 %collective-permute-done.s_c = f32[32,8,128]{2,1,0:T(8,128)S(1)} collective-permute-done((f32[32,8,128]{2,1,0:T(8,128)}, f32[32,8,128]{2,1,0:T(8,128)S(1)}, u32[]{:S(2)}, u32[]{:S(2)}) %collective-permute-start) | collective-permute-done | bytes 131104 | tf_op jit(solution)/shard_map/ppermute | solution.py:608
  15.2 5.6 %collective-permute-start.2 = (f32[32,8,128]{2,1,0:T(8,128)}, f32[32,8,128]{2,1,0:T(8,128)S(1)}, u32[]{:S(2)}, u32[]{:S(2)}) collective-permute-start(f32[32,8,128]{2,1,0:T(8,128)} %get-tuple-element.58), channel_id=1, source_target_pairs={{0,112},{16,0},{32,16},{48,32},{64,48},{80,64},{96,80},{112,96},{1... | collective-permute-start | bytes 393224 | tf_op jit(solution)/shard_map/ppermute | solution.py:608
  20.8 1.0 copy-done
  22.5 4.2 %build.1 = (bf16[128,128,64]{2,1,0:T(8,128)(2,1)S(1)}, bf16[192,64,256]{2,1,0:T(8,128)(2,1)S(1)}, bf16[192,16,256]{2,1,0:T(8,128)(2,1)S(1)}) custom-call(f32[128,8,128]{2,1,0:T(8,128)S(1)} %copy-done, f32[8,128]{1,0:T(8,128)S(1)} %copy-done.6), custom_call_target="tpu_custom_call" | custom-call | tf_op jit(solution)/shard_map/build/pallas_call | solution.py:528
  27.5 23.6 %dil0.1 = (f32[320,128,128]{2,1,0:T(8,128)}, f32[128,128]{1,0:T(8,128)S(1)}, f32[32,128]{1,0:T(8,128)S(1)}, f32[32,128]{1,0:T(8,128)S(1)}, f32[32,128]{1,0:T(8,128)S(1)}, /*index=5*/f32[32,128]{1,0:T(8,128)S(1)}) custom-call(s32[2,320]{1,0:T(2,128)S(1)} %bitcast.20, s32[2]{0:T(128)S(1)} %bitcast.24, s32[2,32]{1,0:T(2,128)S(1)} %bitcast.15, ...), custom_call_target="tpu_custom_call" | custom-call | tf_op jit(solution)/shard_map/dil0/pallas_call | solution.py:498
  51.1 5.7 %collective-permute-start.4 = (f32[32,128]{1,0:T(8,128)S(1)}, f32[32,128]{1,0:T(8,128)S(1)}, u32[]{:S(2)}, u32[]{:S(2)}) collective-permute-start(f32[32,128]{1,0:T(8,128)S(1)} %get-tuple-element.69), channel_id=1, source_target_pairs={{0,112},{16,0},{32,16},{48,32},{64,48},{80,64},{96,80},{112,96},{1... | collective-permute-start | bytes 49160 | tf_op jit(solution)/shard_map/ppermute | solution.py:608
  56.7 1.4 collective-permute-done.4.up_c
  58.2 6.0 %collective-permute-done.6.back_c = f32[32,128]{1,0:T(8,128)S(1)} collective-permute-done((f32[32,128]{1,0:T(8,128)S(1)}, f32[32,128]{1,0:T(8,128)S(1)}, u32[]{:S(2)}, u32[]{:S(2)}) %collective-permute-start.6) | collective-permute-done | bytes 16416 | tf_op jit(solution)/shard_map/ppermute | solution.py:608
  64.2 23.9 %force.2 = (f32[128,128]{1,0:T(8,128)}, f32[128,4,128]{2,1,0:T(4,128)S(1)}, f32[32,4,128]{2,1,0:T(4,128)S(1)}, f32[32,4,128]{2,1,0:T(4,128)S(1)}, f32[32,4,128]{2,1,0:T(4,128)S(1)}, /*index=5*/f32[32,4,128]{2,1,0:T(4,128)S(1)}) custom-call(s32[2,320]{1,0:T(2,128)S(1)} %bitcast.21, s32[2]{0:T(128)S(1)} %bitcast.25, s32[2,32]{1,0:T(2,128)S(1)} %bitcast.16, ...), custom_call_target="tpu_custom_call" | custom-call | tf_op jit(solution)/shard_map/force/pallas_call | solution.py:498
  88.1 8.8 %collective-permute-start.8 = (f32[32,4,128]{2,1,0:T(4,128)S(1)}, f32[32,4,128]{2,1,0:T(4,128)S(1)}, u32[]{:S(2)}, u32[]{:S(2)}) collective-permute-start(f32[32,4,128]{2,1,0:T(4,128)S(1)} %get-tuple-element.75), channel_id=1, source_target_pairs={{0,112},{16,0},{32,16},{48,32},{64,48},{80,64},{96,80},{112,96},{1... | collective-permute-start | bytes 196616 | tf_op jit(solution)/shard_map/ppermute | solution.py:608
  97.5 2.0 %collective-permute-done.8.up_c = f32[32,4,128]{2,1,0:T(4,128)S(1)} collective-permute-done((f32[32,4,128]{2,1,0:T(4,128)S(1)}, f32[32,4,128]{2,1,0:T(4,128)S(1)}, u32[]{:S(2)}, u32[]{:S(2)}) %collective-permute-start.8) | collective-permute-done | bytes 65568 | tf_op jit(solution)/shard_map/ppermute | solution.py:608
  99.4 6.1 %collective-permute-done.10.back_c = f32[32,4,128]{2,1,0:T(4,128)S(1)} collective-permute-done((f32[32,4,128]{2,1,0:T(4,128)S(1)}, f32[32,4,128]{2,1,0:T(4,128)S(1)}, u32[]{:S(2)}, u32[]{:S(2)}) %collective-permute-start.10) | collective-permute-done | bytes 65568 | tf_op jit(solution)/shard_map/ppermute | solution.py:608
  105.5 5.9 %advance.1 = (f32[128,8,128]{2,1,0:T(8,128)S(1)}, f32[32,8,128]{2,1,0:T(8,128)S(1)}, f32[32,8,128]{2,1,0:T(8,128)S(1)}, f32[128,8,128]{2,1,0:T(8,128)S(1)}, f32[...) custom-call(s32[2,32]{1,0:T(2,128)S(1)} %bitcast.17, ...), custom_call_target="tpu_custom_call" | custom-call | tf_op jit(solution)/shard_map/advance/pallas_call | solution.py:528
  111.5 18.3 %dil1.1 = (f32[128,128]{1,0:T(8,128)S(1)}, f32[32,128]{1,0:T(8,128)S(1)}, f32[32,128]{1,0:T(8,128)S(1)}, f32[32,128]{1,0:T(8,128)S(1)}, f32[32,128]{1,0:T(8,128)S(1)}) custom-call(s32[2,320]{1,0:T(2,128)S(1)} %bitcast.22, s32[2]{0:T(128)S(1)} %bitcast.26, s32[2,32]{1,0:T(2,128)S(1)} %bitcast.18, bf16[128,128,64]{2,1,0:T(8,128)(2,1)S(1)} %get-tuple-element.79.left, ...), custom_call_target="tpu_custom_call" | custom-call | tf_op jit(solution)/shard_map/dil1/pallas_call | solution.py:498
  129.8 5.5 %collective-permute-start.12 = (f32[32,128]{1,0:T(8,128)S(1)}, f32[32,128]{1,0:T(8,128)S(1)}, u32[]{:S(2)}, u32[]{:S(2)}) collective-permute-start(f32[32,128]{1,0:T(8,128)S(1)} %get-tuple-element.89), channel_id=1, source_target_pairs={{0,112},{16,0},{32,16},{48,32},{64,48},{80,64},{96,80},{112,96},{1... | collective-permute-start | bytes 49160 | tf_op jit(solution)/shard_map/ppermute | solution.py:608
  135.8 0.9 collective-permute-done.12.up_c
  136.8 5.9 %collective-permute-done.14.back_c = f32[32,128]{1,0:T(8,128)S(1)} collective-permute-done((f32[32,128]{1,0:T(8,128)S(1)}, f32[32,128]{1,0:T(8,128)S(1)}, u32[]{:S(2)}, u32[]{:S(2)}) %collective-permute-start.14) | collective-permute-done | bytes 16416 | tf_op jit(solution)/shard_map/ppermute | solution.py:608
  142.7 24.2 %force.3 = (f32[128,128]{1,0:T(8,128)}, f32[128,4,128]{2,1,0:T(4,128)S(1)}, f32[32,4,128]{2,1,0:T(4,128)S(1)}, f32[32,4,128]{2,1,0:T(4,128)S(1)}, f32[32,4,128]{2,1,0:T(4,128)}, /*index=5*/f32[32,4,128]{2,1,0:T(4,128)}) custom-call(s32[2,320]{1,0:T(2,128)S(1)} %bitcast.23, s32[2]{0:T(128)S(1)} %bitcast.27, s32[2,32]{1,0:T(2,128)S(1)} %bitcast.19, ...), custom_call_target="tpu_custom_call" | custom-call | tf_op jit(solution)/shard_map/force/pallas_call | solution.py:498
  166.9 0.7 copy-done.5
  167.6 9.3 %collective-permute-done.16.back_c = f32[32,4,128]{2,1,0:T(4,128)S(1)} collective-permute-done((f32[32,4,128]{2,1,0:T(4,128)S(1)}, f32[32,4,128]{2,1,0:T(4,128)S(1)}, u32[]{:S(2)}, u32[]{:S(2)}) %collective-permute-start.16) | collective-permute-done | bytes 65568 | tf_op jit(solution)/shard_map/ppermute | solution.py:608
  177.6 2.7 %finish.1 = (f32[3,128,128]{2,1,0:T(8,128)}, f32[3,128,128]{2,1,0:T(8,128)}) custom-call(s32[2,32]{1,0:T(2,128)} %bitcast.14, f32[3,128,128]{2,1,0:T(8,128)} %bitcast.30, f32[128,8,128]{2,1,0:T(8,128)} %get-tuple-element.50.s_own.s_start, f32[128,8,128]{2,1,0:T(8,128)} %copy-done.3, f32[128,8,128]{2,1,0:T(8,128)} %copy-done.4, f32[128,4,128]{2,1,0:T(4,128)} %copy-done.5, ...), custom_call_target="tpu_custom_call" | custom-call | tf_op jit(solution)/shard_map/finish/pallas_call | solution.py:596
  (47 shorter events, 3.5 us)
Async XLA Ops:
  0.6 26.8 %copy-start.8 = (s32[1,1,2,32]{3,2,1,0:T(2,128)S(1)}, s32[1,1,2,32]{3,2,1,0:T(2,128)}, u32[]{:S(2)}) copy-start(s32[1,1,2,32]{3,2,1,0:T(2,128)} %param.16) | copy-start | bytes 772
  3.5 11.3 %collective-permute-start = (f32[32,8,128]{2,1,0:T(8,128)}, f32[32,8,128]{2,1,0:T(8,128)S(1)}, u32[]{:S(2)}, u32[]{:S(2)}) collective-permute-start(f32[32,8,128]{2,1,0:T(8,128)} %get-tuple-element.51), channel_id=1, source_target_pairs={{0,112},{16,0},{32,16},{48,32},{64,48},{80,64},{96,80},{112,96},{1... | collective-permute-start | bytes 393224 | tf_op jit(solution)/shard_map/ppermute | solution.py:608
  10.3 4.9 %collective-permute-start.1 = (f32[32,8,128]{2,1,0:T(8,128)}, f32[32,8,128]{2,1,0:T(8,128)S(1)}, u32[]{:S(2)}, u32[]{:S(2)}) collective-permute-start(f32[32,8,128]{2,1,0:T(8,128)} %get-tuple-element.52), channel_id=1, source_target_pairs={{0,15},{1,0},{2,1},{3,2},{4,3},{5,4},{6,5},{7,6},{8,7},{9,8},{10,9... | collective-permute-start | bytes 393224 | tf_op jit(solution)/shard_map/ppermute | solution.py:608
  15.2 49.0 %collective-permute-start.2 = (f32[32,8,128]{2,1,0:T(8,128)}, f32[32,8,128]{2,1,0:T(8,128)S(1)}, u32[]{:S(2)}, u32[]{:S(2)}) collective-permute-start(f32[32,8,128]{2,1,0:T(8,128)} %get-tuple-element.58), channel_id=1, source_target_pairs={{0,112},{16,0},{32,16},{48,32},{64,48},{80,64},{96,80},{112,96},{1... | collective-permute-start | bytes 393224 | tf_op jit(solution)/shard_map/ppermute | solution.py:608
  20.8 43.4 %collective-permute-start.3 = (f32[32,8,128]{2,1,0:T(8,128)}, f32[32,8,128]{2,1,0:T(8,128)S(1)}, u32[]{:S(2)}, u32[]{:S(2)}) collective-permute-start(f32[32,8,128]{2,1,0:T(8,128)} %get-tuple-element.59), channel_id=1, source_target_pairs={{0,15},{1,0},{2,1},{3,2},{4,3},{5,4},{6,5},{7,6},{8,7},{9,8},{10,9... | collective-permute-start | bytes 393224 | tf_op jit(solution)/shard_map/ppermute | solution.py:608
  27.4 36.8 %copy-start.1 = (f32[128,8,128]{2,1,0:T(8,128)S(1)}, f32[128,8,128]{2,1,0:T(8,128)}, u32[]{:S(2)}) copy-start(f32[128,8,128]{2,1,0:T(8,128)} %get-tuple-element.50.s_own.s_start) | copy-start | bytes 1572868
  27.5 36.8 %copy-start.2 = (f32[128,8,128]{2,1,0:T(8,128)S(1)}, f32[128,8,128]{2,1,0:T(8,128)}, u32[]{:S(2)}) copy-start(f32[128,8,128]{2,1,0:T(8,128)} %get-tuple-element.57.v_own) | copy-start | bytes 1572868
  27.5 36.8 %copy-start.7 = (f32[8,128]{1,0:T(8,128)S(1)}, f32[8,128]{1,0:T(8,128)}, u32[]{:S(2)}) copy-start(f32[8,128]{1,0:T(8,128)} %get-tuple-element.60.mean) | copy-start | bytes 12292
  51.1 7.1 %collective-permute-start.4 = (f32[32,128]{1,0:T(8,128)S(1)}, f32[32,128]{1,0:T(8,128)S(1)}, u32[]{:S(2)}, u32[]{:S(2)}) collective-permute-start(f32[32,128]{1,0:T(8,128)S(1)} %get-tuple-element.69), channel_id=1, source_target_pairs={{0,112},{16,0},{32,16},{48,32},{64,48},{80,64},{96,80},{112,96},{1... | collective-permute-start | bytes 49160 | tf_op jit(solution)/shard_map/ppermute | solution.py:608
  56.7 1.4 collective-permute-start.5
  56.7 7.5 %collective-permute-start.6 = (f32[32,128]{1,0:T(8,128)S(1)}, f32[32,128]{1,0:T(8,128)S(1)}, u32[]{:S(2)}, u32[]{:S(2)}) collective-permute-start(f32[32,128]{1,0:T(8,128)S(1)} %get-tuple-element.67.n_c), channel_id=1, source_target_pairs={{0,16},{16,32},{32,48},{48,64},{64,80},{80,96},{96,112},{112,0},{1... | collective-permute-start | bytes 49160 | tf_op jit(solution)/shard_map/ppermute | solution.py:608
  58.2 6.0 %collective-permute-start.7 = (f32[32,128]{1,0:T(8,128)S(1)}, f32[32,128]{1,0:T(8,128)S(1)}, u32[]{:S(2)}, u32[]{:S(2)}) collective-permute-start(f32[32,128]{1,0:T(8,128)S(1)} %get-tuple-element.68.n_a), channel_id=1, source_target_pairs={{0,1},{1,2},{2,3},{3,4},{4,5},{5,6},{6,7},{7,8},{8,9},{9,10},{10,1... | collective-permute-start | bytes 49160 | tf_op jit(solution)/shard_map/ppermute | solution.py:608
  88.1 11.3 %collective-permute-start.8 = (f32[32,4,128]{2,1,0:T(4,128)S(1)}, f32[32,4,128]{2,1,0:T(4,128)S(1)}, u32[]{:S(2)}, u32[]{:S(2)}) collective-permute-start(f32[32,4,128]{2,1,0:T(4,128)S(1)} %get-tuple-element.75), channel_id=1, source_target_pairs={{0,112},{16,0},{32,16},{48,32},{64,48},{80,64},{96,80},{112,96},{1... | collective-permute-start | bytes 196616 | tf_op jit(solution)/shard_map/ppermute | solution.py:608
  96.9 2.5 %collective-permute-start.9 = (f32[32,4,128]{2,1,0:T(4,128)S(1)}, f32[32,4,128]{2,1,0:T(4,128)S(1)}, u32[]{:S(2)}, u32[]{:S(2)}) collective-permute-start(f32[32,4,128]{2,1,0:T(4,128)S(1)} %get-tuple-element.76), channel_id=1, source_target_pairs={{0,15},{1,0},{2,1},{3,2},{4,3},{5,4},{6,5},{7,6},{8,7},{9,8},{10,9... | collective-permute-start | bytes 196616 | tf_op jit(solution)/shard_map/ppermute | solution.py:608
  96.9 8.6 %collective-permute-start.10 = (f32[32,4,128]{2,1,0:T(4,128)S(1)}, f32[32,4,128]{2,1,0:T(4,128)S(1)}, u32[]{:S(2)}, u32[]{:S(2)}) collective-permute-start(f32[32,4,128]{2,1,0:T(4,128)S(1)} %get-tuple-element.73.f_c), channel_id=1, source_target_pairs={{0,16},{16,32},{32,48},{48,64},{64,80},{80,96},{96,112},{112,0},{1... | collective-permute-start | bytes 196616 | tf_op jit(solution)/shard_map/ppermute | solution.py:608
  96.9 8.6 %collective-permute-start.11 = (f32[32,4,128]{2,1,0:T(4,128)S(1)}, f32[32,4,128]{2,1,0:T(4,128)S(1)}, u32[]{:S(2)}, u32[]{:S(2)}) collective-permute-start(f32[32,4,128]{2,1,0:T(4,128)S(1)} %get-tuple-element.74.f_a), channel_id=1, source_target_pairs={{0,1},{1,2},{2,3},{3,4},{4,5},{5,6},{6,7},{7,8},{8,9},{9,10},{10,1... | collective-permute-start | bytes 196616 | tf_op jit(solution)/shard_map/ppermute | solution.py:608
  111.4 31.2 %copy-start.3 = (f32[128,8,128]{2,1,0:T(8,128)}, f32[128,8,128]{2,1,0:T(8,128)S(1)}, u32[]{:S(2)}) copy-start(f32[128,8,128]{2,1,0:T(8,128)S(1)} %get-tuple-element.77.s_own) | copy-start | bytes 1572868
  111.4 31.2 %copy-start.4 = (f32[128,8,128]{2,1,0:T(8,128)}, f32[128,8,128]{2,1,0:T(8,128)S(1)}, u32[]{:S(2)}) copy-start(f32[128,8,128]{2,1,0:T(8,128)S(1)} %get-tuple-element.78.v_own) | copy-start | bytes 1572868
  129.8 7.0 %collective-permute-start.12 = (f32[32,128]{1,0:T(8,128)S(1)}, f32[32,128]{1,0:T(8,128)S(1)}, u32[]{:S(2)}, u32[]{:S(2)}) collective-permute-start(f32[32,128]{1,0:T(8,128)S(1)} %get-tuple-element.89), channel_id=1, source_target_pairs={{0,112},{16,0},{32,16},{48,32},{64,48},{80,64},{96,80},{112,96},{1... | collective-permute-start | bytes 49160 | tf_op jit(solution)/shard_map/ppermute | solution.py:608
  135.3 1.4 collective-permute-start.13
  135.3 7.4 %collective-permute-start.14 = (f32[32,128]{1,0:T(8,128)S(1)}, f32[32,128]{1,0:T(8,128)S(1)}, u32[]{:S(2)}, u32[]{:S(2)}) collective-permute-start(f32[32,128]{1,0:T(8,128)S(1)} %get-tuple-element.87.n_c), channel_id=1, source_target_pairs={{0,16},{16,32},{32,48},{48,64},{64,80},{80,96},{96,112},{112,0},{1... | collective-permute-start | bytes 49160 | tf_op jit(solution)/shard_map/ppermute | solution.py:608
  135.3 7.4 %collective-permute-start.15 = (f32[32,128]{1,0:T(8,128)S(1)}, f32[32,128]{1,0:T(8,128)S(1)}, u32[]{:S(2)}, u32[]{:S(2)}) collective-permute-start(f32[32,128]{1,0:T(8,128)S(1)} %get-tuple-element.88.n_a), channel_id=1, source_target_pairs={{0,1},{1,2},{2,3},{3,4},{4,5},{5,6},{6,7},{7,8},{8,9},{9,10},{10,1... | collective-permute-start | bytes 49160 | tf_op jit(solution)/shard_map/ppermute | solution.py:608
  167.6 9.3 %collective-permute-start.16 = (f32[32,4,128]{2,1,0:T(4,128)S(1)}, f32[32,4,128]{2,1,0:T(4,128)S(1)}, u32[]{:S(2)}, u32[]{:S(2)}) collective-permute-start(f32[32,4,128]{2,1,0:T(4,128)S(1)} %get-tuple-element.92), channel_id=1, source_target_pairs={{0,16},{16,32},{32,48},{48,64},{64,80},{80,96},{96,112},{112,0},{1... | collective-permute-start | bytes 196616 | tf_op jit(solution)/shard_map/ppermute | solution.py:608
  167.6 9.3 %collective-permute-start.17 = (f32[32,4,128]{2,1,0:T(4,128)S(1)}, f32[32,4,128]{2,1,0:T(4,128)S(1)}, u32[]{:S(2)}, u32[]{:S(2)}) collective-permute-start(f32[32,4,128]{2,1,0:T(4,128)S(1)} %get-tuple-element.93), channel_id=1, source_target_pairs={{0,1},{1,2},{2,3},{3,4},{4,5},{5,6},{6,7},{7,8},{8,9},{9,10},{10,1... | collective-permute-start | bytes 196616 | tf_op jit(solution)/shard_map/ppermute | solution.py:608
  (7 other events, 57.3 us)

commit v4 on v3

--- a/solution.py
+++ b/solution.py
@@ -20,7 +20,8 @@
 TINY = 1e-30
 GROUP = 32
 UNROLL = 16
-KERNEL_VMEM = 36 << 20
+FORCE_UNROLL = 16
+KERNEL_VMEM = 21 << 20
 OWN = CL * PTS
 GHOST = FACING * PTS
 F32 = jnp.float32
@@ -163,6 +164,11 @@
     moments[c] = moment_features(parts)
 
 
+def build_kernel(s_own, mean, left, right, moments, token):
+    build_own(s_own, mean, left, right, moments)
+    token[...] = mean[...]
+
+
 def build_own(s_own, mean, left, right, moments):
     shift = mean[...]
     loop(CL, lambda c: build_one(c, s_own[c] - shift, left, right, moments), 4)
@@ -182,19 +188,20 @@
     build_ghosts(s_c, s_a, mean, right, moments)
 
 
-def turns_here(counts):
-    g = pl.program_id(0)
-    left_over = (counts[1] - g * GROUP + UNROLL - 1) // UNROLL
-    return g, jnp.clip(left_over, 0, GROUP // UNROLL)
-
-
-def first_sweep(pairs, counts, weight_of, left, right, acc, racc):
-    g, turns = turns_here(counts)
+def turns_here(counts, grouped):
+    if not grouped:
+        return 0, (counts[1] + UNROLL - 1) // UNROLL
+    first = pl.program_id(0) * GROUP
+    return first, jnp.clip((counts[1] - first + UNROLL - 1) // UNROLL, 0, GROUP // UNROLL)
+
+
+def first_sweep(pairs, counts, grouped, weight_of, left, right, acc, racc):
+    first, turns = turns_here(counts, grouped)
 
     def turn(i, _):
         for j in range(UNROLL):
             k = i * UNROLL + j
-            slot = g * GROUP + k
+            slot = first + k
             p = pairs[0, slot]
             q = pairs[1, slot]
             live = slot < counts[1]
@@ -249,7 +256,7 @@
 
 def dilatation_first(
     pairs, counts, edges, left, right, damage,
-    w_out, n_own, n_c, n_a, send_c, send_a,
+    mask_out, n_own, n_c, n_a, send_c, send_a,
     acc, racc, cut,
 ):
     g = pl.program_id(0)
@@ -265,11 +272,10 @@
 
     def weight_of(na, k, slot):
         keep = damage[k] > cut[jnp.where(slot < CL, 0, 1)]
-        w = jnp.where(keep, jnp.exp2(na), 0.0)
-        w_out[k] = w
-        return w
-
-    first_sweep(pairs, counts, weight_of, left, right, acc, racc)
+        mask_out[slot] = jnp.where(keep, 1.0, 0.0).astype(BF16)
+        return jnp.where(keep, jnp.exp2(na), 0.0)
+
+    first_sweep(pairs, counts, True, weight_of, left, right, acc, racc)
 
     @pl.when(g == pl.num_programs(0) - 1)
     def _():
@@ -287,20 +293,13 @@
 
 
 def dilatation_again(
-    pairs, counts, edges, left, right, weights, n_own, n_c, n_a, send_c, send_a, acc, racc
+    pairs, counts, edges, left, right, mask, n_own, n_c, n_a, send_c, send_a, acc, racc
 ):
-    g = pl.program_id(0)
-
-    @pl.when(g == 0)
-    def _():
-        clear(acc)
-        clear(racc)
-
-    first_sweep(pairs, counts, lambda na, k, slot: weights[k], left, right, acc, racc)
-
-    @pl.when(g == pl.num_programs(0) - 1)
-    def _():
-        first_finish(edges, acc, racc, n_own, n_c, n_a, send_c, send_a)
+    clear(acc)
+    clear(racc)
+    weight_of = lambda na, k, slot: mask[slot].astype(F32) * jnp.exp2(na)
+    first_sweep(pairs, counts, False, weight_of, left, right, acc, racc)
+    first_finish(edges, acc, racc, n_own, n_c, n_a, send_c, send_a)
 
 
 def advance(edges, s_own, s_c, s_a, v_own, v_c, v_a, f_own, f_c, f_a, up_c, up_a, back_c, back_a,
@@ -328,7 +327,7 @@
 
 def force_pass(
     pairs, counts, edges, left, right, moments, s_own, s_c, s_a, v_own, v_c, v_a, mean,
-    n_own, n_c, n_a, up_c, up_a, back_c, back_a, weights,
+    n_own, n_c, n_a, up_c, up_a, back_c, back_a, mask,
     theta_out, f_own, f_c, f_a, send_c, send_a,
     left2, right2, acc, n_full, geo, halves,
 ):
@@ -345,10 +344,11 @@
         nu = nb - SOFTEN * LOG2E
         za = na * lax.rsqrt(na * nu)
         zb = nb * lax.rsqrt(nb * nu)
-        m = weights[k] * (geo[j, :, 2 * PTS : 3 * PTS] * za + geo[j, :, 3 * PTS :] * zb)
+        m = jnp.exp2(na) * (geo[j, :, 2 * PTS : 3 * PTS] * za + geo[j, :, 3 * PTS :] * zb)
         h, l = hilo(m)
-        halves[j, 0:PTS, :] = h
-        halves[j, PTS:, :] = l
+        keep = mask[k]
+        halves[j, 0:PTS, :] = h * keep
+        halves[j, PTS:, :] = l * keep
 
     def gather(slot, j):
         s = jnp.maximum(slot, 0)
@@ -365,9 +365,7 @@
             acc[qa] += gq
             acc[pa] += gp
 
-    g, turns = turns_here(counts)
-
-    @pl.when(g == 0)
+    @pl.when(counts[1] > 0)
     def _():
         clear(acc)
         n_full[0:CL, :] = n_own[...]
@@ -401,27 +399,28 @@
             coefs(CL + FACING + f, v_a[f])
 
         loop(FACING, ghost, 4)
-        for j in range(UNROLL):
+        for j in range(FORCE_UNROLL):
             geometry(j, j)
 
     def turn(i, _):
-        base = g * GROUP + i * UNROLL
+        base = i * FORCE_UNROLL
         found = []
-        for j in range(UNROLL + 1):
-            if j < UNROLL:
-                found.append(gather(base - UNROLL + j, j))
+        for j in range(FORCE_UNROLL + 1):
+            if j < FORCE_UNROLL:
+                found.append(gather(base - FORCE_UNROLL + j, j))
             if j > 0:
-                chain(i * UNROLL + j - 1, j - 1)
-                geometry(base + UNROLL + j - 1, j - 1)
+                chain(base + j - 1, j - 1)
+                geometry(base + FORCE_UNROLL + j - 1, j - 1)
         flush(found)
         return 0
 
+    turns = (counts[1] + FORCE_UNROLL - 1) // FORCE_UNROLL
     lax.fori_loop(0, turns, turn, 0)
 
-    @pl.when(g == pl.num_programs(0) - 1)
+    @pl.when(counts[1] > 0)
     def _():
-        last = (counts[1] + UNROLL - 1) // UNROLL * UNROLL - UNROLL
-        flush([gather(last + j, j) for j in range(UNROLL)])
+        last = (counts[1] + FORCE_UNROLL - 1) // FORCE_UNROLL * FORCE_UNROLL - FORCE_UNROLL
+        flush([gather(last + j, j) for j in range(FORCE_UNROLL)])
         shift = mean[...]
 
         def force(c, s):
@@ -484,35 +483,23 @@
     return pl.BlockSpec((GROUP, PTS, PTS), index)
 
 
-def sweep(
-    kernel, name, pairs, counts, edges, resident, tables, slab, out_tables, scratch, slab_out=None
-):
-    def whole(x, **kw):
-        return pl.BlockSpec(x.shape, lambda g, a, b: (0,) * x.ndim, **kw)
-
-    outs = [whole(x) for x in out_tables]
-    out_shape = list(out_tables)
-    if slab_out is not None:
-        outs = [slab_spec()] + outs
-        out_shape = [slab_out] + out_shape
+def sweep(kernel, name, pairs, counts, edges, tables, out_tables, scratch, damage=None):
+    slab = [] if damage is None else [damage]
     return pl.pallas_call(
         kernel,
-        out_shape=out_shape,
+        out_shape=out_tables,
         grid_spec=pltpu.PrefetchScalarGridSpec(
             num_scalar_prefetch=2,
-            grid=(SLOTS // GROUP,),
-            in_specs=[SMEM]
-            + [VMEM] * len(resident)
-            + [whole(x, pipeline_mode=pl.Buffered(1)) for x in tables]
-            + [slab_spec()],
-            out_specs=outs,
+            grid=(SLOTS // GROUP,) if slab else (1,),
+            in_specs=[SMEM] + [VMEM] * len(tables) + [slab_spec()] * len(slab),
+            out_specs=[VMEM] * len(out_tables),
             scratch_shapes=scratch,
         ),
         compiler_params=pltpu.CompilerParams(
             dimension_semantics=("arbitrary",), vmem_limit_bytes=KERNEL_VMEM
         ),
         name=name,
-    )(pairs, counts, edges, *resident, *tables, slab)
+    )(pairs, counts, edges, *tables, *slab)
 
 
 LEFT = jax.ShapeDtypeStruct((CL, PTS, 64), BF16)
@@ -524,7 +511,7 @@
 SUMS = [pltpu.VMEM((EXT + 1, 8, PTS), F32), pltpu.VMEM((CL + 1, PTS, PTS), F32)]
 
 
-def small(kernel, name, out_shape, args, smem=0, aliases=None):
+def small(kernel, name, out_shape, args, smem=0, aliases=None, moved=1 << 20):
     return pl.pallas_call(
         kernel,
         out_shape=out_shape,
@@ -532,12 +519,15 @@
         out_specs=[VMEM] * len(out_shape),
         input_output_aliases=aliases or {},
         compiler_params=pltpu.CompilerParams(vmem_limit_bytes=KERNEL_VMEM),
+        cost_estimate=pl.CostEstimate(flops=0, bytes_accessed=moved, transcendentals=0),
         name=name,
     )(*args)
 
 
 def run_build(s_own, mean):
-    return small(build_own, "build", [LEFT, RIGHT, MOMENTS], [s_own, mean])
+    return small(
+        build_kernel, "build", [LEFT, RIGHT, MOMENTS, table(8, PTS)], [s_own, mean], moved=16 << 20
+    )
 
 
 def run_ghosts(s_c, s_a, mean, right, moments):
@@ -553,31 +543,29 @@
     )
 
 
-def run_first(pairs, counts, edges, resident, damage):
+def run_first(pairs, counts, edges, tables, damage):
     return sweep(
-        dilatation_first, "dil0", pairs, counts, edges, resident, [], damage, N_TABLES,
+        dilatation_first, "dil0", pairs, counts, edges, tables,
+        [jax.ShapeDtypeStruct((SLOTS, PTS, PTS), BF16), *N_TABLES],
         [*SUMS, pltpu.VMEM((2, PTS, PTS), jnp.int32)],
-        slab_out=table(SLOTS, PTS, PTS),
-    )
-
-
-def run_again(pairs, counts, edges, resident, weights):
+        damage,
+    )
+
+
+def run_again(pairs, counts, edges, tables):
+    return sweep(dilatation_again, "dil1", pairs, counts, edges, tables, N_TABLES, SUMS)
+
+
+def run_force(pairs, counts, edges, tables):
     return sweep(
-        dilatation_again, "dil1", pairs, counts, edges, resident, [], weights, N_TABLES, SUMS
-    )
-
-
-def run_force(pairs, counts, edges, resident, tables, weights):
-    return sweep(
-        force_pass, "force", pairs, counts, edges, resident, tables, weights,
-        [table(CL, PTS)] + F_TABLES,
+        force_pass, "force", pairs, counts, edges, tables, [table(CL, PTS)] + F_TABLES,
         [
             pltpu.VMEM((CL, PTS, 16), BF16),
             pltpu.VMEM((EXT, 16, 2 * PTS), BF16),
             pltpu.VMEM((EXT + 1, 16, PTS), F32),
             pltpu.VMEM((EXT, PTS), F32),
-            pltpu.VMEM((UNROLL, PTS, 4 * PTS), F32),
-            pltpu.VMEM((UNROLL, 2 * PTS, PTS), BF16),
+            pltpu.VMEM((FORCE_UNROLL, PTS, 4 * PTS), F32),
+            pltpu.VMEM((FORCE_UNROLL, 2 * PTS, PTS), BF16),
         ],
     )
 
@@ -632,20 +620,20 @@
     s_start = s_own
     s_c = shift_ring(s_c, "circ", -1)
     s_a = shift_ring(s_a, "axial", -1)
-    left, right, moments = run_build(s_own, mean)
-    s_c, s_a, v_c, v_a = lax.optimization_barrier((s_c, s_a, v_c, v_a))
+    left, right, moments, token = run_build(s_own, mean)
+    v_c, v_a, mean = lax.optimization_barrier((v_c, v_a, token))
     right, moments = run_ghosts(s_c, s_a, mean, right, moments)
     v_c = shift_ring(v_c, "circ", -1)
     v_a = shift_ring(v_a, "axial", -1)
-    weights, n_own, n_c, n_a, send_c, send_a = run_first(
+    mask, n_own, n_c, n_a, send_c, send_a = run_first(
         pairs, counts, edge, [left, right], damage[0, 0]
     )
     for step in range(STEPS):
         got = exchange(n_c, n_a, send_c, send_a)
         theta, f_own, f_c, f_a, send_c, send_a = run_force(
-            pairs, counts, edge, [left, right, moments],
-            [s_own, s_c, s_a, v_own, v_c, v_a, mean, n_own, n_c, n_a, *got],
-            weights,
+            pairs, counts, edge,
+            [left, right, moments, s_own, s_c, s_a, v_own, v_c, v_a, mean, n_own, n_c, n_a, *got,
+             mask],
         )
         if step == STEPS - 1:
             back_c = shift_ring(f_c, "circ", 1)
@@ -657,7 +645,7 @@
                 edge, [s_own, s_c, s_a, v_own, v_c, v_a, mean, f_own, f_c, f_a, *got]
             )
             n_own, n_c, n_a, send_c, send_a = run_again(
-                pairs, counts, edge, [left, right], weights
+                pairs, counts, edge, [left, right, mask]
             )
     wide = lambda t: t.reshape(3, 1, 1, OWN)
     return wide(u_out), wide(vel_out), theta.reshape(1, 1, OWN)

time: 177 us -> 159 us (0.90)
  the two profiles are of different devices: /device:TPU:0 before, /device:TPU:4 now
where the time goes in v4:
time: 159 us; the launch traced here: 157 us
  Pallas kernels  96.6 us (61%)
  waiting for transfers between devices  30.4 us (19%)
  starting transfers between devices  25.6 us (16%)
  local copies, waits for them, and re-layouts  3.11 us (2%)
    pallas_call x4, Pallas kernels, sweep(): pl.pallas_call(kernel, out_shape=out_tables, grid_spec=pltpu.PrefetchScal...  80.3 us
    ppermute x18, waiting for transfers between devices, shift_ring(): return lax.ppermute(block, axis, [(i, (i + by) % n) for i in range(n)])  30.4 us
    ppermute x18, starting transfers between devices, shift_ring(): return lax.ppermute(block, axis, [(i, (i + by) % n) for i in range(n)])  25.6 us
    pallas_call x3, Pallas kernels, small(): pl.pallas_call(kernel, out_shape=out_shape, in_specs=[SMEM] * smem + [VME...  10.8 us
  transfers between devices with their start and end apart: 18, of which 7 were waited for; matrix products, arithmetic and copies ran while one was open for 0% of the time, Pallas kernels for 16%

profile of v4, /device:TPU:4, one launch (start us, length us, event | category | flops | bytes accessed | tf_op | source)
XLA Modules:
  0.0 156.6 jit_solution(9930836563346646)
XLA Ops:
  0.7 2.9 %pack.1 = (f32[128,8,128]{2,1,0:T(8,128)}, f32[128,8,128]{2,1,0:T(8,128)}, f32[8,128]{1,0:T(8,128)}, f32[32,8,128]{2,1,0:T(8,128)}, f32[32,8,128]{2,1,0:T(8,128)...) custom-call(s32[2,32]{1,0:T(2,128)} %bitcast.13, f32[3,128,128]{2,1,0:T(8,128)} %bitcast.31, f32[3,128,128]{2,1,0:T(8,128)} %bitcast.29, ...), custom_call_target="tpu_custom_call" | custom-call | tf_op jit(solution)/shard_map/pack/pallas_call | solution.py:574
  3.5 6.7 %collective-permute-start = (f32[32,8,128]{2,1,0:T(8,128)}, f32[32,8,128]{2,1,0:T(8,128)S(1)}, u32[]{:S(2)}, u32[]{:S(2)}) collective-permute-start(f32[32,8,128]{2,1,0:T(8,128)} %get-tuple-element.51), channel_id=1, source_target_pairs={{0,112},{16,0},{32,16},{48,32},{64,48},{80,64},{96,80},{112,96},{1... | collective-permute-start | bytes 393224 | tf_op jit(solution)/shard_map/ppermute | solution.py:596
  10.2 1.0 copy-done
  11.3 0.7 copy-done.9
  11.9 4.2 %build.1 = (bf16[128,128,64]{2,1,0:T(8,128)(2,1)S(1)}, bf16[192,64,256]{2,1,0:T(8,128)(2,1)S(1)}, bf16[192,16,256]{2,1,0:T(8,128)(2,1)S(1)}, f32[8,128]{1,0:T(8,128)S(1)}) custom-call(f32[128,8,128]{2,1,0:T(8,128)S(1)} %copy-done, f32[8,128]{1,0:T(8,128)S(1)} %copy-done.9), custom_call_target="tpu_custom_call" | custom-call | bytes 16777216 | tf_op jit(solution)/shard_map/build/pallas_call | solution.py:515
  16.1 1.7 %collective-permute-start.2 = (f32[32,8,128]{2,1,0:T(8,128)}, f32[32,8,128]{2,1,0:T(8,128)S(1)}, u32[]{:S(2)}, u32[]{:S(2)}) collective-permute-start(f32[32,8,128]{2,1,0:T(8,128)} %get-tuple-element.58), channel_id=1, source_target_pairs={{0,112},{16,0},{32,16},{48,32},{64,48},{80,64},{96,80},{112,96},{1... | collective-permute-start | bytes 393224 | tf_op jit(solution)/shard_map/ppermute | solution.py:596
  17.9 0.7 ghosts.1
  18.7 19.8 %dil0.1 = (bf16[320,128,128]{2,1,0:T(8,128)(2,1)S(1)}, f32[128,128]{1,0:T(8,128)S(1)}, f32[32,128]{1,0:T(8,128)S(1)}, f32[32,128]{1,0:T(8,128)S(1)}, f32[32,128]{1,0:T(8,128)S(1)}, /*index=5*/f32[32,128]{1,0:T(8,128)S(1)}) custom-call(s32[2,320]{1,0:T(2,128)S(1)} %bitcast.20, s32[2]{0:T(128)S(1)} %bitcast.24, s32[2,32]{1,0:T(2,128)S(1)} %bitcast.15, ...), custom_call_target="tpu_custom_call" | custom-call | tf_op jit(solution)/shard_map/dil0/pallas_call | solution.py:488
  38.5 5.7 %collective-permute-start.4 = (f32[32,128]{1,0:T(8,128)S(1)}, f32[32,128]{1,0:T(8,128)S(1)}, u32[]{:S(2)}, u32[]{:S(2)}) collective-permute-start(f32[32,128]{1,0:T(8,128)S(1)} %get-tuple-element.69), channel_id=1, source_target_pairs={{0,112},{16,0},{32,16},{48,32},{64,48},{80,64},{96,80},{112,96},{1... | collective-permute-start | bytes 49160 | tf_op jit(solution)/shard_map/ppermute | solution.py:596
  44.7 0.9 collective-permute-done.4.up_c
  45.7 5.9 %collective-permute-done.6.back_c = f32[32,128]{1,0:T(8,128)S(1)} collective-permute-done((f32[32,128]{1,0:T(8,128)S(1)}, f32[32,128]{1,0:T(8,128)S(1)}, u32[]{:S(2)}, u32[]{:S(2)}) %collective-permute-start.6) | collective-permute-done | bytes 16416 | tf_op jit(solution)/shard_map/ppermute | solution.py:596
  51.6 22.0 %force.2 = (f32[128,128]{1,0:T(8,128)}, f32[128,4,128]{2,1,0:T(4,128)S(1)}, f32[32,4,128]{2,1,0:T(4,128)S(1)}, f32[32,4,128]{2,1,0:T(4,128)S(1)}, f32[32,4,128]{2,1,0:T(4,128)S(1)}, /*index=5*/f32[32,4,128]{2,1,0:T(4,128)S(1)}) custom-call(s32[2,320]{1,0:T(2,128)S(1)} %bitcast.21, s32[2]{0:T(128)S(1)} %bitcast.25, s32[2,32]{1,0:T(2,128)S(1)} %bitcast.16, ...), custom_call_target="tpu_custom_call" | custom-call | tf_op jit(solution)/shard_map/force/pallas_call | solution.py:488
  73.6 5.8 %collective-permute-start.8 = (f32[32,4,128]{2,1,0:T(4,128)S(1)}, f32[32,4,128]{2,1,0:T(4,128)S(1)}, u32[]{:S(2)}, u32[]{:S(2)}) collective-permute-start(f32[32,4,128]{2,1,0:T(4,128)S(1)} %get-tuple-element.75), channel_id=1, source_target_pairs={{0,112},{16,0},{32,16},{48,32},{64,48},{80,64},{96,80},{112,96},{1... | collective-permute-start | bytes 196616 | tf_op jit(solution)/shard_map/ppermute | solution.py:596
  79.9 2.5 %collective-permute-done.8.up_c = f32[32,4,128]{2,1,0:T(4,128)S(1)} collective-permute-done((f32[32,4,128]{2,1,0:T(4,128)S(1)}, f32[32,4,128]{2,1,0:T(4,128)S(1)}, u32[]{:S(2)}, u32[]{:S(2)}) %collective-permute-start.8) | collective-permute-done | bytes 65568 | tf_op jit(solution)/shard_map/ppermute | solution.py:596
  82.4 5.5 %collective-permute-done.10.back_c = f32[32,4,128]{2,1,0:T(4,128)S(1)} collective-permute-done((f32[32,4,128]{2,1,0:T(4,128)S(1)}, f32[32,4,128]{2,1,0:T(4,128)S(1)}, u32[]{:S(2)}, u32[]{:S(2)}) %collective-permute-start.10) | collective-permute-done | bytes 65568 | tf_op jit(solution)/shard_map/ppermute | solution.py:596
  88.0 5.9 %advance.1 = (f32[128,8,128]{2,1,0:T(8,128)S(1)}, f32[32,8,128]{2,1,0:T(8,128)S(1)}, f32[32,8,128]{2,1,0:T(8,128)S(1)}, f32[128,8,128]{2,1,0:T(8,128)S(1)}, f32[...) custom-call(s32[2,32]{1,0:T(2,128)S(1)} %bitcast.17, ...), custom_call_target="tpu_custom_call" | custom-call | bytes 1048576 | tf_op jit(solution)/shard_map/advance/pallas_call | solution.py:515
  93.9 16.4 %dil1.1 = (f32[128,128]{1,0:T(8,128)S(1)}, f32[32,128]{1,0:T(8,128)S(1)}, f32[32,128]{1,0:T(8,128)S(1)}, f32[32,128]{1,0:T(8,128)S(1)}, f32[32,128]{1,0:T(8,128)S(1)}) custom-call(s32[2,320]{1,0:T(2,128)S(1)} %bitcast.22, s32[2]{0:T(128)S(1)} %bitcast.26, s32[2,32]{1,0:T(2,128)S(1)} %bitcast.18, bf16[128,128,64]{2,1,0:T(8,128)(2,1)S(1)} %get-tuple-element.79.left, ...), custom_call_target="tpu_custom_call" | custom-call | tf_op jit(solution)/shard_map/dil1/pallas_call | solution.py:488
  110.3 4.1 %collective-permute-start.12 = (f32[32,128]{1,0:T(8,128)S(1)}, f32[32,128]{1,0:T(8,128)S(1)}, u32[]{:S(2)}, u32[]{:S(2)}) collective-permute-start(f32[32,128]{1,0:T(8,128)S(1)} %get-tuple-element.89), channel_id=1, source_target_pairs={{0,112},{16,0},{32,16},{48,32},{64,48},{80,64},{96,80},{112,96},{1... | collective-permute-start | bytes 49160 | tf_op jit(solution)/shard_map/ppermute | solution.py:596
  114.9 0.9 collective-permute-done.12.up_c
  115.9 6.0 %collective-permute-done.14.back_c = f32[32,128]{1,0:T(8,128)S(1)} collective-permute-done((f32[32,128]{1,0:T(8,128)S(1)}, f32[32,128]{1,0:T(8,128)S(1)}, u32[]{:S(2)}, u32[]{:S(2)}) %collective-permute-start.14) | collective-permute-done | bytes 16416 | tf_op jit(solution)/shard_map/ppermute | solution.py:596
  121.9 22.1 %force.3 = (f32[128,128]{1,0:T(8,128)}, f32[128,4,128]{2,1,0:T(4,128)S(1)}, f32[32,4,128]{2,1,0:T(4,128)S(1)}, f32[32,4,128]{2,1,0:T(4,128)S(1)}, f32[32,4,128]{2,1,0:T(4,128)}, /*index=5*/f32[32,4,128]{2,1,0:T(4,128)}) custom-call(s32[2,320]{1,0:T(2,128)S(1)} %bitcast.23, s32[2]{0:T(128)S(1)} %bitcast.27, s32[2,32]{1,0:T(2,128)S(1)} %bitcast.19, ...), custom_call_target="tpu_custom_call" | custom-call | tf_op jit(solution)/shard_map/force/pallas_call | solution.py:488
  144.0 0.7 copy-done.5
  144.7 8.5 %collective-permute-done.16.back_c = f32[32,4,128]{2,1,0:T(4,128)S(1)} collective-permute-done((f32[32,4,128]{2,1,0:T(4,128)S(1)}, f32[32,4,128]{2,1,0:T(4,128)S(1)}, u32[]{:S(2)}, u32[]{:S(2)}) %collective-permute-start.16) | collective-permute-done | bytes 65568 | tf_op jit(solution)/shard_map/ppermute | solution.py:596
  153.9 2.7 %finish.1 = (f32[3,128,128]{2,1,0:T(8,128)}, f32[3,128,128]{2,1,0:T(8,128)}) custom-call(s32[2,32]{1,0:T(2,128)} %bitcast.14, f32[3,128,128]{2,1,0:T(8,128)} %bitcast.30, f32[128,8,128]{2,1,0:T(8,128)} %get-tuple-element.50.s_own.s_start, f32[128,8,128]{2,1,0:T(8,128)} %copy-done.3, f32[128,8,128]{2,1,0:T(8,128)} %copy-done.4, f32[128,4,128]{2,1,0:T(4,128)} %copy-done.5, ...), custom_call_target="tpu_custom_call" | custom-call | tf_op jit(solution)/shard_map/finish/pallas_call | solution.py:584
  (45 shorter events, 2.3 us)
Async XLA Ops:
  0.6 18.0 %copy-start.6 = (s32[1,1,2,32]{3,2,1,0:T(2,128)S(1)}, s32[1,1,2,32]{3,2,1,0:T(2,128)}, u32[]{:S(2)}) copy-start(s32[1,1,2,32]{3,2,1,0:T(2,128)} %param.16) | copy-start | bytes 772
  0.6 18.0 %copy-start.8 = (s32[1,1,2]{2,1,0:T(1,128)S(1)}, s32[1,1,2]{2,1,0:T(1,128)}, u32[]{:S(2)}) copy-start(s32[1,1,2]{2,1,0:T(1,128)} %param.18) | copy-start | bytes 28
  3.5 14.4 %collective-permute-start = (f32[32,8,128]{2,1,0:T(8,128)}, f32[32,8,128]{2,1,0:T(8,128)S(1)}, u32[]{:S(2)}, u32[]{:S(2)}) collective-permute-start(f32[32,8,128]{2,1,0:T(8,128)} %get-tuple-element.51), channel_id=1, source_target_pairs={{0,112},{16,0},{32,16},{48,32},{64,48},{80,64},{96,80},{112,96},{1... | collective-permute-start | bytes 393224 | tf_op jit(solution)/shard_map/ppermute | solution.py:596
  10.2 7.7 %collective-permute-start.1 = (f32[32,8,128]{2,1,0:T(8,128)}, f32[32,8,128]{2,1,0:T(8,128)S(1)}, u32[]{:S(2)}, u32[]{:S(2)}) collective-permute-start(f32[32,8,128]{2,1,0:T(8,128)} %get-tuple-element.52), channel_id=1, source_target_pairs={{0,15},{1,0},{2,1},{3,2},{4,3},{5,4},{6,5},{7,6},{8,7},{9,8},{10,9... | collective-permute-start | bytes 393224 | tf_op jit(solution)/shard_map/ppermute | solution.py:596
  16.1 28.1 %collective-permute-start.2 = (f32[32,8,128]{2,1,0:T(8,128)}, f32[32,8,128]{2,1,0:T(8,128)S(1)}, u32[]{:S(2)}, u32[]{:S(2)}) collective-permute-start(f32[32,8,128]{2,1,0:T(8,128)} %get-tuple-element.58), channel_id=1, source_target_pairs={{0,112},{16,0},{32,16},{48,32},{64,48},{80,64},{96,80},{112,96},{1... | collective-permute-start | bytes 393224 | tf_op jit(solution)/shard_map/ppermute | solution.py:596
  17.9 26.9 %collective-permute-start.3 = (f32[32,8,128]{2,1,0:T(8,128)}, f32[32,8,128]{2,1,0:T(8,128)S(1)}, u32[]{:S(2)}, u32[]{:S(2)}) collective-permute-start(f32[32,8,128]{2,1,0:T(8,128)} %get-tuple-element.59), channel_id=1, source_target_pairs={{0,15},{1,0},{2,1},{3,2},{4,3},{5,4},{6,5},{7,6},{8,7},{9,8},{10,9... | collective-permute-start | bytes 393224 | tf_op jit(solution)/shard_map/ppermute | solution.py:596
  18.7 32.9 %copy-start.1 = (f32[128,8,128]{2,1,0:T(8,128)S(1)}, f32[128,8,128]{2,1,0:T(8,128)}, u32[]{:S(2)}) copy-start(f32[128,8,128]{2,1,0:T(8,128)} %get-tuple-element.50.s_own.s_start) | copy-start | bytes 1572868
  18.7 32.9 %copy-start.2 = (f32[128,8,128]{2,1,0:T(8,128)S(1)}, f32[128,8,128]{2,1,0:T(8,128)}, u32[]{:S(2)}) copy-start(f32[128,8,128]{2,1,0:T(8,128)} %get-tuple-element.53.v_own) | copy-start | bytes 1572868
  38.5 7.2 %collective-permute-start.4 = (f32[32,128]{1,0:T(8,128)S(1)}, f32[32,128]{1,0:T(8,128)S(1)}, u32[]{:S(2)}, u32[]{:S(2)}) collective-permute-start(f32[32,128]{1,0:T(8,128)S(1)} %get-tuple-element.69), channel_id=1, source_target_pairs={{0,112},{16,0},{32,16},{48,32},{64,48},{80,64},{96,80},{112,96},{1... | collective-permute-start | bytes 49160 | tf_op jit(solution)/shard_map/ppermute | solution.py:596
  44.2 1.4 collective-permute-start.5
  44.2 7.4 %collective-permute-start.6 = (f32[32,128]{1,0:T(8,128)S(1)}, f32[32,128]{1,0:T(8,128)S(1)}, u32[]{:S(2)}, u32[]{:S(2)}) collective-permute-start(f32[32,128]{1,0:T(8,128)S(1)} %get-tuple-element.67.n_c), channel_id=1, source_target_pairs={{0,16},{16,32},{32,48},{48,64},{64,80},{80,96},{96,112},{112,0},{1... | collective-permute-start | bytes 49160 | tf_op jit(solution)/shard_map/ppermute | solution.py:596
  44.2 7.3 %collective-permute-start.7 = (f32[32,128]{1,0:T(8,128)S(1)}, f32[32,128]{1,0:T(8,128)S(1)}, u32[]{:S(2)}, u32[]{:S(2)}) collective-permute-start(f32[32,128]{1,0:T(8,128)S(1)} %get-tuple-element.68.n_a), channel_id=1, source_target_pairs={{0,1},{1,2},{2,3},{3,4},{4,5},{5,6},{6,7},{7,8},{8,9},{9,10},{10,1... | collective-permute-start | bytes 49160 | tf_op jit(solution)/shard_map/ppermute | solution.py:596
  73.6 8.8 %collective-permute-start.8 = (f32[32,4,128]{2,1,0:T(4,128)S(1)}, f32[32,4,128]{2,1,0:T(4,128)S(1)}, u32[]{:S(2)}, u32[]{:S(2)}) collective-permute-start(f32[32,4,128]{2,1,0:T(4,128)S(1)} %get-tuple-element.75), channel_id=1, source_target_pairs={{0,112},{16,0},{32,16},{48,32},{64,48},{80,64},{96,80},{112,96},{1... | collective-permute-start | bytes 196616 | tf_op jit(solution)/shard_map/ppermute | solution.py:596
  79.4 3.0 %collective-permute-start.9 = (f32[32,4,128]{2,1,0:T(4,128)S(1)}, f32[32,4,128]{2,1,0:T(4,128)S(1)}, u32[]{:S(2)}, u32[]{:S(2)}) collective-permute-start(f32[32,4,128]{2,1,0:T(4,128)S(1)} %get-tuple-element.76), channel_id=1, source_target_pairs={{0,15},{1,0},{2,1},{3,2},{4,3},{5,4},{6,5},{7,6},{8,7},{9,8},{10,9... | collective-permute-start | bytes 196616 | tf_op jit(solution)/shard_map/ppermute | solution.py:596
  79.4 8.6 %collective-permute-start.10 = (f32[32,4,128]{2,1,0:T(4,128)S(1)}, f32[32,4,128]{2,1,0:T(4,128)S(1)}, u32[]{:S(2)}, u32[]{:S(2)}) collective-permute-start(f32[32,4,128]{2,1,0:T(4,128)S(1)} %get-tuple-element.73.f_c), channel_id=1, source_target_pairs={{0,16},{16,32},{32,48},{48,64},{64,80},{80,96},{96,112},{112,0},{1... | collective-permute-start | bytes 196616 | tf_op jit(solution)/shard_map/ppermute | solution.py:596
  79.4 8.6 %collective-permute-start.11 = (f32[32,4,128]{2,1,0:T(4,128)S(1)}, f32[32,4,128]{2,1,0:T(4,128)S(1)}, u32[]{:S(2)}, u32[]{:S(2)}) collective-permute-start(f32[32,4,128]{2,1,0:T(4,128)S(1)} %get-tuple-element.74.f_a), channel_id=1, source_target_pairs={{0,1},{1,2},{2,3},{3,4},{4,5},{5,6},{6,7},{7,8},{8,9},{9,10},{10,1... | collective-permute-start | bytes 196616 | tf_op jit(solution)/shard_map/ppermute | solution.py:596
  93.9 28.0 %copy-start.3 = (f32[128,8,128]{2,1,0:T(8,128)}, f32[128,8,128]{2,1,0:T(8,128)S(1)}, u32[]{:S(2)}) copy-start(f32[128,8,128]{2,1,0:T(8,128)S(1)} %get-tuple-element.77.s_own) | copy-start | bytes 1572868
  93.9 28.0 %copy-start.4 = (f32[128,8,128]{2,1,0:T(8,128)}, f32[128,8,128]{2,1,0:T(8,128)S(1)}, u32[]{:S(2)}) copy-start(f32[128,8,128]{2,1,0:T(8,128)S(1)} %get-tuple-element.78.v_own) | copy-start | bytes 1572868
  110.3 5.6 %collective-permute-start.12 = (f32[32,128]{1,0:T(8,128)S(1)}, f32[32,128]{1,0:T(8,128)S(1)}, u32[]{:S(2)}, u32[]{:S(2)}) collective-permute-start(f32[32,128]{1,0:T(8,128)S(1)} %get-tuple-element.89), channel_id=1, source_target_pairs={{0,112},{16,0},{32,16},{48,32},{64,48},{80,64},{96,80},{112,96},{1... | collective-permute-start | bytes 49160 | tf_op jit(solution)/shard_map/ppermute | solution.py:596
  114.4 1.4 collective-permute-start.13
  114.4 7.5 %collective-permute-start.14 = (f32[32,128]{1,0:T(8,128)S(1)}, f32[32,128]{1,0:T(8,128)S(1)}, u32[]{:S(2)}, u32[]{:S(2)}) collective-permute-start(f32[32,128]{1,0:T(8,128)S(1)} %get-tuple-element.87.n_c), channel_id=1, source_target_pairs={{0,16},{16,32},{32,48},{48,64},{64,80},{80,96},{96,112},{112,0},{1... | collective-permute-start | bytes 49160 | tf_op jit(solution)/shard_map/ppermute | solution.py:596
  114.4 7.5 %collective-permute-start.15 = (f32[32,128]{1,0:T(8,128)S(1)}, f32[32,128]{1,0:T(8,128)S(1)}, u32[]{:S(2)}, u32[]{:S(2)}) collective-permute-start(f32[32,128]{1,0:T(8,128)S(1)} %get-tuple-element.88.n_a), channel_id=1, source_target_pairs={{0,1},{1,2},{2,3},{3,4},{4,5},{5,6},{6,7},{7,8},{8,9},{9,10},{10,1... | collective-permute-start | bytes 49160 | tf_op jit(solution)/shard_map/ppermute | solution.py:596
  144.7 8.5 %collective-permute-start.16 = (f32[32,4,128]{2,1,0:T(4,128)S(1)}, f32[32,4,128]{2,1,0:T(4,128)S(1)}, u32[]{:S(2)}, u32[]{:S(2)}) collective-permute-start(f32[32,4,128]{2,1,0:T(4,128)S(1)} %get-tuple-element.92), channel_id=1, source_target_pairs={{0,16},{16,32},{32,48},{48,64},{64,80},{80,96},{96,112},{112,0},{1... | collective-permute-start | bytes 196616 | tf_op jit(solution)/shard_map/ppermute | solution.py:596
  144.7 8.5 %collective-permute-start.17 = (f32[32,4,128]{2,1,0:T(4,128)S(1)}, f32[32,4,128]{2,1,0:T(4,128)S(1)}, u32[]{:S(2)}, u32[]{:S(2)}) collective-permute-start(f32[32,4,128]{2,1,0:T(4,128)S(1)} %get-tuple-element.93), channel_id=1, source_target_pairs={{0,1},{1,2},{2,3},{3,4},{4,5},{5,6},{6,7},{7,8},{8,9},{9,10},{10,1... | collective-permute-start | bytes 196616 | tf_op jit(solution)/shard_map/ppermute | solution.py:596
  (6 other events, 21.7 us)
